TPU v7x, 32 devices: a whole 2x2x4 slice. The times are simulated.
32 devices in a mesh: dp: 8 (over y, x, core), tensor: 4 (over z).
Axes of the slice: x: 2, y: 2, z: 4, core: 2. Of those that a mesh axis runs over, the one named last changes fastest.
Arguments:
- latents_in: bfloat16 [24576, 768], P(('dp', 'tensor')), may hold values from -6 to 6
- condition: bfloat16 [96, 768], P(('dp', 'tensor')), may hold values from -6 to 6
- ada_weight: bfloat16 [768, 4608], P(('dp', 'tensor')), may hold values from -0.21875 to 0.21875
- ada_bias: bfloat16 [4608], P(('dp', 'tensor')), may hold values from -3 to 3
- qkv_weight: bfloat16 [3, 768, 768], P(None, 'dp', 'tensor'), may hold values from -0.21875 to 0.21875
- qv_bias: bfloat16 [2, 768], P(None, 'tensor'), may hold values from -3 to 3
- proj_weight: bfloat16 [768, 768], P('tensor', 'dp'), may hold values from -0.875 to 0.875
- proj_bias: bfloat16 [768], replicated, may hold values from -3 to 3
- hidden_weight: bfloat16 [768, 3072], P('dp', 'tensor'), may hold values from -0.21875 to 0.21875
- hidden_bias: bfloat16 [3072], P('tensor'), may hold values from -3 to 3
- down_weight: bfloat16 [3072, 768], P('tensor', 'dp'), may hold values from -0.109375 to 0.109375
- down_bias: bfloat16 [768], replicated, may hold values from -3 to 3
- upstream_grad: bfloat16 [24576, 768], P(('dp', 'tensor')), may hold values from -6 to 6
Outputs:
- block_out: float32 [24576, 768], P(('dp', 'tensor'))
- input_grad: float32 [24576, 768], P(('dp', 'tensor'))
- condition_grad: float32 [96, 768], P(('dp', 'tensor'))
- ada_weight_grad: float32 [768, 4608], P(('dp', 'tensor'))
- ada_bias_grad: float32 [4608], P(('dp', 'tensor'))
- qkv_weight_grad: float32 [3, 768, 768], P(None, 'dp', 'tensor')
- qv_bias_grad: float32 [2, 768], P(None, 'tensor')
- proj_weight_grad: float32 [768, 768], P('tensor', 'dp')
- proj_bias_grad: float32 [768], replicated
- hidden_weight_grad: float32 [768, 3072], P('dp', 'tensor')
- hidden_bias_grad: float32 [3072], P('tensor')
- down_weight_grad: float32 [3072, 768], P('tensor', 'dp')
- down_bias_grad: float32 [768], replicated
All inputs are finite; a program needn't handle non-finite values.
Results may differ from a plain program's by a relative error of at most 0.02.
The roundings to bfloat16 on the way count: a program that leaves them out, or rounds other values in their place, can miss the bound.
Values may be sent and summed in bfloat16 or wider, within the bound.
No kernel may reach another device: no remote copies, remote signals or barrier semaphores. Data moves between devices by JAX's collectives and lax.ppermute only.
A program may use at most 192 MiB of HBM per device.

v0:
```python
import jax
import jax.numpy as jnp
from jax import lax
from jax.sharding import PartitionSpec as P

D = 768
HD = 64
SEQ = 256


def normalize_rows(values):
    centre = values - jnp.mean(values, axis=-1, keepdims=True)
    inverse = lax.rsqrt(jnp.mean(centre * centre, axis=-1, keepdims=True) + 1e-06)
    return (centre * inverse, inverse)


def norm_backward(grad_normed, normed, inverse):
    return inverse * (
        grad_normed
        - jnp.mean(grad_normed, axis=-1, keepdims=True)
        - normed * jnp.mean(grad_normed * normed, axis=-1, keepdims=True)
    )


def contract_rows(left, right):
    return lax.dot_general(
        left, right, (((0,), (0,)), ((), ())), preferred_element_type=jnp.float32
    )


def contract_cols(left, right):
    return lax.dot_general(
        left, right, (((1,), (1,)), ((), ())), preferred_element_type=jnp.float32
    )


def on_device(
    latents_in,
    condition,
    ada_weight,
    ada_bias,
    qkv_weight,
    qv_bias,
    proj_weight,
    proj_bias,
    hidden_weight,
    hidden_bias,
    down_weight,
    down_bias,
    upstream_grad,
):
    qkv_full, proj_full, hidden_full, down_full = (
        lax.all_gather(qkv_weight, "dp", axis=1, tiled=True),
        lax.all_gather(proj_weight, "dp", axis=1, tiled=True),
        lax.all_gather(hidden_weight, "dp", axis=0, tiled=True),
        lax.all_gather(down_weight, "dp", axis=1, tiled=True),
    )
    ada_full, ada_bias_full = (
        lax.all_gather(ada_weight, ("dp", "tensor"), axis=0, tiled=True),
        lax.all_gather(ada_bias, ("dp", "tensor"), axis=0, tiled=True),
    )
    latent_count = condition.shape[0]
    local_rows = latents_in.shape[0]
    cond_float = condition.astype(jnp.float32)
    silu_value, silu_pullback = jax.vjp(jax.nn.silu, cond_float)
    silu_cond = silu_value.astype(jnp.bfloat16)
    modulation = jnp.dot(
        silu_cond, ada_full, preferred_element_type=jnp.float32
    ) + ada_bias_full.astype(jnp.float32)
    pieces = modulation.reshape(latent_count, 6, 1, D)
    shift_one, scale_one, gate_one, shift_two, scale_two, gate_two = [
        pieces[:, number] for number in range(6)
    ]
    resident = latents_in.astype(jnp.float32).reshape(latent_count, SEQ, D)
    normed_one, inverse_one = normalize_rows(resident)
    input_one = (
        (normed_one * (1.0 + scale_one) + shift_one).astype(jnp.bfloat16).reshape(local_rows, D)
    )
    gathered_one = lax.all_gather(input_one, "tensor", axis=0, tiled=True)
    group_rows = gathered_one.shape[0]
    group_latents = group_rows // SEQ
    local_width = qkv_full.shape[2]
    head_count = local_width // HD
    scale_factor = HD ** (-0.5)
    bias_table = jnp.stack([qv_bias[0], jnp.zeros_like(qv_bias[0]), qv_bias[1]]).astype(jnp.float32)
    projected = (
        jnp.einsum("rd,jdc->rjc", gathered_one, qkv_full, preferred_element_type=jnp.float32)
        + bias_table
    ).astype(jnp.bfloat16)

    def split_heads(matrix):
        return matrix.reshape(group_latents, SEQ, head_count, HD)

    queries = split_heads(projected[:, 0])
    key_heads = split_heads(projected[:, 1])
    value_heads = split_heads(projected[:, 2])
    scores = (
        jnp.einsum("lqhd,lkhd->lhqk", queries, key_heads, preferred_element_type=jnp.float32)
        * scale_factor
    )
    probs = jax.nn.softmax(scores, axis=-1)
    probs_low = probs.astype(jnp.bfloat16)
    mixed = (
        jnp.einsum("lhqk,lkhd->lqhd", probs_low, value_heads, preferred_element_type=jnp.float32)
        .reshape(group_rows, local_width)
        .astype(jnp.bfloat16)
    )
    attended = (
        lax.psum_scatter(
            jnp.dot(mixed, proj_full, preferred_element_type=jnp.float32).astype(jnp.bfloat16),
            "tensor",
            scatter_dimension=0,
            tiled=True,
        ).astype(jnp.float32)
        + proj_bias.astype(jnp.float32)
    ).reshape(latent_count, SEQ, D)
    middle = resident + gate_one * attended
    normed_two, inverse_two = normalize_rows(middle)
    input_two = (
        (normed_two * (1.0 + scale_two) + shift_two).astype(jnp.bfloat16).reshape(local_rows, D)
    )
    gathered_two = lax.all_gather(input_two, "tensor", axis=0, tiled=True)
    preact = jnp.dot(
        gathered_two, hidden_full, preferred_element_type=jnp.float32
    ) + hidden_bias.astype(jnp.float32)
    activated, gelu_pullback = jax.vjp(lambda values: jax.nn.gelu(values, approximate=True), preact)
    activated_low = activated.astype(jnp.bfloat16)
    mlp_out = (
        lax.psum_scatter(
            jnp.dot(activated_low, down_full, preferred_element_type=jnp.float32).astype(
                jnp.bfloat16
            ),
            "tensor",
            scatter_dimension=0,
            tiled=True,
        ).astype(jnp.float32)
        + down_bias.astype(jnp.float32)
    ).reshape(latent_count, SEQ, D)
    block_out = (middle + gate_two * mlp_out).reshape(local_rows, D)
    upstream = upstream_grad.astype(jnp.float32).reshape(latent_count, SEQ, D)
    gate_two_grad = jnp.sum(upstream * mlp_out, axis=1)
    mlp_grad = (gate_two * upstream).astype(jnp.bfloat16).reshape(local_rows, D)
    mlp_grad_all = lax.all_gather(mlp_grad, "tensor", axis=0, tiled=True)
    down_bias_grad = jnp.sum(mlp_grad_all.astype(jnp.float32), axis=0)
    down_weight_grad = contract_rows(activated_low, mlp_grad_all)
    act_grad = contract_cols(mlp_grad_all, down_full)
    preact_grad = gelu_pullback(act_grad)[0].astype(jnp.bfloat16)
    hidden_bias_grad = jnp.sum(preact_grad.astype(jnp.float32), axis=0)
    hidden_weight_grad = contract_rows(gathered_two, preact_grad)
    input_two_grad = (
        lax.psum_scatter(
            contract_cols(preact_grad, hidden_full).astype(jnp.bfloat16),
            "tensor",
            scatter_dimension=0,
            tiled=True,
        )
        .astype(jnp.float32)
        .reshape(latent_count, SEQ, D)
    )
    scale_two_grad = jnp.sum(input_two_grad * normed_two, axis=1)
    shift_two_grad = jnp.sum(input_two_grad, axis=1)
    middle_grad = upstream + norm_backward(
        input_two_grad * (1.0 + scale_two), normed_two, inverse_two
    )
    gate_one_grad = jnp.sum(middle_grad * attended, axis=1)
    attended_grad = (gate_one * middle_grad).astype(jnp.bfloat16).reshape(local_rows, D)
    attended_grad_all = lax.all_gather(attended_grad, "tensor", axis=0, tiled=True)
    proj_bias_grad = jnp.sum(attended_grad_all.astype(jnp.float32), axis=0)
    proj_weight_grad = contract_rows(mixed, attended_grad_all)
    mixed_grad = contract_cols(attended_grad_all, proj_full).astype(jnp.bfloat16)
    mixed_heads = split_heads(mixed_grad)
    probs_grad = jnp.einsum(
        "lqhd,lkhd->lhqk", mixed_heads, value_heads, preferred_element_type=jnp.float32
    )
    scores_grad = (
        probs * (probs_grad - jnp.sum(probs * probs_grad, axis=-1, keepdims=True))
    ).astype(jnp.bfloat16)
    query_grad = (
        jnp.einsum("lhqk,lkhd->lqhd", scores_grad, key_heads, preferred_element_type=jnp.float32)
        * scale_factor
    ).astype(jnp.bfloat16)
    key_grad = (
        jnp.einsum("lhqk,lqhd->lkhd", scores_grad, queries, preferred_element_type=jnp.float32)
        * scale_factor
    ).astype(jnp.bfloat16)
    value_grad = jnp.einsum(
        "lhqk,lqhd->lkhd", probs_low, mixed_heads, preferred_element_type=jnp.float32
    ).astype(jnp.bfloat16)
    stacked = jnp.stack(
        [
            query_grad.reshape(group_rows, local_width),
            key_grad.reshape(group_rows, local_width),
            value_grad.reshape(group_rows, local_width),
        ],
        axis=1,
    )
    qkv_weight_grad = jnp.einsum(
        "rd,rjc->jdc", gathered_one, stacked, preferred_element_type=jnp.float32
    )
    column_sums = jnp.sum(stacked.astype(jnp.float32), axis=0)
    qv_bias_grad = jnp.stack([column_sums[0], column_sums[2]])
    input_one_grad = (
        lax.psum_scatter(
            jnp.einsum("rjc,jdc->rd", stacked, qkv_full, preferred_element_type=jnp.float32).astype(
                jnp.bfloat16
            ),
            "tensor",
            scatter_dimension=0,
            tiled=True,
        )
        .astype(jnp.float32)
        .reshape(latent_count, SEQ, D)
    )
    scale_one_grad = jnp.sum(input_one_grad * normed_one, axis=1)
    shift_one_grad = jnp.sum(input_one_grad, axis=1)
    input_grad = (
        middle_grad + norm_backward(input_one_grad * (1.0 + scale_one), normed_one, inverse_one)
    ).reshape(local_rows, D)
    modulation_grad = (
        jnp.stack(
            [
                shift_one_grad,
                scale_one_grad,
                gate_one_grad,
                shift_two_grad,
                scale_two_grad,
                gate_two_grad,
            ],
            axis=1,
        )
        .reshape(latent_count, 6 * D)
        .astype(jnp.bfloat16)
    )
    silu_grad = contract_cols(modulation_grad, ada_full)
    condition_grad = silu_pullback(silu_grad)[0]
    weight_total = contract_rows(silu_cond, modulation_grad)
    bias_total = jnp.sum(modulation_grad.astype(jnp.float32), axis=0)
    ada_weight_grad, ada_bias_grad = (
        lax.psum_scatter(weight_total, ("dp", "tensor"), scatter_dimension=0, tiled=True),
        lax.psum_scatter(bias_total, ("dp", "tensor"), scatter_dimension=0, tiled=True),
    )
    qkv_weight_grad, proj_weight_grad, hidden_weight_grad, down_weight_grad = (
        lax.psum_scatter(qkv_weight_grad, "dp", scatter_dimension=1, tiled=True),
        lax.psum_scatter(proj_weight_grad, "dp", scatter_dimension=1, tiled=True),
        lax.psum_scatter(hidden_weight_grad, "dp", scatter_dimension=0, tiled=True),
        lax.psum_scatter(down_weight_grad, "dp", scatter_dimension=1, tiled=True),
    )
    qv_bias_grad, proj_bias_grad, hidden_bias_grad, down_bias_grad = lax.psum(
        (qv_bias_grad, proj_bias_grad, hidden_bias_grad, down_bias_grad), "dp"
    )
    return (
        block_out,
        input_grad,
        condition_grad,
        ada_weight_grad,
        ada_bias_grad,
        qkv_weight_grad,
        qv_bias_grad,
        proj_weight_grad,
        proj_bias_grad,
        hidden_weight_grad,
        hidden_bias_grad,
        down_weight_grad,
        down_bias_grad,
    )


def solution(mesh):
    placed = (
        P(("dp", "tensor"), None),
        P(("dp", "tensor"), None),
        P(("dp", "tensor"), None),
        P(("dp", "tensor")),
        P(None, "dp", "tensor"),
        P(None, "tensor"),
        P("tensor", "dp"),
        P(),
        P("dp", "tensor"),
        P("tensor"),
        P("tensor", "dp"),
        P(),
        P(("dp", "tensor"), None),
    )
    return jax.shard_map(
        on_device,
        mesh=mesh,
        in_specs=placed,
        out_specs=(
            P(("dp", "tensor"), None),
            P(("dp", "tensor"), None),
            P(("dp", "tensor"), None),
            P(("dp", "tensor"), None),
            P(("dp", "tensor")),
            P(None, "dp", "tensor"),
            P(None, "tensor"),
            P("tensor", "dp"),
            P(),
            P("dp", "tensor"),
            P("tensor"),
            P("tensor", "dp"),
            P(),
        ),
        check_vma=False,
    )
```

profile of v0, /device:TPU:0, one launch (start us, length us, event | category | flops | bytes accessed | tf_op | source)
XLA Modules:
  0.0 1307.3 jit_solution(4185996830534986602)
XLA Ops:
  9.7 42.6 %all-reduce = bf16[4608]{0:T(1024)(128)(2,1)S(1)} all-reduce(bf16[4608]{0:T(1024)(128)(2,1)S(1)} %dynamic-update-slice), channel_id=1, replica_groups=mesh['dp'=8,'tensor'=4] {'dp','tensor'}, use_global_device_ids=true, to_apply=%add | all-reduce | flops 4608 | bytes 18432
  55.6 31.7 %all-gather.8.cloned.1.call-done = bf16[768,4608]{1,0:T(8,128)(2,1)} async-done(((bf16[24,4608]{1,0:T(8,128)(2,1)}), bf16[768,4608]{1,0:T(8,128)(2,1)}) %all-gather.8.cloned.1.call-update) | async-done | bytes 7077904 | tf_op jit(solution)/shard_map/all_gather | solution.py:59
  87.3 4.0 convolution_add_fusion
  94.5 13.2 %all_gather.33 = bf16[3,768,192]{2,0,1:T(4,128)(2,1)S(1)} all-gather(bf16[3,96,192]{2,0,1:T(4,128)(2,1)S(1)} %copy.81), channel_id=1, replica_groups=mesh['dp'=8,'tensor'=4] {'dp'}, dimensions={1}, use_global_device_ids=true | all-gather | bytes 995328 | tf_op jit(solution)/shard_map/all_gather | solution.py:53
  109.9 8.6 all_gather.34
  118.6 63.7 %all-gather.10.cloned.1.call-done = bf16[3072,768]{1,0:T(8,128)(2,1)} async-done(((bf16[768,768]{1,0:T(8,128)(2,1)}), bf16[3072,768]{1,0:T(8,128)(2,1)}) %all-gather.10.cloned.1.call-update) | async-done | bytes 4718608 | tf_op jit(solution)/shard_map/all_gather | solution.py:79
  182.3 5.2 fusion.90
  194.4 3.8 reshape_squeeze.9
  198.2 9.1 fusion.81
  207.3 5.4 fusion.40
  215.1 3.7 convolution_convert_fusion.2
  220.9 81.8 %reduce-scatter.14.cloned.1.call-done = bf16[768,768]{1,0:T(8,128)(2,1)} async-done(((bf16[3072,768]{1,0:T(8,128)(2,1)}), bf16[768,768]{1,0:T(8,128)(2,1)}) %reduce-scatter.14.cloned.1.call-update) | async-done | bytes 1179664 | tf_op jit(solution)/shard_map/reduce_scatter | solution.py:109
  313.7 85.4 %all-gather.12.cloned.1.call-done = bf16[3072,768]{1,0:T(8,128)(2,1)} async-done(((bf16[768,768]{1,0:T(8,128)(2,1)}), bf16[3072,768]{1,0:T(8,128)(2,1)}) %all-gather.12.cloned.1.call-update) | async-done | bytes 4718608 | tf_op jit(solution)/shard_map/all_gather | solution.py:122
  399.0 10.2 fusion.91
  409.2 13.9 %all-gather.16.cloned.1.call-done = bf16[768,768]{0,1:T(8,128)(2,1)} async-done(((bf16[768,96]{0,1:T(8,128)(2,1)}), bf16[768,768]{0,1:T(8,128)(2,1)}) %all-gather.16.cloned.1.call-update) | async-done | bytes 1179664 | tf_op jit(solution)/shard_map/all_gather | solution.py:56
  423.2 90.9 %all-gather.18.cloned.1.call-done = bf16[3072,768]{1,0:T(8,128)(2,1)} async-done(((bf16[768,768]{1,0:T(8,128)(2,1)}), bf16[3072,768]{1,0:T(8,128)(2,1)}) %all-gather.18.cloned.1.call-update) | async-done | bytes 4718608 | tf_op jit(solution)/shard_map/all_gather | solution.py:143
  514.0 15.2 %convert_reduce_fusion.1 = (f32[768]{0:T(1024)}, bf16[3072,768]{1,0:T(8,128)(2,1)S(1)}, bf16[3072,768]{1,0:T(8,128)(2,1)}) fusion(f32[3072,768]{1,0:T(8,128)} %fusion.91, f32[768]{0:T(1024)} %convert_element_type.154, bf16[3072,768]{1,0:T(8,128)(2,1)} %all-gather.18.cloned.1.call-done, bf16[768,768]{0,1:T(8,128)(2,1)} %all-gather.16.cloned.1.call-done), kind=kOutput, calls=%fused_computation.12 | convolution fusion | flops 3682860288 | bytes 24778752 | tf_op jit(solution)/shard_map/dot_general | solution.py:32
  531.4 5.5 convolution_convert_fusion
  537.3 8.8 convolution_convert_fusion.1
  547.5 73.1 %reduce-scatter.18.cloned.1.call-done = bf16[768,768]{1,0:T(8,128)(2,1)} async-done(((bf16[3072,768]{1,0:T(8,128)(2,1)}), bf16[768,768]{1,0:T(8,128)(2,1)}) %reduce-scatter.18.cloned.1.call-update) | async-done | bytes 1179664 | tf_op jit(solution)/shard_map/reduce_scatter | solution.py:151
  624.2 84.4 %reduce-scatter.16.cloned.1.call-done = bf16[768,768]{1,0:T(8,128)(2,1)} async-done(((bf16[3072,768]{1,0:T(8,128)(2,1)}), bf16[768,768]{1,0:T(8,128)(2,1)}) %reduce-scatter.16.cloned.1.call-update) | async-done | bytes 1179664 | tf_op jit(solution)/shard_map/reduce_scatter | solution.py:129
  708.7 6.7 fusion.15
  715.4 90.0 %all-gather.20.cloned.1.call-done = bf16[3072,768]{1,0:T(8,128)(2,1)} async-done(((bf16[768,768]{1,0:T(8,128)(2,1)}), bf16[3072,768]{1,0:T(8,128)(2,1)}) %all-gather.20.cloned.1.call-update) | async-done | bytes 4718608 | tf_op jit(solution)/shard_map/all_gather | solution.py:167
  805.4 5.2 convolution_convert_fusion.3
  810.6 3.5 reshape.269
  814.2 7.0 fusion.37
  822.1 5.3 multiply_reduce_fusion
  827.4 11.0 multiply_convert_fusion
  838.4 5.4 fusion.44
  847.0 3.4 stack_reshape.11
  852.3 3.5 stack_reshape.9
  857.6 3.7 stack_reshape.10
  864.8 5.6 bitcast_convert_fusion
  871.7 5.2 convolution_bitcast_fusion
  876.9 7.5 fusion.28
  884.4 4.3 copy.106
  888.7 4.7 reshape.282
  893.5 9.1 fusion.92
  903.0 9.1 fusion.93
  919.8 34.4 %reduce-scatter.20.cloned.1.call-done = bf16[768,768]{1,0:T(8,128)(2,1)} async-done(((bf16[3072,768]{1,0:T(8,128)(2,1)}), bf16[768,768]{1,0:T(8,128)(2,1)}) %reduce-scatter.20.cloned.1.call-update) | async-done | bytes 1179664 | tf_op jit(solution)/shard_map/reduce_scatter | solution.py:203
  954.2 5.2 multiply_reduce_fusion.3
  959.6 7.8 fusion.73
  974.7 24.7 %all-reduce.2 = (f32[2,192]{1,0:T(2,128)}, f32[768]{0:T(1024)}, f32[768]{0:T(1024)}, f32[768]{0:T(1024)}) all-reduce(f32[2,192]{1,0:T(2,128)S(1)} %pad_maximum_fusion, f32[768]{0:T(1024)S(1)} %convert_reduce_fusion.2, f32[768]{0:T(1024)S(1)} %copy-done.39, f32[768]{0:T(1024)S(1)} %convert_reduce_fusion), channel_id=1, replica_groups=mesh['dp'=8,'tensor'=4] {'dp'}, use_global_device_ids=true, to_apply=%region_26.27 | all-reduce | flops 2688 | bytes 21504 | tf_op jit(solution)/shard_map/psum | solution.py:248
  1001.0 35.2 %reduce-scatter.28.cloned.1.call-done = f32[96,576]{1,0:T(8,128)} async-done(((f32[768,576]{1,0:T(8,128)}), f32[96,576]{1,0:T(8,128)}) %reduce-scatter.28.cloned.1.call-update) | async-done | bytes 221200
  1038.1 39.7 %all-reduce.1 = f32[4608]{0:T(1024)S(1)} all-reduce(f32[4608]{0:T(1024)S(1)} %reduce_sum.208), channel_id=7, replica_groups=mesh['dp'=8,'tensor'=4] {'dp','tensor'}, use_global_device_ids=true, to_apply=%region_23.24.clone | all-reduce | flops 4608 | bytes 36864
  1081.7 5.6 fusion.71
  1087.3 41.8 %reduce-scatter.26.cloned.1.call-done = f32[768,96]{0,1:T(8,128)} async-done(((f32[768,768]{0,1:T(8,128)}), f32[768,96]{0,1:T(8,128)}) %reduce-scatter.26.cloned.1.call-update) | async-done | bytes 294928 | tf_op jit(solution)/shard_map/reduce_scatter | solution.py:246
  1129.1 170.8 %reduce-scatter.22.cloned.1.call-done = f32[24,4608]{1,0:T(8,128)} async-done(((f32[768,4608]{1,0:T(8,128)}), f32[24,4608]{1,0:T(8,128)}) %reduce-scatter.22.cloned.1.call-update) | async-done | bytes 442384 | tf_op jit(solution)/shard_map/reduce_scatter | solution.py:239
  (204 shorter events, 75.5 us)
Async XLA Ops:
  8.0 79.3 %copy-start.33 = (bf16[3,768]{1,0:T(4,128)(2,1)S(1)}, bf16[3,768]{1,0:T(4,128)(2,1)}, u32[]{:S(2)}) copy-start(bf16[3,768]{1,0:T(4,128)(2,1)} %param.14) | copy-start | bytes 13828
  8.0 79.3 %all-gather.8.cloned.1.call-start = ((), (), s32[]{:S(2)}) async-start(), calls=%async_computation.9 | async-start | bytes 7299072 | tf_op jit(solution)/shard_map/all_gather | solution.py:59
  8.8 173.6 %all-gather.10.cloned.1.call-start = ((), (), s32[]{:S(2)}) async-start(), calls=%async_computation.10 | async-start | bytes 5898240 | tf_op jit(solution)/shard_map/all_gather | solution.py:79
  53.8 38.3 %copy-start.25 = (f32[768]{0:T(1024)}, f32[768]{0:T(1024)S(1)}, u32[]{:S(2)}) copy-start(f32[768]{0:T(1024)S(1)} %broadcast_multiply_fusion.5) | copy-start | bytes 9220
  55.6 36.5 %copy-start.30 = (f32[768]{0:T(1024)}, f32[768]{0:T(1024)S(1)}, u32[]{:S(2)}) copy-start(f32[768]{0:T(1024)S(1)} %add_rsqrt_fusion.1) | copy-start | bytes 9220
  55.6 37.1 %copy-start = (bf16[768,768]{1,0:T(8,128)(2,1)S(1)}, bf16[768,768]{1,0:T(8,128)(2,1)}, u32[]{:S(2)}) copy-start(bf16[768,768]{1,0:T(8,128)(2,1)} %param.13) | copy-start | bytes 3538948
  91.3 3.0 copy-start.36
  91.3 3.1 copy-start.27
  94.2 208.5 %reduce-scatter.14.cloned.1.call-start = ((), (), s32[]{:S(2)}) async-start(), calls=%async_computation.11 | async-start | bytes 5898240 | tf_op jit(solution)/shard_map/reduce_scatter | solution.py:109
  94.5 24.0 %copy-start.40 = (bf16[2,192]{1,0:T(2,128)(2,1)S(1)}, bf16[2,192]{1,0:T(2,128)(2,1)}, u32[]{:S(2)}) copy-start(bf16[2,192]{1,0:T(2,128)(2,1)} %param.18) | copy-start | bytes 2308
  118.5 95.5 %copy-start.17 = (bf16[192,768]{0,1:T(8,128)(2,1)}, bf16[192,768]{0,1:T(8,128)(2,1)S(1)}, u32[]{:S(2)}) copy-start(bf16[192,768]{0,1:T(8,128)(2,1)S(1)} %all_gather.34) | copy-start | bytes 884740
  194.4 12.9 copy-start.7
  207.3 5.5 copy-start.37
  218.8 94.8 %all-gather.14.cloned.1.call-start = ((), (), s32[]{:S(2)}) async-start(), calls=%async_computation.13 | async-start | bytes 1327104 | tf_op jit(solution)/shard_map/all_gather | solution.py:55
  219.4 179.6 %all-gather.12.cloned.1.call-start = ((), (), s32[]{:S(2)}) async-start(), calls=%async_computation.12 | async-start | bytes 5898240 | tf_op jit(solution)/shard_map/all_gather | solution.py:122
  304.6 2.7 copy-start.22
  304.6 2.7 copy-start.35
  307.3 3.8 copy-start.3
  309.1 114.0 %all-gather.16.cloned.1.call-start = ((), (), s32[]{:S(2)}) async-start(), calls=%async_computation.14 | async-start | bytes 1327104 | tf_op jit(solution)/shard_map/all_gather | solution.py:56
  309.7 204.3 %all-gather.18.cloned.1.call-start = ((), (), s32[]{:S(2)}) async-start(), calls=%async_computation.16 | async-start | bytes 5898240 | tf_op jit(solution)/shard_map/all_gather | solution.py:143
  312.3 308.3 %reduce-scatter.18.cloned.1.call-start = ((), (), s32[]{:S(2)}) async-start(), calls=%async_computation.17 | async-start | bytes 5898240 | tf_op jit(solution)/shard_map/reduce_scatter | solution.py:151
  514.0 17.4 %copy-start.42 = (bf16[768,768]{1,0:T(8,128)(2,1)S(1)}, bf16[768,768]{1,0:T(8,128)(2,1)}, u32[]{:S(2)}) copy-start(bf16[768,768]{1,0:T(8,128)(2,1)} %all-gather.14.cloned.1.call-done) | copy-start | bytes 3538948
  529.2 2.2 copy-start.43
  536.9 171.8 %reduce-scatter.16.cloned.1.call-start = ((), (), s32[]{:S(2)}) async-start(), calls=%async_computation.15 | async-start | bytes 5898240 | tf_op jit(solution)/shard_map/reduce_scatter | solution.py:129
  546.2 259.3 %all-gather.20.cloned.1.call-start = ((), (), s32[]{:S(2)}) async-start(), calls=%async_computation.18 | async-start | bytes 5898240 | tf_op jit(solution)/shard_map/all_gather | solution.py:167
  715.4 238.8 %reduce-scatter.20.cloned.1.call-start = ((), (), s32[]{:S(2)}) async-start(), calls=%async_computation.19 | async-start | bytes 5898240 | tf_op jit(solution)/shard_map/reduce_scatter | solution.py:203
  805.4 15.8 %slice-start = ((s8[9437184]{0:T(1024)(128)(4,1)}), s8[1048576]{0:T(1024)(128)(4,1)S(1)}, s32[]{:S(2)}) async-start(s8[9437184]{0:T(1024)(128)(4,1)} %bitcast.167), calls=%async_computation.25 | async-start | bytes 2097152
  810.6 3.6 copy-start.38
  814.2 7.0 slice-start.1
  814.2 7.0 slice-start.2
  814.2 7.2 copy-start.18
  814.2 7.9 copy-start.19
  838.4 5.4 copy-start.1
  838.4 5.4 copy-start.8
  852.3 3.5 copy-start.13
  857.6 3.7 copy-start.15
  870.4 129.0 %reduce-scatter.30.cloned.1.call-start = ((), (), s32[]{:S(2)}) async-start(), calls=%async_computation.24 | async-start | bytes 884736
  876.9 159.3 %reduce-scatter.28.cloned.1.call-start = ((), (), s32[]{:S(2)}) async-start(), calls=%async_computation.23 | async-start | bytes 2211840
  893.4 193.9 %reduce-scatter.24.cloned.1.call-start = ((), (), s32[]{:S(2)}) async-start(), calls=%async_computation.21 | async-start | bytes 2654208 | tf_op jit(solution)/shard_map/reduce_scatter | solution.py:245
  902.6 226.5 %reduce-scatter.26.cloned.1.call-start = ((), (), s32[]{:S(2)}) async-start(), calls=%async_computation.22 | async-start | bytes 2654208 | tf_op jit(solution)/shard_map/reduce_scatter | solution.py:246
  912.1 42.0 %copy-start.4 = (bf16[768,768]{1,0:T(8,128)(2,1)S(1)}, bf16[768,768]{1,0:T(8,128)(2,1)}, u32[]{:S(2)}) copy-start(bf16[768,768]{1,0:T(8,128)(2,1)} %reduce-scatter.18.cloned.1.call-done) | copy-start | bytes 3538948
  912.1 387.8 %reduce-scatter.22.cloned.1.call-start = ((), (), s32[]{:S(2)}) async-start(), calls=%async_computation.20 | async-start | bytes 14598144 | tf_op jit(solution)/shard_map/reduce_scatter | solution.py:239
  967.4 3.5 copy-start.12
  971.5 3.2 copy-start.39
  971.5 107.0 %copy-start.5 = (bf16[768,768]{1,0:T(8,128)(2,1)S(1)}, bf16[768,768]{1,0:T(8,128)(2,1)}, u32[]{:S(2)}) copy-start(bf16[768,768]{1,0:T(8,128)(2,1)} %reduce-scatter.20.cloned.1.call-done) | copy-start | bytes 3538948
  971.5 107.0 %copy-start.24 = (f32[3,768]{1,0:T(4,128)S(1)}, f32[3,768]{1,0:T(4,128)}, u32[]{:S(2)}) copy-start(f32[3,768]{1,0:T(4,128)} %copy-done.23) | copy-start | bytes 27652
  971.5 106.9 %copy-start.31 = (f32[768]{0:T(1024)S(1)}, f32[768]{0:T(1024)}, u32[]{:S(2)}) copy-start(f32[768]{0:T(1024)} %copy-done.30) | copy-start | bytes 9220
  1079.5 2.2 copy-start.34
  (15 other events, 19.4 us)
Sparse Core Ops, SparseCore 0:
  11.7 75.5 all-gather.7
  94.3 87.9 all-gather.9
  218.9 83.6 reduce-scatter.13
  715.5 89.8 all-gather.19
Sparse Core Ops, SparseCore 1:
  221.2 22.3 all-gather.13
  309.2 89.8 all-gather.11
  400.8 22.3 all-gather.15
  424.8 89.2 all-gather.17
  537.0 83.6 reduce-scatter.17
  623.0 85.6 reduce-scatter.15
  870.5 83.6 reduce-scatter.19
  957.2 35.5 reduce-scatter.29
  996.0 40.1 reduce-scatter.27
  1040.5 42.4 reduce-scatter.23
  1086.8 42.3 reduce-scatter.25
  1136.8 163.1 reduce-scatter.21
where the time goes:
time: 1310 us
  waiting for transfers between devices  899 us (69%)
  matrix products  141 us (11%)
  blocking collectives  129 us (10%)
  local copies, waits for them, and re-layouts  67.8 us (5%)
  other arithmetic  52.7 us (4%)
  between operations  16.1 us (1%)
    reduce_scatter x1, waiting for transfers between devices, on_device(): lax.psum_scatter(weight_total, ('dp', 'tensor'), scatter_dimension=0, til...  171 us
    all_gather x1, waiting for transfers between devices, on_device(): mlp_grad_all = lax.all_gather(mlp_grad, 'tensor', axis=0, tiled=True)  90.9 us
    all_gather x1, waiting for transfers between devices, on_device(): lax.all_gather(attended_grad, 'tensor', axis=0, tiled=True)  90 us
    all_gather x1, waiting for transfers between devices, on_device(): gathered_two = lax.all_gather(input_two, 'tensor', axis=0, tiled=True)  85.4 us
    reduce_scatter x1, waiting for transfers between devices, on_device(): lax.psum_scatter(jnp.dot(activated_low, down_full, preferred_element_type...  84.4 us
    unnamed x2, blocking collectives  82.3 us
    reduce_scatter x1, waiting for transfers between devices, on_device(): lax.psum_scatter(jnp.dot(mixed, proj_full, preferred_element_type=jnp.flo...  81.8 us
    reduce_scatter x1, waiting for transfers between devices, on_device(): lax.psum_scatter(contract_cols(preact_grad, hidden_full).astype(jnp.bfloa...  73.1 us
  transfers between devices with their start and end apart: 16, of which 13 were waited for; matrix products, arithmetic and copies ran while one was open for 9% of the time, Pallas kernels for 0%

commit v1 on v0

--- a/solution.py
+++ b/solution.py
@@ -1,3 +1,5 @@
+import functools
+
 import jax
 import jax.numpy as jnp
 from jax import lax
@@ -32,6 +34,14 @@
     return lax.dot_general(
         left, right, (((1,), (1,)), ((), ())), preferred_element_type=jnp.float32
     )
+
+
+def exchange(slots, axes):
+    return lax.all_to_all(slots, axes, 0, 0, tiled=True)
+
+
+def share(row, axes, count):
+    return exchange(jnp.broadcast_to(row[None], (count,) + row.shape), axes)
 
 
 def on_device(
@@ -48,25 +58,49 @@
     down_weight,
     down_bias,
     upstream_grad,
+    dp_size,
+    tensor_size,
 ):
-    qkv_full, proj_full, hidden_full, down_full = (
-        lax.all_gather(qkv_weight, "dp", axis=1, tiled=True),
-        lax.all_gather(proj_weight, "dp", axis=1, tiled=True),
-        lax.all_gather(hidden_weight, "dp", axis=0, tiled=True),
-        lax.all_gather(down_weight, "dp", axis=1, tiled=True),
-    )
-    ada_full, ada_bias_full = (
-        lax.all_gather(ada_weight, ("dp", "tensor"), axis=0, tiled=True),
-        lax.all_gather(ada_bias, ("dp", "tensor"), axis=0, tiled=True),
-    )
+    axes = ("dp", "tensor")
+    count = dp_size * tensor_size
+    bf16, f32 = jnp.bfloat16, jnp.float32
     latent_count = condition.shape[0]
     local_rows = latents_in.shape[0]
-    cond_float = condition.astype(jnp.float32)
+    ada_rows, ada_cols = ada_weight.shape[0], ada_bias.shape[0]
+    here = lax.axis_index("dp") * tensor_size + lax.axis_index("tensor")
+
+    def gathered(shard):
+        whole = lax.all_gather(shard, axes, axis=0)
+        return whole.reshape((dp_size, tensor_size) + shard.shape)
+
+    cond_float = condition.astype(f32)
     silu_value, silu_pullback = jax.vjp(jax.nn.silu, cond_float)
-    silu_cond = silu_value.astype(jnp.bfloat16)
-    modulation = jnp.dot(
-        silu_cond, ada_full, preferred_element_type=jnp.float32
-    ) + ada_bias_full.astype(jnp.float32)
+    silu_cond = silu_value.astype(bf16)
+    sent = jnp.concatenate(
+        [
+            ada_weight.reshape(ada_rows, count, ada_cols).transpose(1, 0, 2).reshape(count, -1),
+            silu_cond.reshape(latent_count, count, ada_rows).transpose(1, 0, 2).reshape(count, -1),
+            jnp.broadcast_to(silu_cond.reshape(1, -1), (count, latent_count * D)),
+        ],
+        axis=1,
+    )
+    got = exchange(sent, axes)
+    first, second = ada_rows * ada_cols, ada_rows * (ada_cols + latent_count)
+    ada_columns = got[:, :first].reshape(D, ada_cols)
+    silu_columns = got[:, first:second].reshape(count * latent_count, ada_rows)
+    silu_all = got[:, second:].reshape(count * latent_count, D)
+    modulation_columns = jnp.dot(
+        silu_all, ada_columns, preferred_element_type=f32
+    ) + ada_bias.astype(f32)
+    modulation = exchange(modulation_columns.reshape(count, latent_count, ada_cols), axes)
+    modulation = modulation.transpose(1, 0, 2)
+
+    qkv_full = gathered(qkv_weight).transpose(2, 0, 3, 1, 4).reshape(3, D, D)
+    proj_full = gathered(proj_weight).transpose(1, 2, 0, 3).reshape(D, D)
+    hidden_full = gathered(hidden_weight).transpose(0, 2, 1, 3).reshape(D, -1)
+    down_full = gathered(down_weight).transpose(1, 2, 0, 3).reshape(-1, D)
+    qv_full = lax.all_gather(qv_bias, "tensor", axis=1, tiled=True)
+    hidden_bias_full = lax.all_gather(hidden_bias, "tensor", axis=0, tiled=True)
     pieces = modulation.reshape(latent_count, 6, 1, D)
     shift_one, scale_one, gate_one, shift_two, scale_two, gate_two = [
         pieces[:, number] for number in range(6)
@@ -76,13 +110,13 @@
     input_one = (
         (normed_one * (1.0 + scale_one) + shift_one).astype(jnp.bfloat16).reshape(local_rows, D)
     )
-    gathered_one = lax.all_gather(input_one, "tensor", axis=0, tiled=True)
+    gathered_one = input_one
     group_rows = gathered_one.shape[0]
     group_latents = group_rows // SEQ
     local_width = qkv_full.shape[2]
     head_count = local_width // HD
     scale_factor = HD ** (-0.5)
-    bias_table = jnp.stack([qv_bias[0], jnp.zeros_like(qv_bias[0]), qv_bias[1]]).astype(jnp.float32)
+    bias_table = jnp.stack([qv_full[0], jnp.zeros_like(qv_full[0]), qv_full[1]]).astype(jnp.float32)
     projected = (
         jnp.einsum("rd,jdc->rjc", gathered_one, qkv_full, preferred_element_type=jnp.float32)
         + bias_table
@@ -106,12 +140,7 @@
         .astype(jnp.bfloat16)
     )
     attended = (
-        lax.psum_scatter(
-            jnp.dot(mixed, proj_full, preferred_element_type=jnp.float32).astype(jnp.bfloat16),
-            "tensor",
-            scatter_dimension=0,
-            tiled=True,
-        ).astype(jnp.float32)
+        jnp.dot(mixed, proj_full, preferred_element_type=jnp.float32)
         + proj_bias.astype(jnp.float32)
     ).reshape(latent_count, SEQ, D)
     middle = resident + gate_one * attended
@@ -119,28 +148,21 @@
     input_two = (
         (normed_two * (1.0 + scale_two) + shift_two).astype(jnp.bfloat16).reshape(local_rows, D)
     )
-    gathered_two = lax.all_gather(input_two, "tensor", axis=0, tiled=True)
+    gathered_two = input_two
     preact = jnp.dot(
         gathered_two, hidden_full, preferred_element_type=jnp.float32
-    ) + hidden_bias.astype(jnp.float32)
+    ) + hidden_bias_full.astype(jnp.float32)
     activated, gelu_pullback = jax.vjp(lambda values: jax.nn.gelu(values, approximate=True), preact)
     activated_low = activated.astype(jnp.bfloat16)
     mlp_out = (
-        lax.psum_scatter(
-            jnp.dot(activated_low, down_full, preferred_element_type=jnp.float32).astype(
-                jnp.bfloat16
-            ),
-            "tensor",
-            scatter_dimension=0,
-            tiled=True,
-        ).astype(jnp.float32)
+        jnp.dot(activated_low, down_full, preferred_element_type=jnp.float32)
         + down_bias.astype(jnp.float32)
     ).reshape(latent_count, SEQ, D)
     block_out = (middle + gate_two * mlp_out).reshape(local_rows, D)
     upstream = upstream_grad.astype(jnp.float32).reshape(latent_count, SEQ, D)
     gate_two_grad = jnp.sum(upstream * mlp_out, axis=1)
     mlp_grad = (gate_two * upstream).astype(jnp.bfloat16).reshape(local_rows, D)
-    mlp_grad_all = lax.all_gather(mlp_grad, "tensor", axis=0, tiled=True)
+    mlp_grad_all = mlp_grad
     down_bias_grad = jnp.sum(mlp_grad_all.astype(jnp.float32), axis=0)
     down_weight_grad = contract_rows(activated_low, mlp_grad_all)
     act_grad = contract_cols(mlp_grad_all, down_full)
@@ -148,13 +170,7 @@
     hidden_bias_grad = jnp.sum(preact_grad.astype(jnp.float32), axis=0)
     hidden_weight_grad = contract_rows(gathered_two, preact_grad)
     input_two_grad = (
-        lax.psum_scatter(
-            contract_cols(preact_grad, hidden_full).astype(jnp.bfloat16),
-            "tensor",
-            scatter_dimension=0,
-            tiled=True,
-        )
-        .astype(jnp.float32)
+        contract_cols(preact_grad, hidden_full)
         .reshape(latent_count, SEQ, D)
     )
     scale_two_grad = jnp.sum(input_two_grad * normed_two, axis=1)
@@ -164,7 +180,7 @@
     )
     gate_one_grad = jnp.sum(middle_grad * attended, axis=1)
     attended_grad = (gate_one * middle_grad).astype(jnp.bfloat16).reshape(local_rows, D)
-    attended_grad_all = lax.all_gather(attended_grad, "tensor", axis=0, tiled=True)
+    attended_grad_all = attended_grad
     proj_bias_grad = jnp.sum(attended_grad_all.astype(jnp.float32), axis=0)
     proj_weight_grad = contract_rows(mixed, attended_grad_all)
     mixed_grad = contract_cols(attended_grad_all, proj_full).astype(jnp.bfloat16)
@@ -200,15 +216,7 @@
     column_sums = jnp.sum(stacked.astype(jnp.float32), axis=0)
     qv_bias_grad = jnp.stack([column_sums[0], column_sums[2]])
     input_one_grad = (
-        lax.psum_scatter(
-            jnp.einsum("rjc,jdc->rd", stacked, qkv_full, preferred_element_type=jnp.float32).astype(
-                jnp.bfloat16
-            ),
-            "tensor",
-            scatter_dimension=0,
-            tiled=True,
-        )
-        .astype(jnp.float32)
+        jnp.einsum("rjc,jdc->rd", stacked, qkv_full, preferred_element_type=jnp.float32)
         .reshape(latent_count, SEQ, D)
     )
     scale_one_grad = jnp.sum(input_one_grad * normed_one, axis=1)
@@ -231,23 +239,55 @@
         .reshape(latent_count, 6 * D)
         .astype(jnp.bfloat16)
     )
-    silu_grad = contract_cols(modulation_grad, ada_full)
-    condition_grad = silu_pullback(silu_grad)[0]
-    weight_total = contract_rows(silu_cond, modulation_grad)
-    bias_total = jnp.sum(modulation_grad.astype(jnp.float32), axis=0)
-    ada_weight_grad, ada_bias_grad = (
-        lax.psum_scatter(weight_total, ("dp", "tensor"), scatter_dimension=0, tiled=True),
-        lax.psum_scatter(bias_total, ("dp", "tensor"), scatter_dimension=0, tiled=True),
-    )
-    qkv_weight_grad, proj_weight_grad, hidden_weight_grad, down_weight_grad = (
-        lax.psum_scatter(qkv_weight_grad, "dp", scatter_dimension=1, tiled=True),
-        lax.psum_scatter(proj_weight_grad, "dp", scatter_dimension=1, tiled=True),
-        lax.psum_scatter(hidden_weight_grad, "dp", scatter_dimension=0, tiled=True),
-        lax.psum_scatter(down_weight_grad, "dp", scatter_dimension=1, tiled=True),
-    )
-    qv_bias_grad, proj_bias_grad, hidden_bias_grad, down_bias_grad = lax.psum(
-        (qv_bias_grad, proj_bias_grad, hidden_bias_grad, down_bias_grad), "dp"
-    )
+    vectors = jnp.concatenate(
+        [
+            modulation_grad.reshape(-1),
+            qv_bias_grad.astype(bf16).reshape(-1),
+            proj_bias_grad.astype(bf16),
+            hidden_bias_grad.astype(bf16),
+            down_bias_grad.astype(bf16),
+        ]
+    )
+    shared = share(vectors, axes, count)
+    split = latent_count * 6 * D
+    modulation_all = shared[:, :split].reshape(count * latent_count, 6 * D)
+    totals = jnp.sum(shared[:, split:].astype(f32), axis=0)
+    place = lax.axis_index("tensor")
+    qv_bias_grad = lax.dynamic_index_in_dim(
+        totals[: 2 * D].reshape(2, tensor_size, -1), place, 1, keepdims=False
+    )
+    proj_bias_grad = totals[2 * D : 3 * D]
+    wide = hidden_bias_full.shape[0]
+    hidden_bias_grad = lax.dynamic_index_in_dim(
+        totals[3 * D : 3 * D + wide].reshape(tensor_size, -1), place, 0, keepdims=False
+    )
+    down_bias_grad = totals[3 * D + wide :]
+    ada_weight_grad = contract_rows(silu_columns, modulation_all)
+    ada_bias_grad = lax.dynamic_index_in_dim(
+        jnp.sum(modulation_all.astype(f32), axis=0).reshape(count, ada_cols), here, 0, keepdims=False
+    )
+    silu_grad = exchange(
+        contract_cols(modulation_all, ada_weight).reshape(count, latent_count, ada_rows), axes
+    )
+    condition_grad = silu_pullback(silu_grad.transpose(1, 0, 2).reshape(latent_count, D))[0]
+
+    def scattered(blocks):
+        flat = blocks.astype(bf16).reshape((-1,) + blocks.shape[-1:])
+        flat = lax.psum_scatter(flat, "dp", scatter_dimension=0, tiled=True)
+        return lax.psum_scatter(flat, "tensor", scatter_dimension=0, tiled=True).astype(f32)
+
+    down_weight_grad = scattered(
+        down_weight_grad.reshape(tensor_size, -1, dp_size, D // dp_size).transpose(2, 0, 1, 3)
+    ).reshape(down_weight.shape)
+    hidden_weight_grad = scattered(
+        hidden_weight_grad.reshape(dp_size, -1, tensor_size, hidden_weight.shape[1]).transpose(0, 2, 1, 3)
+    ).reshape(hidden_weight.shape)
+    proj_weight_grad = scattered(
+        proj_weight_grad.reshape(tensor_size, -1, dp_size, D // dp_size).transpose(2, 0, 1, 3)
+    ).reshape(proj_weight.shape)
+    qkv_weight_grad = scattered(
+        qkv_weight_grad.reshape(3, dp_size, -1, tensor_size, D // tensor_size).transpose(1, 3, 0, 2, 4)
+    ).reshape(qkv_weight.shape)
     return (
         block_out,
         input_grad,
@@ -282,7 +322,9 @@
         P(("dp", "tensor"), None),
     )
     return jax.shard_map(
-        on_device,
+        functools.partial(
+            on_device, dp_size=mesh.shape["dp"], tensor_size=mesh.shape["tensor"]
+        ),
         mesh=mesh,
         in_specs=placed,
         out_specs=(

time: 1310 us -> 696 us (0.53)
  waiting for transfers between devices: 899 us -> 196 us
  local copies, waits for them, and re-layouts: 67.8 us -> 253 us
  blocking collectives: 129 us -> 25.9 us
  matrix products: 141 us -> 108 us
  starting transfers between devices: 1.7 us -> 21.2 us
  other arithmetic: 52.7 us -> 68 us
    reduce_scatter x7, waiting for transfers between devices: 486 us -> 70 us  [the longest x3 51.5 us: scattered(): lax.psum_scatter(flat, 'tensor', scatter_dimension=0, tiled=True)]
    all_gather x7 -> x4, waiting for transfers between devices: 376 us -> 94.6 us  [gathered(): whole = lax.all_gather(shard, axes, axis=0)]
    unnamed x2 -> x0, blocking collectives: 82.3 us -> none
    reshape x0 -> x24, local copies, waits for them, and re-layouts: none -> 76.7 us  [the longest x5 31 us: gathered(): return whole.reshape((dp_size, tensor_size) + shard.shape)]
    unnamed x18 -> x13, waiting for transfers between devices: 37.1 us -> 3.84 us
    convert_element_type x0 -> x7, local copies, waits for them, and re-layouts: none -> 28.5 us  [the longest x4 26 us: scattered(): flat = blocks.astype(bf16).reshape((-1,) + blocks.shape[-1:])]
    all_to_all x0 -> x4, waiting for transfers between devices: none -> 27.7 us  [exchange(): return lax.all_to_all(slots, axes, 0, 0, tiled=True)]
    psum x1 -> x0, blocking collectives: 24.7 us -> none  [on_device(): lax.psum((qv_bias_grad, proj_bias_grad, hidden_bias_grad, down_bias_grad)...]
  transfers between devices with their start and end apart: 16 -> 16, of which waited for: 13 -> 8; matrix products, arithmetic and copies ran while one was open for 9% -> 47% of each run, Pallas kernels for 0% -> 0%
where the time goes in v1:
time: 696 us; the launch traced here: 688 us
  local copies, waits for them, and re-layouts  253 us (36%)
  waiting for transfers between devices  196 us (28%)
  matrix products  108 us (16%)
  other arithmetic  68 us (10%)
  blocking collectives  25.9 us (4%)
  starting transfers between devices  21.2 us (3%)
  between operations  15.7 us (2%)
    all_gather x4, waiting for transfers between devices, gathered(): whole = lax.all_gather(shard, axes, axis=0)  94.6 us
    reduce_scatter x3, waiting for transfers between devices, scattered(): lax.psum_scatter(flat, 'tensor', scatter_dimension=0, tiled=True)  51.5 us
    unnamed x183, local copies, waits for them, and re-layouts  42 us
    reshape x5, local copies, waits for them, and re-layouts, gathered(): return whole.reshape((dp_size, tensor_size) + shard.shape)  31 us
    all_to_all x4, waiting for transfers between devices, exchange(): return lax.all_to_all(slots, axes, 0, 0, tiled=True)  27.7 us
    convert_element_type x4, local copies, waits for them, and re-layouts, scattered(): flat = blocks.astype(bf16).reshape((-1,) + blocks.shape[-1:])  26 us
    another operation x6, local copies, waits for them, and re-layouts, split_heads(): return matrix.reshape(group_latents, SEQ, head_count, HD)  23.3 us
    dot_general x4, matrix products, contract_cols(): lax.dot_general(left, right, (((1,), (1,)), ((), ())), preferred_element_...  22 us
  transfers between devices with their start and end apart: 16, of which 8 were waited for; matrix products, arithmetic and copies ran while one was open for 47% of the time, Pallas kernels for 0%

profile of v1, /device:TPU:0, one launch (start us, length us, event | category | flops | bytes accessed | tf_op | source)
XLA Modules:
  0.0 687.9 jit_solution(11701341772023649165)
XLA Ops:
  15.9 7.3 %all-to-all-start = ((bf16[32,2,2916]{2,1,0:T(2,128)(2,1)}), bf16[32,2,2916]{2,1,0:T(2,128)(2,1)S(1)}, u32[]{:S(2)}, u32[]{:S(2)}) async-start(bf16[32,2,2916]{2,1,0:T(2,128)(2,1)} %reshape.398), calls=%async_computation | async-start | bytes 753664 | tf_op jit(solution)/shard_map/all_to_all | solution.py:40
  24.1 12.3 %all-gather.4 = bf16[4,192,2]{1,2,0:T(2,128)(2,1)S(1)} all-gather(bf16[1,192,2]{1,2,0:T(2,128)(2,1)S(1)} %bitcast.325), channel_id=1, replica_groups=mesh['dp'=8,'tensor'=4] {'tensor'}, dimensions={0}, use_global_device_ids=true | all-gather | bytes 3840 | tf_op jit(solution)/shard_map/all_gather | solution.py:102
  40.9 5.3 all-to-all-start.1
  49.3 13.7 %all-gather.5 = bf16[4,1,768]{2,1,0:T(2,128)(2,1)S(1)} all-gather(bf16[1,1,768]{2,1,0:T(2,128)(2,1)S(1)} %reshape.373), channel_id=1, replica_groups=mesh['dp'=8,'tensor'=4] {'tensor'}, dimensions={0}, use_global_device_ids=true | all-gather | bytes 7680 | tf_op jit(solution)/shard_map/all_gather | solution.py:103
  92.4 43.0 %all-gather.11.cloned.1.call-done = bf16[96,96,192]{2,1,0:T(8,128)(2,1)} async-done(((bf16[3,96,192]{2,1,0:T(8,128)(2,1)}), bf16[96,96,192]{2,1,0:T(8,128)(2,1)}) %all-gather.11.cloned.1.call-update) | async-done | bytes 3538960 | tf_op jit(solution)/shard_map/all_gather | solution.py:73
  135.4 8.7 %copy.344 = bf16[8,4,3,96,192]{4,1,3,0,2:T(4,128)(2,1)} copy(bf16[8,4,3,96,192]{4,3,2,1,0:T(8,128)(2,1)} %bitcast.295) | data formatting | bytes 7077888 | tf_op jit(solution)/shard_map/reshape | solution.py:74
  144.1 9.0 %reshape.336 = bf16[3,768,768]{2,1,0:T(8,128)(2,1)} reshape(bf16[3,8,96,4,192]{4,3,2,1,0:T(4,128)(2,1)} %bitcast.264) | data formatting | bytes 7077888 | tf_op jit(solution)/shard_map/reshape | solution.py:98
  153.1 5.7 add_convert_fusion
  174.0 4.9 reshape.392
  178.9 4.6 copy.247
  183.5 6.2 fusion.75
  189.7 5.0 fusion.45
  206.5 8.5 %copy.350 = bf16[8,4,96,768]{3,1,2,0:T(4,128)(2,1)} copy(bf16[8,4,96,768]{3,2,1,0:T(8,128)(2,1)} %bitcast.293) | data formatting | bytes 9437184 | tf_op jit(solution)/shard_map/reshape | solution.py:74
  215.0 51.6 %all-gather.17.cloned.1.call-done = bf16[24576,96]{0,1:T(8,128)(2,1)} async-done(((bf16[768,96]{0,1:T(8,128)(2,1)}), bf16[24576,96]{0,1:T(8,128)(2,1)}) %all-gather.17.cloned.1.call-update) | async-done | bytes 4718608 | tf_op jit(solution)/shard_map/all_gather | solution.py:73
  266.6 7.4 %reshape.341 = bf16[8,4,768,96]{2,1,0,3:T(4,128)(2,1)} reshape(bf16[24576,96]{0,1:T(8,128)(2,1)} %all-gather.17.cloned.1.call-done) | data formatting | bytes 9437184 | tf_op jit(solution)/shard_map/reshape | solution.py:74
  281.2 9.7 %reshape.377 = bf16[768,3072,1]{1,0,2:T(8,128)(2,1)} reshape(bf16[8,96,4,768]{3,2,1,0:T(4,128)(2,1)} %bitcast.262) | data formatting | bytes 9437184 | tf_op jit(solution)/shard_map/reshape | solution.py:100
  298.6 11.8 %fusion.67 = (bf16[3072]{0:T(1024)(128)(2,1)}, bf16[768,3072]{1,0:T(8,128)(2,1)}, f32[768,3072]{1,0:T(8,128)}) fusion(f32[768,3072]{1,0:T(8,128)S(1)} %fusion.76, f32[3072]{0:T(1024)S(1)} %bitcast.320, bf16[768,768]{1,0:T(8,128)(2,1)S(1)} %copy-done.23, bf16[3072,768]{0,1:T(8,128)(2,1)S(1)} %bitcast.299), kind=kOutput, calls=%fused_computation.144 | convolution fusion | flops 3675780096 | bytes 29509632 | tf_op jit(solution)/shard_map/dot_general | solution.py:34
  310.4 8.5 %multiply_reduce_fusion.3 = (bf16[3,768]{1,0:T(4,128)(2,1)}, f32[3,256]{1,0:T(4,128)S(1)}, f32[3,256]{1,0:T(4,128)S(1)}, bf16[3,768]{1,0:T(4,128)(2,1)}, f32[3,2...) fusion(f32[3,768]{1,0:T(4,128)S(1)} %copy-done.44, f32[3,256]{1,0:T(4,128)S(1)} %rsqrt.26, f32[3,256]{1,0:T(4,128)S(1)} %copy-done.64, ...), kind=kOutput, calls=%fused_computation.48 | convolution fusion | flops 3630360576 | bytes 18914304 | tf_op jit(solution)/shard_map/dot_general | solution.py:34
  327.6 4.8 copy.261
  332.5 6.8 fusion.42
  340.0 5.1 multiply_reduce_fusion
  351.4 4.1 copy.281
  355.5 4.2 reshape.358
  362.0 4.1 stack_reshape.11
  366.1 11.5 %multiply_convert_fusion = bf16[3,12,256,256]{2,3,1,0:T(8,128)(2,1)} fusion(f32[3,12,256,256]{2,3,1,0:T(8,128)} %get-tuple-element.126, f32[3,12,256]{2,1,0:T(8,128)} %get-tuple-element.125, f32[3,12,256,256]{2,3,1,0:T(8,128)} %get-tuple-element.119, f32[3,12,256]{2,1,0:T(8,128)} %get-tuple-element.118), kind=kLoop, calls=%fused_computation.26 | loop fusion | flops 9437184 | bytes 23666688 | tf_op jit(solution)/shard_map/convert_element_type | solution.py:193
  383.2 4.1 stack_reshape.9
  393.4 4.2 stack_reshape.10
  401.0 4.4 convert_bitcast_fusion.1
  405.4 8.8 %convert_element_type.198 = bf16[3,8,96,4,192]{2,1,4,3,0:T(8,128)(2,1)} reshape(bf16[3,768,768]{1,2,0:T(8,128)(2,1)} %convert_bitcast_fusion.1) | data formatting | bytes 7077888 | tf_op jit(solution)/shard_map/convert_element_type | solution.py:275
  414.2 7.2 %copy.279 = bf16[3,8,96,4,192]{4,2,0,3,1:T(8,128)(2,1)} copy(bf16[3,8,96,4,192]{2,1,4,3,0:T(8,128)(2,1)} %convert_element_type.198) | data formatting | bytes 7077888 | tf_op jit(solution)/shard_map/convert_element_type | solution.py:275
  424.5 15.3 %fusion.15 = (bf16[3072,768]{0,1:T(8,128)(2,1)}, bf16[3072,768]{0,1:T(8,128)(2,1)}) fusion(f32[768,3072]{1,0:T(8,128)} %copy-done, f32[3072]{0:T(1024)S(1)} %bitcast.321, f32[768,3072]{1,0:T(8,128)} %get-tuple-element.123), kind=kLoop, calls=%fused_computation.21 | loop fusion | flops 54263808 | bytes 28323840 | tf_op jit(solution)/shard_map/convert_element_type | solution.py:156
  439.7 6.8 copy.302
  446.5 6.4 convert_bitcast_fusion
  453.0 5.8 copy.285
  458.8 7.5 %reshape.360 = bf16[24576,96]{0,1:T(8,128)(2,1)} reshape(bf16[8,4,768,96]{2,1,0,3:T(4,128)(2,1)} %copy.285) | data formatting | bytes 9437184 | tf_op jit(solution)/shard_map/reshape | solution.py:275
  466.4 6.7 copy.301
  474.9 8.1 %convolution_convert_fusion = bf16[8,96,4,768]{3,1,2,0:T(8,128)(2,1)} fusion(bf16[8,96,768,1]{2,1,3,0:T(8,128)(2,1)S(1)} %bitcast.303, bf16[4,768,768,1]{2,1,0,3:T(8,128)(2,1)} %bitcast.300), kind=kOutput, calls=%fused_computation.42 | convolution fusion | flops 3626237952 | bytes 10616832 | tf_op jit(solution)/shard_map/dot_general | solution.py:28
  489.1 9.1 %reshape.378 = bf16[3,768,768,1]{2,1,0,3:T(8,128)(2,1)} reshape(bf16[3,8,96,4,192]{4,3,2,1,0:T(4,128)(2,1)} %bitcast.265) | data formatting | bytes 7077888 | tf_op jit(solution)/shard_map/reshape | solution.py:98
  501.7 12.2 %multiply_add_fusion.2 = (f32[768,768]{0,1:T(8,128)}, f32[768,768]{0,1:T(8,128)}) fusion(f32[768,768]{0,1:T(8,128)S(1)} %get-tuple-element.96, f32[768,768]{0,1:T(8,128)} %copy.257, f32[768]{0:T(1024)S(1)} %convert_element_type.179, bf16[3072,768]{0,1:T(8,128)(2,1)} %bitcast.296, f32[768,3072]{1,0:T(8,128)} %copy-done, f32[3072]{0:T(1024)S(1)} %bitcast.322), kind=kOutput, calls=%fused_computation.60 | convolution fusion | flops 3649241088 | bytes 23608320 | tf_op jit(solution)/shard_map/dot_general | solution.py:158
  521.6 7.3 %fusion.28 = (bf16[3,768]{1,0:T(4,128)(2,1)S(1)}, f32[3,256]{1,0:T(4,128)S(1)}, f32[3,256]{1,0:T(4,128)S(1)}, bf16[3,768]{1,0:T(4,128)(2,1)S(1)}, f32[3,256,768,1]{2,1,0,3:T(8,128)S(1)}) fusion(f32[3,256,768]{2,1,0:T(8,128)} %bitcast.270, f32[3,256]{1,0:T(4,128)S(1)} %div.51, f32[3,256]{1,0:T(4,128)} %rsqrt.27, f32[3,768]{1,0:T(4,128)S(1)} %copy-done.41, ...), kind=kOutput, calls=%fused_computation.46 | convolution fusion | flops 2723211264 | bytes 11827200 | tf_op jit(solution)/shard_map/rjc,jdc->rd/dot_general | solution.py:219
  535.9 9.5 %reduce.13 = bf16[32,19968]{1,0:T(8,128)(2,1)} reduce(bf16[32,1,19968]{2,1,0:T(2,128)(2,1)S(1)} %broadcast_in_dim.8, bf16[]{:T(256)} %broadcast.233), dimensions={1}, to_apply=%broadcast_in_dim.8.reduce_sub_computation | reduce | bytes 2555906 | tf_op jit(solution)/shard_map/broadcast_in_dim | solution.py:44
  557.2 23.8 %all-to-all-done.2 = bf16[32,2,9984]{2,1,0:T(2,128)(2,1)} async-done(((bf16[32,2,9984]{2,1,0:T(2,128)(2,1)}), bf16[32,2,9984]{2,1,0:T(2,128)(2,1)}, u32[]{:S(2)}, u32[]{:S(2)}) %all-to-all-start.2) | async-done | bytes 1277984 | tf_op jit(solution)/shard_map/all_to_all | solution.py:40
  581.0 7.6 %reshape.403 = bf16[32,1,19968]{2,1,0:T(2,128)(2,1)S(1)} reshape(bf16[32,2,9984]{2,1,0:T(2,128)(2,1)} %all-to-all-done.2) | data formatting | bytes 2555904
  591.0 18.5 %reduce-scatter.17.cloned.1.call-done = bf16[384,768]{1,0:T(8,128)(2,1)} async-done(((bf16[3072,768]{1,0:T(8,128)(2,1)}), bf16[384,768]{1,0:T(8,128)(2,1)}) %reduce-scatter.17.cloned.1.call-update) | async-done | bytes 589840 | tf_op jit(solution)/shard_map/reduce_scatter | solution.py:276
  611.4 4.6 all-to-all-start.3
  624.3 9.4 %reduce-scatter.13.cloned.1.call-done = bf16[288,192]{1,0:T(8,128)(2,1)} async-done(((bf16[1152,192]{1,0:T(8,128)(2,1)}), bf16[288,192]{1,0:T(8,128)(2,1)}) %reduce-scatter.13.cloned.1.call-update) | async-done | bytes 110608 | tf_op jit(solution)/shard_map/reduce_scatter | solution.py:277
  635.4 21.3 %reduce-scatter.23.cloned.1.call-done = bf16[768,96]{0,1:T(8,128)(2,1)} async-done(((bf16[3072,96]{0,1:T(8,128)(2,1)}), bf16[768,96]{0,1:T(8,128)(2,1)}) %reduce-scatter.23.cloned.1.call-update) | async-done | bytes 147472 | tf_op jit(solution)/shard_map/reduce_scatter | solution.py:277
  658.3 20.8 %reduce-scatter.19.cloned.1.call-done = bf16[96,768]{1,0:T(8,128)(2,1)} async-done(((bf16[384,768]{1,0:T(8,128)(2,1)}), bf16[96,768]{1,0:T(8,128)(2,1)}) %reduce-scatter.19.cloned.1.call-update) | async-done | bytes 147472 | tf_op jit(solution)/shard_map/reduce_scatter | solution.py:277
  (343 shorter events, 179.0 us)
Async XLA Ops:
  7.2 80.6 %all-gather.13.cloned.1.call-start = ((), (), s32[]{:S(2)}) async-start(), calls=%async_computation.20 | async-start | bytes 1622016 | tf_op jit(solution)/shard_map/all_gather | solution.py:73
  7.9 127.4 %all-gather.11.cloned.1.call-start = ((), (), s32[]{:S(2)}) async-start(), calls=%async_computation.19 | async-start | bytes 4866048 | tf_op jit(solution)/shard_map/all_gather | solution.py:73
  8.7 197.8 %all-gather.15.cloned.1.call-start = ((), (), s32[]{:S(2)}) async-start(), calls=%async_computation.21 | async-start | bytes 4866048 | tf_op jit(solution)/shard_map/all_gather | solution.py:73
  9.4 257.2 %all-gather.17.cloned.1.call-start = ((), (), s32[]{:S(2)}) async-start(), calls=%async_computation.22 | async-start | bytes 4866048 | tf_op jit(solution)/shard_map/all_gather | solution.py:73
  12.6 10.6 %copy-start.32 = (bf16[768,768]{1,0:T(8,128)(2,1)S(1)}, bf16[768,768]{1,0:T(8,128)(2,1)}, u32[]{:S(2)}) copy-start(bf16[768,768]{1,0:T(8,128)(2,1)} %param.13) | copy-start | bytes 3538948
  14.8 9.3 %copy-start.69 = (bf16[144]{0:T(256)(128)(2,1)S(1)}, bf16[144]{0:T(256)(128)(2,1)}, u32[]{:S(2)}) copy-start(bf16[144]{0:T(256)(128)(2,1)} %param.16) | copy-start | bytes 868
  14.8 9.4 %copy-start.68 = (bf16[2,192]{1,0:T(2,128)(2,1)S(1)}, bf16[2,192]{1,0:T(2,128)(2,1)}, u32[]{:S(2)}) copy-start(bf16[2,192]{1,0:T(2,128)(2,1)} %param.18) | copy-start | bytes 2308
  15.9 21.7 %all-to-all-start = ((bf16[32,2,2916]{2,1,0:T(2,128)(2,1)}), bf16[32,2,2916]{2,1,0:T(2,128)(2,1)S(1)}, u32[]{:S(2)}, u32[]{:S(2)}) async-start(bf16[32,2,2916]{2,1,0:T(2,128)(2,1)} %reshape.398), calls=%async_computation | async-start | bytes 753664 | tf_op jit(solution)/shard_map/all_to_all | solution.py:40
  24.1 60.5 %copy-start.46 = (f32[768]{0:T(1024)}, f32[768]{0:T(1024)S(1)}, u32[]{:S(2)}) copy-start(f32[768]{0:T(1024)S(1)} %broadcast_multiply_fusion.5) | copy-start | bytes 9220
  39.6 9.1 %copy-start.67 = (bf16[768]{0:T(1024)(128)(2,1)S(1)}, bf16[768]{0:T(1024)(128)(2,1)}, u32[]{:S(2)}) copy-start(bf16[768]{0:T(1024)(128)(2,1)} %param.22) | copy-start | bytes 4612
  39.6 9.1 %copy-start.65 = (bf16[768]{0:T(1024)(128)(2,1)S(1)}, bf16[768]{0:T(1024)(128)(2,1)}, u32[]{:S(2)}) copy-start(bf16[768]{0:T(1024)(128)(2,1)} %param.20) | copy-start | bytes 4612
  40.9 22.7 %all-to-all-start.1 = ((f32[32,1,432]{2,1,0:T(1,128)}), f32[32,1,432]{2,1,0:T(1,128)S(1)}, u32[]{:S(2)}, u32[]{:S(2)}) async-start(f32[32,1,432]{2,1,0:T(1,128)} %reshape.400), calls=%async_computation.1 | async-start | bytes 131072 | tf_op jit(solution)/shard_map/all_to_all | solution.py:40
  46.2 426.9 %reduce-scatter.15.cloned.1.call-start = ((), (), s32[]{:S(2)}) async-start(), calls=%async_computation.14 | async-start | bytes 1327104 | tf_op jit(solution)/shard_map/reduce_scatter | solution.py:276
  65.9 15.5 %copy-start.42 = (f32[3,768]{1,0:T(4,128)}, f32[3,768]{1,0:T(4,128)S(1)}, u32[]{:S(2)}) copy-start(f32[3,768]{1,0:T(4,128)S(1)} %get-tuple-element.130) | copy-start | bytes 27652
  144.1 9.1 %copy-start.34 = (bf16[768,768,1]{0,1,2:T(8,128)(2,1)S(1)}, bf16[768,768,1]{0,1,2:T(8,128)(2,1)}, u32[]{:S(2)}) copy-start(bf16[768,768,1]{0,1,2:T(8,128)(2,1)} %fusion.50) | copy-start | bytes 3538948
  144.1 9.1 %copy-start.58 = (f32[3,768]{1,0:T(4,128)S(1)}, f32[3,768]{1,0:T(4,128)}, u32[]{:S(2)}) copy-start(f32[3,768]{1,0:T(4,128)} %maximum_convert_fusion) | copy-start | bytes 27652
  167.0 16.4 %copy-start.21 = (bf16[3,256,12,64]{1,3,2,0:T(8,128)(2,1)}, bf16[3,256,12,64]{1,3,2,0:T(8,128)(2,1)S(1)}, u32[]{:S(2)}) copy-start(bf16[3,256,12,64]{1,3,2,0:T(8,128)(2,1)S(1)} %copy.246) | copy-start | bytes 3538948
  174.0 9.5 %copy-start.12 = (bf16[3,256,12,64]{1,3,2,0:T(8,128)(2,1)}, bf16[3,256,12,64]{1,3,2,0:T(8,128)(2,1)S(1)}, u32[]{:S(2)}) copy-start(bf16[3,256,12,64]{1,3,2,0:T(8,128)(2,1)S(1)} %copy.245) | copy-start | bytes 3538948
  206.5 88.0 %copy-start.28 = (bf16[768,768]{0,1:T(8,128)(2,1)}, bf16[768,768]{0,1:T(8,128)(2,1)S(1)}, u32[]{:S(2)}) copy-start(bf16[768,768]{0,1:T(8,128)(2,1)S(1)} %add_convert_fusion.1) | copy-start | bytes 3538948
  291.0 7.5 %slice-start.3 = ((s8[4718592]{0:T(1024)(128)(4,1)}), s8[4194304]{0:T(1024)(128)(4,1)S(1)}, s32[]{:S(2)}) async-start(s8[4718592]{0:T(1024)(128)(4,1)} %bitcast.297), calls=%async_computation.27 | async-start | bytes 8388608
  298.4 11.9 %copy-start = (f32[768,3072]{1,0:T(8,128)}, f32[768,3072]{1,0:T(8,128)S(1)}, u32[]{:S(2)}) copy-start(f32[768,3072]{1,0:T(8,128)S(1)} %fusion.76) | copy-start | bytes 28311556
  298.5 11.9 %copy-start.3 = (f32[768,768]{1,0:T(8,128)S(1)}, f32[768,768]{1,0:T(8,128)}, u32[]{:S(2)}) copy-start(f32[768,768]{1,0:T(8,128)} %copy.258) | copy-start | bytes 7077892
  298.5 11.9 %copy-start.5 = (f32[768,768]{1,0:T(8,128)S(1)}, f32[768,768]{1,0:T(8,128)}, u32[]{:S(2)}) copy-start(f32[768,768]{1,0:T(8,128)} %copy.259) | copy-start | bytes 7077892
  298.5 11.9 %copy-start.44 = (f32[3,768]{1,0:T(4,128)S(1)}, f32[3,768]{1,0:T(4,128)}, u32[]{:S(2)}) copy-start(f32[3,768]{1,0:T(4,128)} %get-tuple-element.129) | copy-start | bytes 27652
  298.5 11.9 %copy-start.45 = (f32[3,768]{1,0:T(4,128)S(1)}, f32[3,768]{1,0:T(4,128)}, u32[]{:S(2)}) copy-start(f32[3,768]{1,0:T(4,128)} %get-tuple-element.133) | copy-start | bytes 27652
  298.5 11.9 %copy-start.64 = (f32[3,256]{1,0:T(4,128)S(1)}, f32[3,256]{1,0:T(4,128)}, u32[]{:S(2)}) copy-start(f32[3,256]{1,0:T(4,128)} %div.48) | copy-start | bytes 9220
  310.4 8.5 %copy-start.16 = (bf16[768,768]{1,0:T(8,128)(2,1)S(1)}, bf16[768,768]{1,0:T(8,128)(2,1)}, u32[]{:S(2)}) copy-start(bf16[768,768]{1,0:T(8,128)(2,1)} %param.25) | copy-start | bytes 3538948
  327.6 11.6 %slice-start = ((s8[9437184]{0:T(1024)(128)(4,1)}), s8[1048576]{0:T(1024)(128)(4,1)S(1)}, s32[]{:S(2)}) async-start(s8[9437184]{0:T(1024)(128)(4,1)} %bitcast.276), calls=%async_computation.24 | async-start | bytes 2097152
  332.4 6.8 slice-start.1
  332.5 6.8 slice-start.2
  332.5 6.8 copy-start.36
  332.5 7.5 %copy-start.38 = (bf16[3,256,12,64]{1,3,2,0:T(8,128)(2,1)S(1)}, bf16[3,256,12,64]{1,3,2,0:T(8,128)(2,1)}, u32[]{:S(2)}) copy-start(bf16[3,256,12,64]{1,3,2,0:T(8,128)(2,1)} %copy.261) | copy-start | bytes 3538948
  359.7 191.5 %reduce-scatter.11.cloned.1.call-start = ((), (), s32[]{:S(2)}) async-start(), calls=%async_computation.12 | async-start | bytes 5308416 | tf_op jit(solution)/shard_map/reduce_scatter | solution.py:276
  366.1 11.5 %copy-start.22 = (bf16[3,256,12,64]{1,3,2,0:T(8,128)(2,1)S(1)}, bf16[3,256,12,64]{1,3,2,0:T(8,128)(2,1)}, u32[]{:S(2)}) copy-start(bf16[3,256,12,64]{1,3,2,0:T(8,128)(2,1)} %copy-done.21) | copy-start | bytes 3538948
  421.4 130.4 %reduce-scatter.21.cloned.1.call-start = ((), (), s32[]{:S(2)}) async-start(), calls=%async_computation.17 | async-start | bytes 5308416 | tf_op jit(solution)/shard_map/reduce_scatter | solution.py:276
  466.3 89.3 %reduce-scatter.25.cloned.1.call-start = ((), (), s32[]{:S(2)}) async-start(), calls=%async_computation.23 | async-start | bytes 245760
  466.4 8.6 %copy-start.29 = (bf16[768,768]{0,1:T(8,128)(2,1)S(1)}, bf16[768,768]{0,1:T(8,128)(2,1)}, u32[]{:S(2)}) copy-start(bf16[768,768]{0,1:T(8,128)(2,1)} %copy-done.28) | copy-start | bytes 3538948
  474.9 134.6 %reduce-scatter.17.cloned.1.call-start = ((), (), s32[]{:S(2)}) async-start(), calls=%async_computation.15 | async-start | bytes 5308416 | tf_op jit(solution)/shard_map/reduce_scatter | solution.py:276
  521.5 7.4 %copy-start.4 = (f32[768,768]{1,0:T(8,128)S(1)}, f32[768,768]{1,0:T(8,128)}, u32[]{:S(2)}) copy-start(f32[768,768]{1,0:T(8,128)} %copy.258) | copy-start | bytes 7077892
  521.5 7.4 %copy-start.6 = (f32[768,768]{1,0:T(8,128)S(1)}, f32[768,768]{1,0:T(8,128)}, u32[]{:S(2)}) copy-start(f32[768,768]{1,0:T(8,128)} %copy.259) | copy-start | bytes 7077892
  521.5 7.4 %copy-start.9 = (f32[3,256,768]{2,1,0:T(8,128)S(1)}, f32[3,256,768]{2,1,0:T(8,128)}, u32[]{:S(2)}) copy-start(f32[3,256,768]{2,1,0:T(8,128)} %get-tuple-element.92) | copy-start | bytes 7077892
  521.6 7.4 %copy-start.55 = (f32[3,256]{1,0:T(4,128)S(1)}, f32[3,256]{1,0:T(4,128)}, u32[]{:S(2)}) copy-start(f32[3,256]{1,0:T(4,128)} %rsqrt.27) | copy-start | bytes 9220
  547.7 33.3 %all-to-all-start.2 = ((bf16[32,2,9984]{2,1,0:T(2,128)(2,1)}), bf16[32,2,9984]{2,1,0:T(2,128)(2,1)}, u32[]{:S(2)}, u32[]{:S(2)}) async-start(bf16[32,2,9984]{2,1,0:T(2,128)(2,1)} %reshape.402), calls=%async_computation.2 | async-start | bytes 2555904 | tf_op jit(solution)/shard_map/all_to_all | solution.py:40
  551.2 82.5 %reduce-scatter.13.cloned.1.call-start = ((), (), s32[]{:S(2)}) async-start(), calls=%async_computation.13 | async-start | bytes 737280 | tf_op jit(solution)/shard_map/reduce_scatter | solution.py:277
  551.8 104.9 %reduce-scatter.23.cloned.1.call-start = ((), (), s32[]{:S(2)}) async-start(), calls=%async_computation.18 | async-start | bytes 737280 | tf_op jit(solution)/shard_map/reduce_scatter | solution.py:277
  552.5 126.6 %reduce-scatter.19.cloned.1.call-start = ((), (), s32[]{:S(2)}) async-start(), calls=%async_computation.16 | async-start | bytes 737280 | tf_op jit(solution)/shard_map/reduce_scatter | solution.py:277
  590.4 33.3 %copy-start.54 = (bf16[3,768]{1,0:T(4,128)(2,1)S(1)}, bf16[3,768]{1,0:T(4,128)(2,1)}, u32[]{:S(2)}) copy-start(bf16[3,768]{1,0:T(4,128)(2,1)} %param.14) | copy-start | bytes 13828
  611.4 12.2 %all-to-all-start.3 = ((f32[32,3,24]{2,1,0:T(4,128)}), f32[32,3,24]{2,1,0:T(4,128)S(1)}, u32[]{:S(2)}, u32[]{:S(2)}) async-start(f32[32,3,24]{2,1,0:T(4,128)} %copy.276), calls=%async_computation.3 | async-start | bytes 131072 | tf_op jit(solution)/shard_map/all_to_all | solution.py:40
  (43 other events, 114.3 us)
Sparse Core Ops, SparseCore 0:
  10.9 59.1 all-gather.12
  72.9 62.4 all-gather.10
  138.2 62.3 all-gather.14
  203.3 63.2 all-gather.16
  359.9 34.9 reduce-scatter.14
  421.5 52.1 reduce-scatter.10
  477.1 53.8 reduce-scatter.20
  534.0 19.3 reduce-scatter.24
  556.8 52.6 reduce-scatter.16
  611.7 21.9 reduce-scatter.12
  636.1 20.5 reduce-scatter.22
  658.9 20.1 reduce-scatter.18

commit v2 on v1

v2 whole, which is shorter than its diff:
```python
import functools

import jax
import jax.numpy as jnp
from jax import lax
from jax.experimental import pallas as pl
from jax.experimental.pallas import tpu as pltpu
from jax.sharding import PartitionSpec as P

D = 768
HD = 64
SEQ = 256
BF16 = jnp.bfloat16
F32 = jnp.float32


def normalize_rows(values):
    centre = values - jnp.mean(values, axis=-1, keepdims=True)
    inverse = lax.rsqrt(jnp.mean(centre * centre, axis=-1, keepdims=True) + 1e-06)
    return (centre * inverse, inverse)


def norm_backward(grad_normed, normed, inverse):
    return inverse * (
        grad_normed
        - jnp.mean(grad_normed, axis=-1, keepdims=True)
        - normed * jnp.mean(grad_normed * normed, axis=-1, keepdims=True)
    )


def contract(left, right, left_axis, right_axis):
    return lax.dot_general(
        left, right, (((left_axis,), (right_axis,)), ((), ())), preferred_element_type=F32
    )


def matrix(ref, *place):
    block = ref[(slice(None),) + place]
    return block.reshape(-1, block.shape[-1])


def column_sum(values):
    return jnp.sum(values, axis=0, keepdims=True)


def head_masks(width):
    lanes = lax.broadcasted_iota(jnp.int32, (1, width), 1)
    return [
        ((lanes >= start) & (lanes < start + HD)).astype(F32).astype(BF16)
        for start in range(0, width, HD)
    ]


def head_probs(query, key):
    scores = contract(query, key, 1, 1) * HD ** (-0.5)
    raised = jnp.exp(scores - jnp.max(scores, axis=-1, keepdims=True))
    return raised * (1.0 / jnp.sum(raised, axis=-1, keepdims=True))


def attend_kernel(rows, modulation, weight, bias, input_ref, qkv_ref, mixed_ref):
    normed, _ = normalize_rows(rows[...].astype(F32))
    pieces = modulation[0]
    inputs = (normed * (1.0 + pieces[1:2]) + pieces[0:1]).astype(BF16)
    input_ref[...] = inputs
    masks = head_masks(qkv_ref.shape[-1])
    for part in range(qkv_ref.shape[0]):
        query = (contract(inputs, matrix(weight, part, 0), 1, 0) + bias[part, 0:1].astype(F32)).astype(BF16)
        key = contract(inputs, matrix(weight, part, 1), 1, 0).astype(BF16)
        value = (contract(inputs, matrix(weight, part, 2), 1, 0) + bias[part, 1:2].astype(F32)).astype(BF16)
        qkv_ref[part, 0] = query
        qkv_ref[part, 1] = key
        qkv_ref[part, 2] = value
        mixed = None
        for mask in masks:
            probs = head_probs(query * mask, key).astype(BF16)
            own = contract(probs, value * mask, 1, 0)
            mixed = own if mixed is None else mixed + own
        mixed_ref[part] = mixed.astype(BF16)


def block_kernel(
    mixed,
    rows,
    upstream_rows,
    modulation,
    proj,
    proj_bias,
    hidden,
    hidden_bias,
    down,
    down_bias,
    out_ref,
    act_ref,
    preact_grad_ref,
    mlp_grad_ref,
    input_ref,
    middle_grad_ref,
    attended_grad_ref,
    pieces_ref,
    sums_ref,
):
    parts = act_ref.shape[0]
    pieces = modulation[0]
    gate_one, shift_two, scale_two, gate_two = [pieces[k : k + 1] for k in (2, 3, 4, 5)]
    attended = proj_bias[...].astype(F32)
    for part in range(parts):
        attended = attended + contract(mixed[part], matrix(proj, part), 1, 1)
    middle = rows[...].astype(F32) + gate_one * attended
    normed, inverse = normalize_rows(middle)
    inputs = (normed * (1.0 + scale_two) + shift_two).astype(BF16)
    input_ref[...] = inputs
    upstream = upstream_rows[...].astype(F32)
    mlp_grad = (gate_two * upstream).astype(BF16)
    mlp_grad_ref[...] = mlp_grad

    @pl.when(pl.program_id(0) == 0)
    def _():
        sums_ref[...] = jnp.zeros_like(sums_ref)

    mlp = down_bias[...].astype(F32)
    input_grad = None
    root = 0.7978845608028654
    for part in range(parts):
        hidden_part = matrix(hidden, part)
        down_part = matrix(down, part)
        preact = contract(inputs, hidden_part, 1, 0) + hidden_bias[part : part + 1].astype(F32)
        square = preact * preact
        bent = jnp.tanh(root * preact * (1.0 + 0.044715 * square))
        half = 0.5 + 0.5 * bent
        activated = (preact * half).astype(BF16)
        slope = half + (0.5 * root) * preact * (1.0 - bent * bent) * (1.0 + (3 * 0.044715) * square)
        act_ref[part] = activated
        mlp = mlp + contract(activated, down_part, 1, 1)
        preact_grad = (contract(mlp_grad, down_part, 1, 0) * slope).astype(BF16)
        preact_grad_ref[part] = preact_grad
        sums_ref[part : part + 1] += column_sum(preact_grad.astype(F32))
        own = contract(preact_grad, hidden_part, 1, 1)
        input_grad = own if input_grad is None else input_grad + own
    out_ref[...] = middle + gate_two * mlp
    middle_grad = upstream + norm_backward(input_grad * (1.0 + scale_two), normed, inverse)
    middle_grad_ref[...] = middle_grad
    attended_grad = (gate_one * middle_grad).astype(BF16)
    attended_grad_ref[...] = attended_grad
    pieces_ref[0, 0:1] = column_sum(middle_grad * attended)
    pieces_ref[0, 1:2] = column_sum(input_grad)
    pieces_ref[0, 2:3] = column_sum(input_grad * normed)
    pieces_ref[0, 3:4] = column_sum(upstream * mlp)
    sums_ref[parts : parts + 1] += column_sum(attended_grad.astype(F32))
    sums_ref[parts + 1 : parts + 2] += column_sum(mlp_grad.astype(F32))


def attend_back_kernel(attended_grad, qkv, proj, grad_ref, sums_ref):
    width = qkv.shape[-1]
    masks = head_masks(width)

    @pl.when(pl.program_id(0) == 0)
    def _():
        sums_ref[...] = jnp.zeros_like(sums_ref)

    for part in range(qkv.shape[0]):
        query, key, value = qkv[part, 0], qkv[part, 1], qkv[part, 2]
        mixed_grad = contract(attended_grad[...], matrix(proj, part), 1, 0).astype(BF16)
        totals = [None, None, None]
        for mask in masks:
            own_query, own_grad = query * mask, mixed_grad * mask
            probs = head_probs(own_query, key)
            probs_grad = contract(own_grad, value, 1, 1)
            scores_grad = (
                probs * (probs_grad - jnp.sum(probs * probs_grad, axis=-1, keepdims=True))
            ).astype(BF16)
            own = (
                contract(scores_grad, key * mask, 1, 0),
                contract(scores_grad, own_query, 0, 0),
                contract(probs.astype(BF16), own_grad, 0, 0),
            )
            totals = [new if old is None else old + new for old, new in zip(totals, own)]
        for kind, factor in enumerate((HD ** (-0.5), HD ** (-0.5), 1.0)):
            low = (totals[kind] * factor).astype(BF16)
            grad_ref[part, kind] = low
            sums_ref[part, kind : kind + 1] += column_sum(low.astype(F32))


def entry_back_kernel(qkv_grad, weight, rows, modulation, middle_grad, grad_ref, pieces_ref):
    input_grad = None
    for part in range(qkv_grad.shape[0]):
        for kind in range(3):
            own = contract(qkv_grad[part, kind], matrix(weight, part, kind), 1, 1)
            input_grad = own if input_grad is None else input_grad + own
    normed, inverse = normalize_rows(rows[...].astype(F32))
    pieces = modulation[0]
    grad_ref[...] = middle_grad[...] + norm_backward(
        input_grad * (1.0 + pieces[1:2]), normed, inverse
    )
    pieces_ref[0, 0:1] = column_sum(input_grad)
    pieces_ref[0, 1:2] = column_sum(input_grad * normed)


def weight_kernel(left, right, grad_ref):
    grad = contract(left[...], right[0], 0, 0)
    grad_ref[:, 0] = grad.reshape(grad_ref.shape[0], grad_ref.shape[2], -1).astype(BF16)


def whole(array, first=0):
    return pl.BlockSpec(
        array.shape, lambda step: (0,) * array.ndim, pipeline_mode=pl.Buffered(1)
    )


def row_block(array, first=0):
    lead = array.shape[:-2]
    return pl.BlockSpec(
        lead + (SEQ, array.shape[-1]), lambda step: (0,) * len(lead) + (step + first, 0)
    )


def per_latent(array, first=0):
    return pl.BlockSpec((1,) + array.shape[1:], lambda step: (step + first, 0, 0))


def kept(array, first=0):
    return pl.BlockSpec(array.shape, lambda step: (0,) * array.ndim)


def over_latents(kernel, steps, inputs, outputs, flops, first=0, carried=()):
    shapes = [jax.ShapeDtypeStruct(shape, kind) for _, shape, kind in outputs]
    moved = sum(a.size * a.dtype.itemsize for _, a in inputs) + sum(
        s.size * s.dtype.itemsize for s in shapes
    )
    taken = len(inputs)

    def body(*refs):
        kernel(*refs[:taken], *refs[taken + len(carried) :])

    return pl.pallas_call(
        body,
        grid=(steps,),
        in_specs=[spec(array, first) for spec, array in inputs]
        + [pl.BlockSpec(memory_space=pl.ANY) for _ in carried],
        out_specs=[spec(shape, first) for (spec, _, _), shape in zip(outputs, shapes)],
        out_shape=shapes,
        input_output_aliases={taken + number: number for number in range(len(carried))},
        cost_estimate=pl.CostEstimate(flops=flops, transcendentals=0, bytes_accessed=moved),
        compiler_params=pltpu.CompilerParams(vmem_limit_bytes=56 << 20),
    )(*[array for _, array in inputs], *carried)


class Flow:
    def __init__(self, stages):
        self.stages = stages
        self.pending = next(stages)
        self.value = None

    def advance(self, results):
        try:
            self.pending = self.stages.send(results)
        except StopIteration as end:
            self.value = end.value


def settle_kernel(place, own, other, whole_ref):
    flip = place[0]
    for pair in range(own.shape[0]):
        for core, source in enumerate((own, other)):
            slot = jnp.bitwise_xor(2 * pair + core, flip)
            whole_ref[0, slot] = source[pair, 0]


def settle_heads_kernel(place, own, other, qkv_ref, proj_ref):
    flip = place[0]
    width = proj_ref.shape[-1]
    for pair in range(own.shape[0]):
        for core, source in enumerate((own, other)):
            slot = jnp.bitwise_xor(2 * pair + core, flip)
            block = source[pair, 0]
            for kind in range(3):
                qkv_ref[0, kind, slot] = block[:, kind * width : (kind + 1) * width]
            proj_ref[0, slot] = block[:, 3 * width :]


def split_rows(place, grad, keep_ref, send_ref, lanes):
    slab = keep_ref.shape[2]
    core = jnp.bitwise_and(place[0], 1)
    flip = place[0] // 2
    for pair in range(keep_ref.shape[0]):
        low = grad[2 * pair * slab : (2 * pair + 1) * slab]
        high = grad[(2 * pair + 1) * slab : (2 * pair + 2) * slab]
        slot = jnp.bitwise_xor(pair, flip)
        keep_ref[slot, 0, :, lanes] = jnp.where(core == 0, low, high)
        send_ref[slot, 0, :, lanes] = jnp.where(core == 0, high, low).astype(BF16)


def weight_split_kernel(place, left, right, keep_ref, send_ref):
    split_rows(place, contract(left[...], right[0], 0, 0), keep_ref, send_ref, slice(None))


def heads_split_kernel(place, entry, qkv_grad, outer, mixed, keep_ref, send_ref):
    width = mixed.shape[-1]
    for kind in range(3):
        grad = contract(entry[...], qkv_grad[0, kind], 0, 0)
        split_rows(place, grad, keep_ref, send_ref, slice(kind * width, (kind + 1) * width))
    grad = contract(outer[...], mixed[0], 0, 0)
    split_rows(place, grad, keep_ref, send_ref, slice(3 * width, 4 * width))


def placed_call(kernel, place, steps, inputs, outputs, flops):
    shapes = [jax.ShapeDtypeStruct(shape, kind) for _, shape, kind in outputs]
    moved = sum(a.size * a.dtype.itemsize for _, a in inputs) + sum(
        s.size * s.dtype.itemsize for s in shapes
    )
    return pl.pallas_call(
        kernel,
        grid_spec=pltpu.PrefetchScalarGridSpec(
            num_scalar_prefetch=1,
            grid=(steps,),
            in_specs=[spec(array) for spec, array in inputs],
            out_specs=[spec(shape) for (spec, _, _), shape in zip(outputs, shapes)],
        ),
        out_shape=shapes,
        cost_estimate=pl.CostEstimate(flops=flops, transcendentals=0, bytes_accessed=moved),
        compiler_params=pltpu.CompilerParams(vmem_limit_bytes=56 << 20),
    )(place, *[array for _, array in inputs])


def resident(array):
    return pl.BlockSpec(
        array.shape, lambda step, place: (0,) * array.ndim, pipeline_mode=pl.Buffered(1)
    )


def by_first(array):
    rest = (0,) * (array.ndim - 1)
    return pl.BlockSpec((1,) + array.shape[1:], lambda step, place: (step,) + rest)


def to_first(array):
    rest = (0,) * (array.ndim - 1)
    return pl.BlockSpec(
        (1,) + array.shape[1:], lambda step, place: (jnp.bitwise_xor(step, place[1]),) + rest
    )


def by_second(array):
    shape = array.shape
    return pl.BlockSpec((shape[0], 1) + shape[2:], lambda step, place: (0, step, 0, 0))


def to_second(array):
    shape = array.shape
    return pl.BlockSpec(
        (shape[0], 1) + shape[2:], lambda step, place: (0, jnp.bitwise_xor(step, place[1]), 0, 0)
    )


def weight_grad(left, right, groups=1):
    batch, tokens, width = right.shape
    shape = (groups, batch, D // groups, width)
    return pl.pallas_call(
        weight_kernel,
        grid=(batch,),
        in_specs=[whole(left), pl.BlockSpec((1, tokens, width), lambda step: (step, 0, 0))],
        out_specs=pl.BlockSpec(
            (groups, 1, D // groups, width), lambda step: (0, step, 0, 0)
        ),
        out_shape=jax.ShapeDtypeStruct(shape, BF16),
        cost_estimate=pl.CostEstimate(
            flops=2 * D * batch * tokens * width, transcendentals=0, bytes_accessed=4 * D * batch * width
        ),
        compiler_params=pltpu.CompilerParams(vmem_limit_bytes=56 << 20),
    )(left, right)


def exchange(slots, axes):
    return lax.all_to_all(slots, axes, 0, 0, tiled=True)


def on_device(
    latents_in,
    condition,
    ada_weight,
    ada_bias,
    qkv_weight,
    qv_bias,
    proj_weight,
    proj_bias,
    hidden_weight,
    hidden_bias,
    down_weight,
    down_bias,
    upstream_grad,
    dp_size,
    tensor_size,
):
    axes = ("dp", "tensor")
    count = dp_size * tensor_size
    latents = condition.shape[0]
    tokens = latents_in.shape[0]
    ada_rows, ada_cols = ada_weight.shape[0], ada_bias.shape[0]
    here = lax.axis_index("dp") * tensor_size + lax.axis_index("tensor")
    place = lax.axis_index("tensor")
    slab = D // dp_size
    direct = dp_size == 8 and tensor_size == 4 and slab % 16 == 0
    head_width, hidden_width = qkv_weight.shape[2], hidden_weight.shape[1]

    silu_value, silu_pullback = jax.vjp(jax.nn.silu, condition.astype(F32))
    silu_cond = silu_value.astype(BF16)
    sent = jnp.concatenate(
        [
            ada_weight.reshape(ada_rows, count, ada_cols).transpose(1, 0, 2).reshape(count, -1),
            silu_cond.reshape(latents, count, ada_rows).transpose(1, 0, 2).reshape(count, -1),
            jnp.broadcast_to(
                jnp.concatenate([silu_cond.reshape(-1), qv_bias.reshape(-1), hidden_bias])[None],
                (count, latents * D + 2 * head_width + hidden_width),
            ),
        ],
        axis=1,
    )
    def swap(array, mask):
        return lax.ppermute(array, axes, [(device, device ^ mask) for device in range(count)])

    def slot(flows, inputs, run):
        moving = [[array for array, _ in flow.pending] for flow in flows]
        moving, inputs = lax.optimization_barrier((moving, inputs))
        results = [
            [swap(array, mask) for array, (_, mask) in zip(arrays, flow.pending)]
            for arrays, flow in zip(moving, flows)
        ]
        results, made = lax.optimization_barrier((results, run(*inputs)))
        for flow, arrived in zip(flows, results):
            flow.advance(arrived)
        return made

    across, along, upward = [tensor_size << bit for bit in range(3)]
    half = tensor_size // 2
    position = jnp.stack([lax.axis_index("dp"), place])

    def gather_stages(shard):
        line = yield [(shard, mask) for mask in range(1, tensor_size)]
        line = jnp.stack([shard] + line)
        side, above = yield [(line, along), (line, upward)]
        first, second = yield [(side[:half], upward), (above[half:], along)]
        own = jnp.stack([line, side, above, jnp.concatenate([first, second])])
        (other,) = yield [(own, across)]
        return own, other

    def reduce_stages(keep, send):
        (arrived,) = yield [(send, across)]
        summed = keep + arrived.astype(F32)
        line, side, above, far = [summed[number] for number in range(4)]
        low = [block.astype(BF16) for block in (side[:half], above[half:], far[:half], far[half:])]
        arrived = yield list(zip(low, (along, upward, along, upward)))
        side_low, above_high, far_low, far_high = [block.astype(F32) for block in arrived]
        arrived = yield [
            ((above[:half] + far_low).astype(BF16), upward),
            ((side[half:] + far_high).astype(BF16), along),
        ]
        low = line[:half] + side_low + arrived[0].astype(F32)
        high = line[half:] + above_high + arrived[1].astype(F32)
        pieces = [low[number] for number in range(half)] + [high[number] for number in range(half)]
        arrived = yield [(pieces[mask].astype(BF16), mask) for mask in range(1, tensor_size)]
        return sum([block.astype(F32) for block in arrived], pieces[0])

    def gathered(shard):
        whole_set = lax.all_gather(shard, axes, axis=0)
        whole_set = whole_set.reshape((dp_size, tensor_size) + shard.shape)
        rows = whole_set.ndim - 2
        whole_set = jnp.moveaxis(whole_set, 0, rows - 1)
        return whole_set.reshape((1,) + whole_set.shape[: rows - 1] + (D, shard.shape[-1]))

    def scattered(blocks):
        blocks = blocks[0].reshape(-1, dp_size, slab, blocks.shape[-1]).swapaxes(0, 1)
        flat = blocks.reshape(-1, blocks.shape[-1])
        flat = lax.psum_scatter(flat, "dp", scatter_dimension=0, tiled=True)
        return lax.psum_scatter(flat, "tensor", scatter_dimension=0, tiled=True).astype(F32)

    def settled(own, other):
        shape = (tensor_size, dp_size, slab, D)
        (whole_set,) = placed_call(
            settle_kernel,
            position,
            tensor_size,
            [(by_second, own), (by_second, other)],
            [(to_first, shape, BF16)],
            0,
        )
        return whole_set.reshape(1, tensor_size, D, D)

    def settled_heads(own, other):
        qkv_set, proj_set = placed_call(
            settle_heads_kernel,
            position,
            tensor_size,
            [(by_second, own), (by_second, other)],
            [
                (to_first, (tensor_size, 3, dp_size, slab, head_width), BF16),
                (to_first, (tensor_size, dp_size, slab, head_width), BF16),
            ],
            0,
        )
        return (
            qkv_set.reshape(1, tensor_size, 3, D, head_width),
            proj_set.reshape(1, tensor_size, D, head_width),
        )

    ends = [ada_rows * ada_cols]
    for size in (ada_rows * latents, latents * D, 2 * head_width):
        ends.append(ends[-1] + size)

    def modulate(silu_all, ada_columns):
        columns = jnp.dot(silu_all, ada_columns, preferred_element_type=F32) + ada_bias.astype(F32)
        back = exchange(columns.reshape(count, latents, ada_cols), axes)
        return back.transpose(1, 0, 2).reshape(latents, 6, D)

    heads_in = hidden_in = down_in = None
    if direct:
        heads_in, hidden_in, down_in = [
            Flow(gather_stages(shard))
            for shard in (
                jnp.concatenate(list(qkv_weight) + [proj_weight.T], axis=1),
                hidden_weight,
                down_weight.T,
            )
        ]
    got = slot([heads_in] if direct else [], (sent,), lambda slots: exchange(slots, axes))
    ada_columns = got[:, : ends[0]].reshape(D, ada_cols)
    silu_columns = got[:, ends[0] : ends[1]].reshape(count * latents, ada_rows)
    silu_all = got[:, ends[1] : ends[2]].reshape(count * latents, D)
    qv_full = got[:tensor_size, ends[2] : ends[3]].reshape(tensor_size, 2, head_width)
    hidden_bias_full = got[:tensor_size, ends[3] :]
    modulation = slot(
        [heads_in, hidden_in] if direct else [], (silu_all, ada_columns), modulate
    )
    if direct:
        slot([heads_in, hidden_in, down_in], (), lambda: ())
        slot([heads_in, hidden_in, down_in], (), lambda: ())
        qkv_full, proj_full = settled_heads(*heads_in.value)
    else:
        qkv_full = gathered(qkv_weight)
        proj_full = gathered(proj_weight.T)
        hidden_full = gathered(hidden_weight)
        down_full = gathered(down_weight.T)

    def spread(*last):
        return (tensor_size,) + last

    unit = 2 * tokens * D * D

    def attend(rows, pieces, weight, bias):
        return over_latents(
            attend_kernel,
            latents,
            [(row_block, rows), (per_latent, pieces), (whole, weight), (whole, bias)],
            [
                (row_block, (tokens, D), BF16),
                (row_block, spread(3, tokens, head_width), BF16),
                (row_block, spread(tokens, head_width), BF16),
            ],
            5 * unit,
        )

    input_one, qkv, mixed = slot(
        [hidden_in, down_in] if direct else [],
        (latents_in, modulation, qkv_full, qv_full),
        attend,
    )
    if direct:
        hidden_full = slot([down_in], hidden_in.value, settled)
        down_full = settled(*down_in.value)
    (
        block_out,
        activated,
        preact_grad,
        mlp_grad,
        input_two,
        middle_grad,
        attended_grad,
        late_pieces,
        late_sums,
    ) = over_latents(
        block_kernel,
        latents,
        [
            (row_block, mixed),
            (row_block, latents_in),
            (row_block, upstream_grad),
            (per_latent, modulation),
            (whole, proj_full),
            (whole, proj_bias[None]),
            (whole, hidden_full),
            (whole, hidden_bias_full),
            (whole, down_full),
            (whole, down_bias[None]),
        ],
        [
            (row_block, (tokens, D), F32),
            (row_block, spread(tokens, hidden_width), BF16),
            (row_block, spread(tokens, hidden_width), BF16),
            (row_block, (tokens, D), BF16),
            (row_block, (tokens, D), BF16),
            (row_block, (tokens, D), F32),
            (row_block, (tokens, D), BF16),
            (per_latent, (latents, 4, D), F32),
            (kept, (tensor_size + 2, D), F32),
        ],
        18 * unit,
    )

    split_shape = (dp_size // 2, tensor_size, slab, D)
    split_out = [(to_second, split_shape, F32), (to_second, split_shape, BF16)]

    def square_grad(left, right):
        return placed_call(
            weight_split_kernel,
            position,
            tensor_size,
            [(resident, left), (by_first, right)],
            split_out,
            4 * unit,
        )

    def heads_grad(entry, heads, outer, inner):
        return placed_call(
            heads_split_kernel,
            position,
            tensor_size,
            [(resident, entry), (by_first, heads), (resident, outer), (by_first, inner)],
            split_out,
            4 * unit,
        )

    def attend_back(first, steps, carried):
        def run(outer, heads, weight, *kept_back):
            return over_latents(
                attend_back_kernel,
                steps,
                [(row_block, outer), (row_block, heads), (whole, weight)],
                [
                    (row_block, spread(3, tokens, head_width), BF16),
                    (kept, spread(3, head_width), F32),
                ],
                4 * unit * steps,
                first,
                kept_back,
            )

        return (attended_grad, qkv, proj_full) + carried, run

    def entry_back(first, steps, carried):
        def run(heads, weight, rows, pieces, outer, *kept_back):
            return over_latents(
                entry_back_kernel,
                steps,
                [
                    (row_block, heads),
                    (whole, weight),
                    (row_block, rows),
                    (per_latent, pieces),
                    (row_block, outer),
                ],
                [(row_block, (tokens, D), F32), (per_latent, (latents, 2, D), F32)],
                unit * steps,
                first,
                kept_back,
            )

        return (qkv_grad, qkv_full, latents_in, modulation, middle_grad) + carried, run

    if direct:
        down_out = Flow(reduce_stages(*square_grad(mlp_grad, activated)))
        hidden_out = Flow(
            reduce_stages(*slot([down_out], (input_two, preact_grad), square_grad))
        )
        qkv_sums, carried = 0.0, ()
        for latent in range(latents):
            flows = [flow for flow in (down_out, hidden_out) if flow.value is None]
            qkv_grad, own_sums = slot(flows, *attend_back(latent, 1, carried))
            carried, qkv_sums = (qkv_grad,), qkv_sums + own_sums
        flows = [flow for flow in (down_out, hidden_out) if flow.value is None]
        heads_out = Flow(
            reduce_stages(*slot(flows, (input_one, qkv_grad, attended_grad, mixed), heads_grad))
        )
        input_grad, early_pieces = slot([heads_out], *entry_back(0, latents, ()))
        while heads_out.value is None:
            slot([heads_out], (), lambda: ())
        while hidden_out.value is None:
            slot([hidden_out], (), lambda: ())
        down_weight_grad, hidden_weight_grad = down_out.value.T, hidden_out.value
        packed_grad = heads_out.value.reshape(slab, 4, head_width)
        qkv_weight_grad = packed_grad[:, :3].swapaxes(0, 1)
        proj_weight_grad = packed_grad[:, 3].T
    else:
        inputs, run = attend_back(0, latents, ())
        qkv_grad, qkv_sums = run(*inputs)
        down_weight_grad = scattered(weight_grad(mlp_grad, activated)).T
        hidden_weight_grad = scattered(weight_grad(input_two, preact_grad))
        proj_weight_grad = scattered(weight_grad(attended_grad, mixed)).T
        qkv_weight_grad = scattered(
            weight_grad(input_one, qkv_grad.reshape(-1, tokens, head_width))
        ).reshape(qkv_weight.shape)
        inputs, run = entry_back(0, latents, ())
        input_grad, early_pieces = run(*inputs)
    modulation_grad = jnp.concatenate([early_pieces, late_pieces], axis=1).astype(BF16)
    vectors = jnp.concatenate(
        [
            modulation_grad.reshape(-1),
            qkv_sums[:, ::2].astype(BF16).reshape(-1),
            late_sums.astype(BF16).reshape(-1),
        ]
    )
    shared = exchange(jnp.broadcast_to(vectors[None], (count, vectors.shape[0])), axes)
    split = latents * 6 * D
    modulation_all = shared[:, :split].reshape(count * latents, 6 * D)
    ones = jnp.ones((1, count), BF16)
    totals = contract(ones, shared[:, split:], 1, 0)[0]
    qv_bias_grad = lax.dynamic_index_in_dim(
        totals[: 2 * D].reshape(tensor_size, 2, head_width), place, 0, keepdims=False
    )
    rest = totals[2 * D :].reshape(tensor_size + 2, D)
    hidden_bias_grad = lax.dynamic_index_in_dim(rest, place, 0, keepdims=False)
    proj_bias_grad, down_bias_grad = rest[tensor_size], rest[tensor_size + 1]
    ada_weight_grad = contract(silu_columns, modulation_all, 0, 0)
    ada_bias_grad = lax.dynamic_index_in_dim(
        contract(jnp.ones((1, count * latents), BF16), modulation_all, 1, 0).reshape(count, ada_cols), here, 0, keepdims=False
    )
    silu_grad = exchange(
        contract(modulation_all, ada_weight, 1, 1).reshape(count, latents, ada_rows), axes
    )
    condition_grad = silu_pullback(silu_grad.transpose(1, 0, 2).reshape(latents, D))[0]
    return (
        block_out,
        input_grad,
        condition_grad,
        ada_weight_grad,
        ada_bias_grad,
        qkv_weight_grad,
        qv_bias_grad,
        proj_weight_grad,
        proj_bias_grad,
        hidden_weight_grad,
        hidden_bias_grad,
        down_weight_grad,
        down_bias_grad,
    )


def solution(mesh):
    both = ("dp", "tensor")
    placed = (
        P(both, None),
        P(both, None),
        P(both, None),
        P(both),
        P(None, "dp", "tensor"),
        P(None, "tensor"),
        P("tensor", "dp"),
        P(),
        P("dp", "tensor"),
        P("tensor"),
        P("tensor", "dp"),
        P(),
        P(both, None),
    )
    return jax.shard_map(
        functools.partial(
            on_device, dp_size=mesh.shape["dp"], tensor_size=mesh.shape["tensor"]
        ),
        mesh=mesh,
        in_specs=placed,
        out_specs=(P(both, None), P(both, None)) + placed[1:-1],
        check_vma=False,
    )
```

time: 696 us -> 417 us (0.60)
  local copies, waits for them, and re-layouts: 253 us -> 46 us
  Pallas kernels: 0 us -> 134 us
  matrix products: 108 us -> 2.75 us
  waiting for transfers between devices: 196 us -> 97.8 us
  starting transfers between devices: 21.2 us -> 76.1 us
  other arithmetic: 68 us -> 38.9 us
  between operations: 15.7 us -> 2.13 us
  blocking collectives: 25.9 us -> 13 us
    pallas_call x0 -> x12, Pallas kernels: none -> 134 us  [the longest x6 85.6 us: over_latents(): pl.pallas_call(body, grid=(steps,), in_specs=[spec(array, first) for spec...]
    dot_general x20 -> x5, matrix products: 102 us -> 2.75 us  [the longest x4 2.47 us: contract(): lax.dot_general(left, right, (((left_axis,), (right_axis,)), ((), ())), p...]
    all_gather x4 -> x0, waiting for transfers between devices: 94.6 us -> none  [gathered(): whole = lax.all_gather(shard, axes, axis=0)]
    ppermute x0 -> x54, waiting for transfers between devices: none -> 86 us  [swap(): lax.ppermute(array, axes, [(device, device ^ mask) for device in range(co...]
    reshape x24 -> x16, local copies, waits for them, and re-layouts: 82.6 us -> 4.9 us  [the longest x2 1.27 us: on_device(): modulation_all = shared[:, :split].reshape(count * latents, 6 * D)]
    reduce_scatter x7 -> x0, waiting for transfers between devices: 70 us -> none  [the longest x3 51.5 us: scattered(): lax.psum_scatter(flat, 'tensor', scatter_dimension=0, tiled=True)]
    ppermute x0 -> x54, starting transfers between devices: none -> 61.3 us  [swap(): lax.ppermute(array, axes, [(device, device ^ mask) for device in range(co...]
    convert_element_type x11 -> x10, local copies, waits for them, and re-layouts: 36 us -> 0.4 us  [the longest x3 0.23 us: reduce_stages(): block.astype(BF16)]
  transfers between devices with their start and end apart: 16 -> 57, of which waited for: 8 -> 20; matrix products, arithmetic and copies ran while one was open for 47% -> 5% of each run, Pallas kernels for 0% -> 20%
where the time goes in v2:
time: 417 us; the launch traced here: 411 us
  Pallas kernels  134 us (32%)
  waiting for transfers between devices  97.8 us (23%)
  starting transfers between devices  76.1 us (18%)
  local copies, waits for them, and re-layouts  46 us (11%)
  other arithmetic  38.9 us (9%)
  blocking collectives  13 us (3%)
    ppermute x54, waiting for transfers between devices, swap(): lax.ppermute(array, axes, [(device, device ^ mask) for device in range(co...  86 us
    pallas_call x6, Pallas kernels, over_latents(): pl.pallas_call(body, grid=(steps,), in_specs=[spec(array, first) for spec...  85.6 us
    ppermute x54, starting transfers between devices, swap(): lax.ppermute(array, axes, [(device, device ^ mask) for device in range(co...  61.3 us
    pallas_call x6, Pallas kernels, placed_call(): pl.pallas_call(kernel, grid_spec=pltpu.PrefetchScalarGridSpec(num_scalar_...  48.2 us
    unnamed x105, local copies, waits for them, and re-layouts  22.3 us
    all_to_all x3, starting transfers between devices, exchange(): return lax.all_to_all(slots, axes, 0, 0, tiled=True)  14.8 us
    all_to_all x1, blocking collectives, exchange(): return lax.all_to_all(slots, axes, 0, 0, tiled=True)  13 us
    all_to_all x3, waiting for transfers between devices, exchange(): return lax.all_to_all(slots, axes, 0, 0, tiled=True)  11.8 us
  transfers between devices with their start and end apart: 57, of which 20 were waited for; matrix products, arithmetic and copies ran while one was open for 5% of the time, Pallas kernels for 20%

profile of v2, /device:TPU:0, one launch (start us, length us, event | category | flops | bytes accessed | tf_op | source)
XLA Modules:
  0.0 410.5 jit_solution(11918950871592042258)
XLA Ops:
  9.6 7.3 %all-to-all-start = ((bf16[32,2,3492]{2,1,0:T(2,128)(2,1)}), bf16[32,2,3492]{2,1,0:T(2,128)(2,1)S(1)}, u32[]{:S(2)}, u32[]{:S(2)}) async-start(bf16[32,2,3492]{2,1,0:T(2,128)(2,1)} %reshape.209), calls=%async_computation | async-start | bytes 917504 | tf_op jit(solution)/shard_map/all_to_all | solution.py:373
  16.9 1.8 collective-permute-start
  18.7 2.4 collective-permute-start.1
  21.4 8.6 %all-to-all-done = bf16[32,2,3492]{2,1,0:T(2,128)(2,1)S(1)} async-done(((bf16[32,2,3492]{2,1,0:T(2,128)(2,1)}), bf16[32,2,3492]{2,1,0:T(2,128)(2,1)S(1)}, u32[]{:S(2)}, u32[]{:S(2)}) %all-to-all-start) | async-done | bytes 447008 | tf_op jit(solution)/shard_map/all_to_all | solution.py:373
  30.7 9.7 %collective-permute-done.1 = bf16[96,768]{1,0:T(8,128)(2,1)S(1)} collective-permute-done((bf16[96,768]{1,0:T(8,128)(2,1)S(1)}, bf16[96,768]{1,0:T(8,128)(2,1)S(1)}, u32[]{:S(2)}, u32[]{:S(2)}) %collective-permute-start.1) | collective-permute-done | bytes 147488 | tf_op jit(solution)/shard_map/ppermute | solution.py:418
  45.2 3.3 collective-permute-start.5
  48.6 2.4 collective-permute-start.7
  51.7 13.0 %all_to_all.31 = f32[32,1,432]{2,1,0:T(1,128)S(1)} all-to-all(f32[32,1,432]{2,1,0:T(1,128)S(1)} %reshape.211), channel_id=1, replica_groups=mesh['dp'=8,'tensor'=4] {'dp','tensor'}, dimensions={0} | all-to-all | bytes 110592 | tf_op jit(solution)/shard_map/all_to_all | solution.py:373
  72.5 1.8 collective-permute-start.13
  74.9 4.6 %collective-permute-done.12 = bf16[96,768]{1,0:T(8,128)(2,1)S(1)} collective-permute-done((bf16[96,768]{1,0:T(8,128)(2,1)S(1)}, bf16[96,768]{1,0:T(8,128)(2,1)S(1)}, u32[]{:S(2)}, u32[]{:S(2)}) %collective-permute-start.12) | collective-permute-done | bytes 147488 | tf_op jit(solution)/shard_map/ppermute | solution.py:418
  82.8 5.4 %collective-permute-done.14 = bf16[96,768]{1,0:T(8,128)(2,1)S(1)} collective-permute-done((bf16[96,768]{1,0:T(8,128)(2,1)S(1)}, bf16[96,768]{1,0:T(8,128)(2,1)S(1)}, u32[]{:S(2)}, u32[]{:S(2)}) %collective-permute-start.14) | collective-permute-done | bytes 147488 | tf_op jit(solution)/shard_map/ppermute | solution.py:418
  88.2 3.5 collective-permute-done.8
  102.5 16.6 %collective-permute-done.16 = bf16[2,96,768]{2,1,0:T(8,128)(2,1)} collective-permute-done((bf16[2,96,768]{2,1,0:T(8,128)(2,1)}, bf16[2,96,768]{2,1,0:T(8,128)(2,1)}, u32[]{:S(2)}, u32[]{:S(2)}) %collective-permute-start.16) | collective-permute-done | bytes 294944 | tf_op jit(solution)/shard_map/ppermute | solution.py:418
  119.1 1.7 slice.305
  123.7 6.8 %shard_map.228 = (bf16[4,3,8,96,192]{4,3,2,1,0:T(8,128)(2,1)}, bf16[4,8,96,192]{3,2,1,0:T(8,128)(2,1)}) custom-call(s32[2]{0:T(128)} %pad_add_fusion.place, bf16[4,4,96,768]{3,2,1,0:T(8,128)(2,1)} %copy-done.1, bf16[4,4,96,768]{3,2,1,0:T(8,128)(2,1)} %collective-permute-done.15.other), custom_call_target="tpu_custom_call" | custom-call | bytes 9437184 | tf_op jit(solution)/shard_map/pallas_call | solution.py:310
  134.3 17.5 %shard_map.229 = (bf16[768,768]{1,0:T(8,128)(2,1)}, bf16[4,3,768,192]{3,2,1,0:T(8,128)(2,1)}, bf16[4,768,192]{2,1,0:T(8,128)(2,1)}) custom-call(bf16[768,768]{1,0:T(8,128)(2,1)} %refs_2_.2, f32[3,6,768]{2,1,0:T(8,128)} %reshape.191.refs_1_.refs_3_, bf16[1,4,3,768,192]{4,3,2,1,0:T(8,128)(2,1)} %bitcast.244, bf16[4,2,192]{2,1,0:T(2,128)(2,1)} %reshape.193.refs_3_), custom_call_target="tpu_custom_call" | custom-call | flops 4529848320 | bytes 10675200 | tf_op jit(solution)/shard_map/pallas_call | solution.py:234
  151.9 2.3 pad_maximum_fusion.2.own
  157.0 5.7 %shard_map.230 = bf16[4,8,96,768]{3,2,1,0:T(8,128)(2,1)} custom-call(s32[2]{0:T(128)} %pad_add_fusion.place, bf16[4,4,96,768]{3,2,1,0:T(8,128)(2,1)} %copy-done.2, bf16[4,4,96,768]{3,2,1,0:T(8,128)(2,1)} %copy-done.6), custom_call_target="tpu_custom_call" | custom-call | bytes 9437184 | tf_op jit(solution)/shard_map/pallas_call | solution.py:310
  164.2 5.8 %shard_map.231 = bf16[4,8,96,768]{3,2,1,0:T(8,128)(2,1)} custom-call(s32[2]{0:T(128)} %pad_add_fusion.place, bf16[4,4,96,768]{3,2,1,0:T(8,128)(2,1)} %copy-done.3, bf16[4,4,96,768]{3,2,1,0:T(8,128)(2,1)} %copy-done.7), custom_call_target="tpu_custom_call" | custom-call | bytes 9437184 | tf_op jit(solution)/shard_map/pallas_call | solution.py:310
  169.9 29.4 %shard_map.232 = (f32[768,768]{1,0:T(8,128)}, bf16[4,768,768]{2,1,0:T(8,128)(2,1)}, bf16[4,768,768]{2,1,0:T(8,128)(2,1)}, bf16[768,768]{1,0:T(8,128)(2,1)}, bf16...) custom-call(bf16[4,768,192]{2,1,0:T(8,128)(2,1)} %get-tuple-element., ...), custom_call_target="tpu_custom_call" | custom-call | flops 16307453952 | bytes 31970304 | tf_op jit(solution)/shard_map/pallas_call | solution.py:234
  199.4 9.0 %shard_map.233 = (f32[4,4,96,768]{3,2,1,0:T(8,128)}, bf16[4,4,96,768]{3,2,1,0:T(8,128)(2,1)}) custom-call(s32[2]{0:T(128)} %pad_add_fusion.place, bf16[768,768]{1,0:T(8,128)(2,1)} %get-tuple-element.265.left, bf16[4,768,768]{2,1,0:T(8,128)(2,1)} %get-tuple-element.266.right), custom_call_target="tpu_custom_call" | custom-call | flops 3623878656 | bytes 12976128 | tf_op jit(solution)/shard_map/pallas_call | solution.py:310
  208.8 9.7 %shard_map.234 = (f32[4,4,96,768]{3,2,1,0:T(8,128)}, bf16[4,4,96,768]{3,2,1,0:T(8,128)(2,1)}) custom-call(s32[2]{0:T(128)} %pad_add_fusion.place, bf16[768,768]{1,0:T(8,128)(2,1)} %get-tuple-element.271.left, bf16[4,768,768]{2,1,0:T(8,128)(2,1)} %get-tuple-element.272.right), custom_call_target="tpu_custom_call" | custom-call | flops 3623878656 | bytes 12976128 | tf_op jit(solution)/shard_map/pallas_call | solution.py:310
  218.5 2.9 fusion.62
  227.5 9.6 %shard_map.235 = (bf16[4,3,768,192]{3,2,1,0:T(8,128)(2,1)}, f32[4,3,192]{2,1,0:T(4,128)}) custom-call(bf16[768,768]{1,0:T(8,128)(2,1)} %get-tuple-element.336.refs_0_.outer, bf16[4,3,768,192]{3,2,1,0:T(8,128)(2,1)} %get-tuple-element.321.refs_1_, bf16[1,4,768,192]{3,2,1,0:T(8,128)(2,1)} %bitcast.286), custom_call_target="tpu_custom_call" | custom-call | flops 3623878656 | bytes 9446400 | tf_op jit(solution)/shard_map/pallas_call | solution.py:234
  239.1 3.0 fusion.61
  242.2 2.1 fusion.25
  249.9 4.4 %collective-permute-done.30 = bf16[2,96,768]{2,1,0:T(8,128)(2,1)S(1)} collective-permute-done((bf16[2,96,768]{2,1,0:T(8,128)(2,1)S(1)}, bf16[2,96,768]{2,1,0:T(8,128)(2,1)S(1)}, u32[]{:S(2)}, u32[]{:S(2)}) %collective-permute-start.30) | collective-permute-done | bytes 294944 | tf_op jit(solution)/shard_map/ppermute | solution.py:418
  254.9 9.8 %shard_map.236 = (bf16[4,3,768,192]{3,2,1,0:T(8,128)(2,1)}, f32[4,3,192]{2,1,0:T(4,128)}) custom-call(bf16[768,768]{1,0:T(8,128)(2,1)} %get-tuple-element.336.refs_0_.outer, bf16[4,3,768,192]{3,2,1,0:T(8,128)(2,1)} %get-tuple-element.321.refs_1_, bf16[1,4,768,192]{3,2,1,0:T(8,128)(2,1)} %bitcast.287, ...), custom_call_target="tpu_custom_call", output_to_operand_aliasing={{0}: (3, {})} | custom-call | flops 3623878656 | bytes 9446400 | tf_op jit(solution)/shard_map/pallas_call | solution.py:234
  270.0 2.2 collective-permute-start.38
  275.2 9.7 %shard_map.237 = (bf16[4,3,768,192]{3,2,1,0:T(8,128)(2,1)}, f32[4,3,192]{2,1,0:T(4,128)}) custom-call(bf16[768,768]{1,0:T(8,128)(2,1)} %get-tuple-element.336.refs_0_.outer, bf16[4,3,768,192]{3,2,1,0:T(8,128)(2,1)} %get-tuple-element.321.refs_1_, bf16[1,4,768,192]{3,2,1,0:T(8,128)(2,1)} %bitcast.288, ...), custom_call_target="tpu_custom_call", output_to_operand_aliasing={{0}: (3, {})} | custom-call | flops 3623878656 | bytes 9446400 | tf_op jit(solution)/shard_map/pallas_call | solution.py:234
  285.9 1.9 collective-permute-start.42
  287.8 2.5 collective-permute-start.43
  290.2 11.2 %shard_map.238 = (f32[4,4,96,768]{3,2,1,0:T(8,128)}, bf16[4,4,96,768]{3,2,1,0:T(8,128)(2,1)}) custom-call(s32[2]{0:T(128)} %pad_add_fusion.place, bf16[768,768]{1,0:T(8,128)(2,1)} %get-tuple-element.334.entry, bf16[4,3,768,192]{3,2,1,0:T(8,128)(2,1)} %get-tuple-element.343.qkv_grad.refs_0_, bf16[768,768]{1,0:T(8,128)(2,1)} %get-tuple-element.336.refs_0_.outer, ...), custom_call_target="tpu_custom_call" | custom-call | flops 3623878656 | bytes 14155776 | tf_op jit(solution)/shard_map/pallas_call | solution.py:310
  302.4 9.7 %shard_map.239 = (f32[768,768]{1,0:T(8,128)}, f32[3,2,768]{2,1,0:T(2,128)}) custom-call(bf16[4,3,768,192]{3,2,1,0:T(8,128)(2,1)} %get-tuple-element.343.qkv_grad.refs_0_, bf16[1,4,3,768,192]{4,3,2,1,0:T(8,128)(2,1)} %bitcast.245, bf16[768,768]{1,0:T(8,128)(2,1)} %refs_2_.2, f32[3,6,768]{2,1,0:T(8,128)} %reshape.191.refs_1_.refs_3_, ...), custom_call_target="tpu_custom_call" | custom-call | flops 2717908992 | bytes 13049856 | tf_op jit(solution)/shard_map/pallas_call | solution.py:234
  314.9 9.5 %reduce.4 = bf16[32,19968]{1,0:T(8,128)(2,1)} reduce(bf16[32,1,19968]{2,1,0:T(2,128)(2,1)S(1)} %broadcast_in_dim.26, bf16[]{:T(256)} %broadcast.21), dimensions={1}, to_apply=%broadcast_in_dim.26.reduce_sub_computation | reduce | bytes 2555906 | tf_op jit(solution)/shard_map/broadcast_in_dim | solution.py:709
  324.3 2.4 reshape.213
  326.8 3.6 all-to-all-start.2
  330.4 3.1 fusion.60
  333.7 1.8 collective-permute-start.45
  337.8 12.4 %collective-permute-done.45 = bf16[2,96,768]{2,1,0:T(8,128)(2,1)S(1)} collective-permute-done((bf16[2,96,768]{2,1,0:T(8,128)(2,1)S(1)}, bf16[2,96,768]{2,1,0:T(8,128)(2,1)S(1)}, u32[]{:S(2)}, u32[]{:S(2)}) %collective-permute-start.45) | collective-permute-done | bytes 294944 | tf_op jit(solution)/shard_map/ppermute | solution.py:418
  350.3 8.2 %collective-permute-done.47 = bf16[2,96,768]{2,1,0:T(8,128)(2,1)S(1)} collective-permute-done((bf16[2,96,768]{2,1,0:T(8,128)(2,1)S(1)}, bf16[2,96,768]{2,1,0:T(8,128)(2,1)S(1)}, u32[]{:S(2)}, u32[]{:S(2)}) %collective-permute-start.47) | collective-permute-done | bytes 294944 | tf_op jit(solution)/shard_map/ppermute | solution.py:418
  362.4 5.5 %collective-permute-done.49 = bf16[2,96,768]{2,1,0:T(8,128)(2,1)S(1)} collective-permute-done((bf16[2,96,768]{2,1,0:T(8,128)(2,1)S(1)}, bf16[2,96,768]{2,1,0:T(8,128)(2,1)S(1)}, u32[]{:S(2)}, u32[]{:S(2)}) %collective-permute-start.49) | collective-permute-done | bytes 294944 | tf_op jit(solution)/shard_map/ppermute | solution.py:418
  370.6 2.0 collective-permute-start.51
  372.6 1.9 collective-permute-start.52
  376.9 8.7 %collective-permute-done.52 = bf16[96,768]{1,0:T(8,128)(2,1)S(1)} collective-permute-done((bf16[96,768]{1,0:T(8,128)(2,1)S(1)}, bf16[96,768]{1,0:T(8,128)(2,1)S(1)}, u32[]{:S(2)}, u32[]{:S(2)}) %collective-permute-start.52) | collective-permute-done | bytes 147488 | tf_op jit(solution)/shard_map/ppermute | solution.py:418
  387.6 7.6 %reshape.214 = bf16[32,1,19968]{2,1,0:T(2,128)(2,1)S(1)} reshape(bf16[32,2,9984]{2,1,0:T(2,128)(2,1)} %all-to-all-done.2) | data formatting | bytes 2555904
  398.1 3.9 all-to-all-start.3
  406.3 3.2 all-to-all-done.3
  (291 shorter events, 97.1 us)
Async XLA Ops:
  9.6 20.5 %all-to-all-start = ((bf16[32,2,3492]{2,1,0:T(2,128)(2,1)}), bf16[32,2,3492]{2,1,0:T(2,128)(2,1)S(1)}, u32[]{:S(2)}, u32[]{:S(2)}) async-start(bf16[32,2,3492]{2,1,0:T(2,128)(2,1)} %reshape.209), calls=%async_computation | async-start | bytes 917504 | tf_op jit(solution)/shard_map/all_to_all | solution.py:373
  16.9 13.9 %collective-permute-start = (bf16[96,768]{1,0:T(8,128)(2,1)S(1)}, bf16[96,768]{1,0:T(8,128)(2,1)S(1)}, u32[]{:S(2)}, u32[]{:S(2)}) collective-permute-start(bf16[96,768]{1,0:T(8,128)(2,1)S(1)} %pad_maximum_fusion.6), channel_id=1, source_target_pairs={{0,1},{1,0},{2,3},{3,2},{4,5},{5,4},{6,7},{7,6},{8,9},{9,8},{10,11... | collective-permute-start | bytes 442376 | tf_op jit(solution)/shard_map/ppermute | solution.py:418
  18.7 21.7 %collective-permute-start.1 = (bf16[96,768]{1,0:T(8,128)(2,1)S(1)}, bf16[96,768]{1,0:T(8,128)(2,1)S(1)}, u32[]{:S(2)}, u32[]{:S(2)}) collective-permute-start(bf16[96,768]{1,0:T(8,128)(2,1)S(1)} %pad_maximum_fusion.6), channel_id=1, source_target_pairs={{0,2},{1,3},{2,0},{3,1},{4,6},{5,7},{6,4},{7,5},{8,10},{9,11},{10,... | collective-permute-start | bytes 442376 | tf_op jit(solution)/shard_map/ppermute | solution.py:418
  21.1 19.3 %collective-permute-start.2 = (bf16[96,768]{1,0:T(8,128)(2,1)S(1)}, bf16[96,768]{1,0:T(8,128)(2,1)S(1)}, u32[]{:S(2)}, u32[]{:S(2)}) collective-permute-start(bf16[96,768]{1,0:T(8,128)(2,1)S(1)} %pad_maximum_fusion.6), channel_id=1, source_target_pairs={{0,3},{1,2},{2,1},{3,0},{4,7},{5,6},{6,5},{7,4},{8,11},{9,10},{10,... | collective-permute-start | bytes 442376 | tf_op jit(solution)/shard_map/ppermute | solution.py:418
  42.2 24.7 %collective-permute-start.3 = (bf16[4,96,768]{2,1,0:T(8,128)(2,1)S(1)}, bf16[4,96,768]{2,1,0:T(8,128)(2,1)S(1)}, u32[]{:S(2)}, u32[]{:S(2)}) collective-permute-start(bf16[4,96,768]{2,1,0:T(8,128)(2,1)S(1)} %get-tuple-element.207), channel_id=1, source_target_pairs={{0,8},{1,9},{2,10},{3,11},{4,12},{5,13},{6,14},{7,15},{8,0},{9,1},... | collective-permute-start | bytes 1769480 | tf_op jit(solution)/shard_map/ppermute | solution.py:418
  43.7 23.2 %collective-permute-start.4 = (bf16[4,96,768]{2,1,0:T(8,128)(2,1)S(1)}, bf16[4,96,768]{2,1,0:T(8,128)(2,1)S(1)}, u32[]{:S(2)}, u32[]{:S(2)}) collective-permute-start(bf16[4,96,768]{2,1,0:T(8,128)(2,1)S(1)} %get-tuple-element.207), channel_id=1, source_target_pairs={{0,16},{1,17},{2,18},{3,19},{4,20},{5,21},{6,22},{7,23},{8,24},{9,... | collective-permute-start | bytes 1769480 | tf_op jit(solution)/shard_map/ppermute | solution.py:418
  45.2 21.7 %collective-permute-start.5 = (bf16[96,768]{1,0:T(8,128)(2,1)S(1)}, bf16[96,768]{1,0:T(8,128)(2,1)S(1)}, u32[]{:S(2)}, u32[]{:S(2)}) collective-permute-start(bf16[96,768]{1,0:T(8,128)(2,1)S(1)} %copy-done.20), channel_id=1, source_target_pairs={{0,1},{1,0},{2,3},{3,2},{4,5},{5,4},{6,7},{7,6},{8,9},{9,8},{10,11... | collective-permute-start | bytes 442376 | tf_op jit(solution)/shard_map/ppermute | solution.py:418
  48.6 18.4 %collective-permute-start.6 = (bf16[96,768]{1,0:T(8,128)(2,1)S(1)}, bf16[96,768]{1,0:T(8,128)(2,1)S(1)}, u32[]{:S(2)}, u32[]{:S(2)}) collective-permute-start(bf16[96,768]{1,0:T(8,128)(2,1)S(1)} %copy-done.20), channel_id=1, source_target_pairs={{0,2},{1,3},{2,0},{3,1},{4,6},{5,7},{6,4},{7,5},{8,10},{9,11},{10,... | collective-permute-start | bytes 442376 | tf_op jit(solution)/shard_map/ppermute | solution.py:418
  48.6 18.3 %collective-permute-start.7 = (bf16[96,768]{1,0:T(8,128)(2,1)S(1)}, bf16[96,768]{1,0:T(8,128)(2,1)}, u32[]{:S(2)}, u32[]{:S(2)}) collective-permute-start(bf16[96,768]{1,0:T(8,128)(2,1)S(1)} %copy-done.20), channel_id=1, source_target_pairs={{0,3},{1,2},{2,1},{3,0},{4,7},{5,6},{6,5},{7,4},{8,11},{9,10},{10,... | collective-permute-start | bytes 442376 | tf_op jit(solution)/shard_map/ppermute | solution.py:418
  68.9 22.9 %collective-permute-start.10 = (bf16[4,96,768]{2,1,0:T(8,128)(2,1)S(1)}, bf16[4,96,768]{2,1,0:T(8,128)(2,1)S(1)}, u32[]{:S(2)}, u32[]{:S(2)}) collective-permute-start(bf16[4,96,768]{2,1,0:T(8,128)(2,1)S(1)} %get-tuple-element.221), channel_id=1, source_target_pairs={{0,8},{1,9},{2,10},{3,11},{4,12},{5,13},{6,14},{7,15},{8,0},{9,1},... | collective-permute-start | bytes 1769480 | tf_op jit(solution)/shard_map/ppermute | solution.py:418
  70.3 21.4 %collective-permute-start.11 = (bf16[4,96,768]{2,1,0:T(8,128)(2,1)S(1)}, bf16[4,96,768]{2,1,0:T(8,128)(2,1)S(1)}, u32[]{:S(2)}, u32[]{:S(2)}) collective-permute-start(bf16[4,96,768]{2,1,0:T(8,128)(2,1)S(1)} %get-tuple-element.221), channel_id=1, source_target_pairs={{0,16},{1,17},{2,18},{3,19},{4,20},{5,21},{6,22},{7,23},{8,24},{9,... | collective-permute-start | bytes 1769480 | tf_op jit(solution)/shard_map/ppermute | solution.py:418
  74.3 17.4 %collective-permute-start.8 = (bf16[2,96,768]{2,1,0:T(8,128)(2,1)S(1)}, bf16[2,96,768]{2,1,0:T(8,128)(2,1)S(1)}, u32[]{:S(2)}, u32[]{:S(2)}) collective-permute-start(bf16[2,96,768]{2,1,0:T(8,128)(2,1)S(1)} %slice.301), channel_id=1, source_target_pairs={{0,16},{1,17},{2,18},{3,19},{4,20},{5,21},{6,22},{7,23},{8,24},{9,... | collective-permute-start | bytes 884744 | tf_op jit(solution)/shard_map/ppermute | solution.py:418
  79.5 12.2 %collective-permute-start.9 = (bf16[2,96,768]{2,1,0:T(8,128)(2,1)S(1)}, bf16[2,96,768]{2,1,0:T(8,128)(2,1)S(1)}, u32[]{:S(2)}, u32[]{:S(2)}) collective-permute-start(bf16[2,96,768]{2,1,0:T(8,128)(2,1)S(1)} %slice.302), channel_id=1, source_target_pairs={{0,8},{1,9},{2,10},{3,11},{4,12},{5,13},{6,14},{7,15},{8,0},{9,1},... | collective-permute-start | bytes 884744 | tf_op jit(solution)/shard_map/ppermute | solution.py:418
  96.4 22.7 %collective-permute-start.15 = (bf16[4,4,96,768]{3,2,1,0:T(8,128)(2,1)S(1)}, bf16[4,4,96,768]{3,2,1,0:T(8,128)(2,1)}, u32[]{:S(2)}, u32[]{:S(2)}) collective-permute-start(bf16[4,4,96,768]{3,2,1,0:T(8,128)(2,1)S(1)} %pad_maximum_fusion.own), channel_id=1, source_target_pairs={{0,4},{1,5},{2,6},{3,7},{4,0},{5,1},{6,2},{7,3},{8,12},{9,13},{10,... | collective-permute-start | bytes 7077896 | tf_op jit(solution)/shard_map/ppermute | solution.py:418
  96.4 22.7 %collective-permute-start.18 = (bf16[4,96,768]{2,1,0:T(8,128)(2,1)}, bf16[4,96,768]{2,1,0:T(8,128)(2,1)}, u32[]{:S(2)}, u32[]{:S(2)}) collective-permute-start(bf16[4,96,768]{2,1,0:T(8,128)(2,1)} %get-tuple-element.236), channel_id=1, source_target_pairs={{0,8},{1,9},{2,10},{3,11},{4,12},{5,13},{6,14},{7,15},{8,0},{9,1},... | collective-permute-start | bytes 1769480 | tf_op jit(solution)/shard_map/ppermute | solution.py:418
  97.0 22.1 %collective-permute-start.19 = (bf16[4,96,768]{2,1,0:T(8,128)(2,1)}, bf16[4,96,768]{2,1,0:T(8,128)(2,1)}, u32[]{:S(2)}, u32[]{:S(2)}) collective-permute-start(bf16[4,96,768]{2,1,0:T(8,128)(2,1)} %get-tuple-element.236), channel_id=1, source_target_pairs={{0,16},{1,17},{2,18},{3,19},{4,20},{5,21},{6,22},{7,23},{8,24},{9,... | collective-permute-start | bytes 1769480 | tf_op jit(solution)/shard_map/ppermute | solution.py:418
  98.4 20.7 %collective-permute-start.16 = (bf16[2,96,768]{2,1,0:T(8,128)(2,1)}, bf16[2,96,768]{2,1,0:T(8,128)(2,1)}, u32[]{:S(2)}, u32[]{:S(2)}) collective-permute-start(bf16[2,96,768]{2,1,0:T(8,128)(2,1)} %slice.303), channel_id=1, source_target_pairs={{0,16},{1,17},{2,18},{3,19},{4,20},{5,21},{6,22},{7,23},{8,24},{9,... | collective-permute-start | bytes 884744 | tf_op jit(solution)/shard_map/ppermute | solution.py:418
  99.0 20.1 %collective-permute-start.17 = (bf16[2,96,768]{2,1,0:T(8,128)(2,1)}, bf16[2,96,768]{2,1,0:T(8,128)(2,1)}, u32[]{:S(2)}, u32[]{:S(2)}) collective-permute-start(bf16[2,96,768]{2,1,0:T(8,128)(2,1)} %slice.304), channel_id=1, source_target_pairs={{0,8},{1,9},{2,10},{3,11},{4,12},{5,13},{6,14},{7,15},{8,0},{9,1},... | collective-permute-start | bytes 884744 | tf_op jit(solution)/shard_map/ppermute | solution.py:418
  130.8 21.0 %collective-permute-start.20 = (bf16[4,4,96,768]{3,2,1,0:T(8,128)(2,1)S(1)}, bf16[4,4,96,768]{3,2,1,0:T(8,128)(2,1)S(1)}, u32[]{:S(2)}, u32[]{:S(2)}) collective-permute-start(bf16[4,4,96,768]{3,2,1,0:T(8,128)(2,1)S(1)} %pad_maximum_fusion.1.own), channel_id=1, source_target_pairs={{0,4},{1,5},{2,6},{3,7},{4,0},{5,1},{6,2},{7,3},{8,12},{9,13},{10,... | collective-permute-start | bytes 7077896 | tf_op jit(solution)/shard_map/ppermute | solution.py:418
  131.4 20.4 %collective-permute-start.21 = (bf16[2,96,768]{2,1,0:T(8,128)(2,1)S(1)}, bf16[2,96,768]{2,1,0:T(8,128)(2,1)S(1)}, u32[]{:S(2)}, u32[]{:S(2)}) collective-permute-start(bf16[2,96,768]{2,1,0:T(8,128)(2,1)S(1)} %copy-done.18), channel_id=1, source_target_pairs={{0,16},{1,17},{2,18},{3,19},{4,20},{5,21},{6,22},{7,23},{8,24},{9,... | collective-permute-start | bytes 884744 | tf_op jit(solution)/shard_map/ppermute | solution.py:418
  132.8 19.0 %collective-permute-start.22 = (bf16[2,96,768]{2,1,0:T(8,128)(2,1)S(1)}, bf16[2,96,768]{2,1,0:T(8,128)(2,1)S(1)}, u32[]{:S(2)}, u32[]{:S(2)}) collective-permute-start(bf16[2,96,768]{2,1,0:T(8,128)(2,1)S(1)} %copy-done.17), channel_id=1, source_target_pairs={{0,8},{1,9},{2,10},{3,11},{4,12},{5,13},{6,14},{7,15},{8,0},{9,1},... | collective-permute-start | bytes 884744 | tf_op jit(solution)/shard_map/ppermute | solution.py:418
  208.4 10.1 %collective-permute-start.24 = (bf16[4,4,96,768]{3,2,1,0:T(8,128)(2,1)}, bf16[4,4,96,768]{3,2,1,0:T(8,128)(2,1)S(1)}, u32[]{:S(2)}, u32[]{:S(2)}) collective-permute-start(bf16[4,4,96,768]{3,2,1,0:T(8,128)(2,1)} %get-tuple-element.270), channel_id=1, source_target_pairs={{0,4},{1,5},{2,6},{3,7},{4,0},{5,1},{6,2},{7,3},{8,12},{9,13},{10,... | collective-permute-start | bytes 7077896 | tf_op jit(solution)/shard_map/ppermute | solution.py:418
  223.1 16.0 %collective-permute-start.29 = (bf16[4,4,96,768]{3,2,1,0:T(8,128)(2,1)S(1)}, bf16[4,4,96,768]{3,2,1,0:T(8,128)(2,1)S(1)}, u32[]{:S(2)}, u32[]{:S(2)}) collective-permute-start(bf16[4,4,96,768]{3,2,1,0:T(8,128)(2,1)S(1)} %copy-done.43), channel_id=1, source_target_pairs={{0,4},{1,5},{2,6},{3,7},{4,0},{5,1},{6,2},{7,3},{8,12},{9,13},{10,... | collective-permute-start | bytes 7077896 | tf_op jit(solution)/shard_map/ppermute | solution.py:418
  223.5 13.7 %collective-permute-start.25 = (bf16[2,96,768]{2,1,0:T(8,128)(2,1)S(1)}, bf16[2,96,768]{2,1,0:T(8,128)(2,1)S(1)}, u32[]{:S(2)}, u32[]{:S(2)}) collective-permute-start(bf16[2,96,768]{2,1,0:T(8,128)(2,1)S(1)} %get-tuple-element.281), channel_id=1, source_target_pairs={{0,8},{1,9},{2,10},{3,11},{4,12},{5,13},{6,14},{7,15},{8,0},{9,1},... | collective-permute-start | bytes 884744 | tf_op jit(solution)/shard_map/ppermute | solution.py:418
  224.0 13.1 %collective-permute-start.26 = (bf16[2,96,768]{2,1,0:T(8,128)(2,1)S(1)}, bf16[2,96,768]{2,1,0:T(8,128)(2,1)S(1)}, u32[]{:S(2)}, u32[]{:S(2)}) collective-permute-start(bf16[2,96,768]{2,1,0:T(8,128)(2,1)S(1)} %get-tuple-element.282), channel_id=1, source_target_pairs={{0,16},{1,17},{2,18},{3,19},{4,20},{5,21},{6,22},{7,23},{8,24},{9,... | collective-permute-start | bytes 884744 | tf_op jit(solution)/shard_map/ppermute | solution.py:418
  224.6 14.2 %collective-permute-start.27 = (bf16[2,96,768]{2,1,0:T(8,128)(2,1)S(1)}, bf16[2,96,768]{2,1,0:T(8,128)(2,1)S(1)}, u32[]{:S(2)}, u32[]{:S(2)}) collective-permute-start(bf16[2,96,768]{2,1,0:T(8,128)(2,1)S(1)} %get-tuple-element.283), channel_id=1, source_target_pairs={{0,8},{1,9},{2,10},{3,11},{4,12},{5,13},{6,14},{7,15},{8,0},{9,1},... | collective-permute-start | bytes 884744 | tf_op jit(solution)/shard_map/ppermute | solution.py:418
  226.0 13.0 %collective-permute-start.28 = (bf16[2,96,768]{2,1,0:T(8,128)(2,1)S(1)}, bf16[2,96,768]{2,1,0:T(8,128)(2,1)S(1)}, u32[]{:S(2)}, u32[]{:S(2)}) collective-permute-start(bf16[2,96,768]{2,1,0:T(8,128)(2,1)S(1)} %get-tuple-element.284), channel_id=1, source_target_pairs={{0,16},{1,17},{2,18},{3,19},{4,20},{5,21},{6,22},{7,23},{8,24},{9,... | collective-permute-start | bytes 884744 | tf_op jit(solution)/shard_map/ppermute | solution.py:418
  244.9 19.7 %collective-permute-start.31 = (bf16[2,96,768]{2,1,0:T(8,128)(2,1)}, bf16[2,96,768]{2,1,0:T(8,128)(2,1)S(1)}, u32[]{:S(2)}, u32[]{:S(2)}) collective-permute-start(bf16[2,96,768]{2,1,0:T(8,128)(2,1)} %get-tuple-element.296), channel_id=1, source_target_pairs={{0,8},{1,9},{2,10},{3,11},{4,12},{5,13},{6,14},{7,15},{8,0},{9,1},... | collective-permute-start | bytes 884744 | tf_op jit(solution)/shard_map/ppermute | solution.py:418
  246.3 18.3 %collective-permute-start.32 = (bf16[2,96,768]{2,1,0:T(8,128)(2,1)S(1)}, bf16[2,96,768]{2,1,0:T(8,128)(2,1)S(1)}, u32[]{:S(2)}, u32[]{:S(2)}) collective-permute-start(bf16[2,96,768]{2,1,0:T(8,128)(2,1)S(1)} %get-tuple-element.297), channel_id=1, source_target_pairs={{0,8},{1,9},{2,10},{3,11},{4,12},{5,13},{6,14},{7,15},{8,0},{9,1},... | collective-permute-start | bytes 884744 | tf_op jit(solution)/shard_map/ppermute | solution.py:418
  247.0 17.7 %collective-permute-start.33 = (bf16[2,96,768]{2,1,0:T(8,128)(2,1)S(1)}, bf16[2,96,768]{2,1,0:T(8,128)(2,1)S(1)}, u32[]{:S(2)}, u32[]{:S(2)}) collective-permute-start(bf16[2,96,768]{2,1,0:T(8,128)(2,1)S(1)} %get-tuple-element.298), channel_id=1, source_target_pairs={{0,16},{1,17},{2,18},{3,19},{4,20},{5,21},{6,22},{7,23},{8,24},{9,... | collective-permute-start | bytes 884744 | tf_op jit(solution)/shard_map/ppermute | solution.py:418
  248.4 17.0 %collective-permute-start.34 = (bf16[2,96,768]{2,1,0:T(8,128)(2,1)S(1)}, bf16[2,96,768]{2,1,0:T(8,128)(2,1)S(1)}, u32[]{:S(2)}, u32[]{:S(2)}) collective-permute-start(bf16[2,96,768]{2,1,0:T(8,128)(2,1)S(1)} %get-tuple-element.299), channel_id=1, source_target_pairs={{0,8},{1,9},{2,10},{3,11},{4,12},{5,13},{6,14},{7,15},{8,0},{9,1},... | collective-permute-start | bytes 884744 | tf_op jit(solution)/shard_map/ppermute | solution.py:418
  254.3 11.1 %collective-permute-start.35 = (bf16[2,96,768]{2,1,0:T(8,128)(2,1)S(1)}, bf16[2,96,768]{2,1,0:T(8,128)(2,1)S(1)}, u32[]{:S(2)}, u32[]{:S(2)}) collective-permute-start(bf16[2,96,768]{2,1,0:T(8,128)(2,1)S(1)} %get-tuple-element.300), channel_id=1, source_target_pairs={{0,16},{1,17},{2,18},{3,19},{4,20},{5,21},{6,22},{7,23},{8,24},{9,... | collective-permute-start | bytes 884744 | tf_op jit(solution)/shard_map/ppermute | solution.py:418
  267.8 17.0 %collective-permute-start.36 = (bf16[96,768]{1,0:T(8,128)(2,1)S(1)}, bf16[96,768]{1,0:T(8,128)(2,1)S(1)}, u32[]{:S(2)}, u32[]{:S(2)}) collective-permute-start(bf16[96,768]{1,0:T(8,128)(2,1)S(1)} %fusion.43), channel_id=1, source_target_pairs={{0,1},{1,0},{2,3},{3,2},{4,5},{5,4},{6,7},{7,6},{8,9},{9,8},{10,11... | collective-permute-start | bytes 442376 | tf_op jit(solution)/shard_map/ppermute | solution.py:418
  268.5 16.3 %collective-permute-start.37 = (bf16[96,768]{1,0:T(8,128)(2,1)S(1)}, bf16[96,768]{1,0:T(8,128)(2,1)S(1)}, u32[]{:S(2)}, u32[]{:S(2)}) collective-permute-start(bf16[96,768]{1,0:T(8,128)(2,1)S(1)} %get-tuple-element.316), channel_id=1, source_target_pairs={{0,2},{1,3},{2,0},{3,1},{4,6},{5,7},{6,4},{7,5},{8,10},{9,11},{10,... | collective-permute-start | bytes 442376 | tf_op jit(solution)/shard_map/ppermute | solution.py:418
  270.0 14.8 %collective-permute-start.38 = (bf16[96,768]{1,0:T(8,128)(2,1)S(1)}, bf16[96,768]{1,0:T(8,128)(2,1)S(1)}, u32[]{:S(2)}, u32[]{:S(2)}) collective-permute-start(bf16[96,768]{1,0:T(8,128)(2,1)S(1)} %get-tuple-element.317), channel_id=1, source_target_pairs={{0,3},{1,2},{2,1},{3,0},{4,7},{5,6},{6,5},{7,4},{8,11},{9,10},{10,... | collective-permute-start | bytes 442376 | tf_op jit(solution)/shard_map/ppermute | solution.py:418
  272.3 12.6 %collective-permute-start.39 = (bf16[2,96,768]{2,1,0:T(8,128)(2,1)S(1)}, bf16[2,96,768]{2,1,0:T(8,128)(2,1)S(1)}, u32[]{:S(2)}, u32[]{:S(2)}) collective-permute-start(bf16[2,96,768]{2,1,0:T(8,128)(2,1)S(1)} %get-tuple-element.318), channel_id=1, source_target_pairs={{0,16},{1,17},{2,18},{3,19},{4,20},{5,21},{6,22},{7,23},{8,24},{9,... | collective-permute-start | bytes 884744 | tf_op jit(solution)/shard_map/ppermute | solution.py:418
  273.7 11.1 %collective-permute-start.40 = (bf16[2,96,768]{2,1,0:T(8,128)(2,1)S(1)}, bf16[2,96,768]{2,1,0:T(8,128)(2,1)S(1)}, u32[]{:S(2)}, u32[]{:S(2)}) collective-permute-start(bf16[2,96,768]{2,1,0:T(8,128)(2,1)S(1)} %get-tuple-element.319), channel_id=1, source_target_pairs={{0,8},{1,9},{2,10},{3,11},{4,12},{5,13},{6,14},{7,15},{8,0},{9,1},... | collective-permute-start | bytes 884744 | tf_op jit(solution)/shard_map/ppermute | solution.py:418
  285.8 15.6 %collective-permute-start.41 = (bf16[96,768]{1,0:T(8,128)(2,1)S(1)}, bf16[96,768]{1,0:T(8,128)(2,1)S(1)}, u32[]{:S(2)}, u32[]{:S(2)}) collective-permute-start(bf16[96,768]{1,0:T(8,128)(2,1)S(1)} %fusion.44), channel_id=1, source_target_pairs={{0,1},{1,0},{2,3},{3,2},{4,5},{5,4},{6,7},{7,6},{8,9},{9,8},{10,11... | collective-permute-start | bytes 442376 | tf_op jit(solution)/shard_map/ppermute | solution.py:418
  285.9 15.6 %collective-permute-start.42 = (bf16[96,768]{1,0:T(8,128)(2,1)S(1)}, bf16[96,768]{1,0:T(8,128)(2,1)S(1)}, u32[]{:S(2)}, u32[]{:S(2)}) collective-permute-start(bf16[96,768]{1,0:T(8,128)(2,1)S(1)} %get-tuple-element.332), channel_id=1, source_target_pairs={{0,2},{1,3},{2,0},{3,1},{4,6},{5,7},{6,4},{7,5},{8,10},{9,11},{10,... | collective-permute-start | bytes 442376 | tf_op jit(solution)/shard_map/ppermute | solution.py:418
  287.8 13.7 %collective-permute-start.43 = (bf16[96,768]{1,0:T(8,128)(2,1)S(1)}, bf16[96,768]{1,0:T(8,128)(2,1)S(1)}, u32[]{:S(2)}, u32[]{:S(2)}) collective-permute-start(bf16[96,768]{1,0:T(8,128)(2,1)S(1)} %get-tuple-element.333), channel_id=1, source_target_pairs={{0,3},{1,2},{2,1},{3,0},{4,7},{5,6},{6,5},{7,4},{8,11},{9,10},{10,... | collective-permute-start | bytes 442376 | tf_op jit(solution)/shard_map/ppermute | solution.py:418
  326.8 60.8 %all-to-all-start.2 = ((bf16[32,2,9984]{2,1,0:T(2,128)(2,1)}), bf16[32,2,9984]{2,1,0:T(2,128)(2,1)}, u32[]{:S(2)}, u32[]{:S(2)}) async-start(bf16[32,2,9984]{2,1,0:T(2,128)(2,1)} %reshape.213), calls=%async_computation.2 | async-start | bytes 2555904 | tf_op jit(solution)/shard_map/all_to_all | solution.py:373
  333.7 16.5 %collective-permute-start.45 = (bf16[2,96,768]{2,1,0:T(8,128)(2,1)S(1)}, bf16[2,96,768]{2,1,0:T(8,128)(2,1)S(1)}, u32[]{:S(2)}, u32[]{:S(2)}) collective-permute-start(bf16[2,96,768]{2,1,0:T(8,128)(2,1)S(1)} %get-tuple-element.359), channel_id=1, source_target_pairs={{0,8},{1,9},{2,10},{3,11},{4,12},{5,13},{6,14},{7,15},{8,0},{9,1},... | collective-permute-start | bytes 884744 | tf_op jit(solution)/shard_map/ppermute | solution.py:418
  335.5 14.8 %collective-permute-start.46 = (bf16[2,96,768]{2,1,0:T(8,128)(2,1)S(1)}, bf16[2,96,768]{2,1,0:T(8,128)(2,1)S(1)}, u32[]{:S(2)}, u32[]{:S(2)}) collective-permute-start(bf16[2,96,768]{2,1,0:T(8,128)(2,1)S(1)} %get-tuple-element.360), channel_id=1, source_target_pairs={{0,16},{1,17},{2,18},{3,19},{4,20},{5,21},{6,22},{7,23},{8,24},{9,... | collective-permute-start | bytes 884744 | tf_op jit(solution)/shard_map/ppermute | solution.py:418
  337.0 21.5 %collective-permute-start.47 = (bf16[2,96,768]{2,1,0:T(8,128)(2,1)S(1)}, bf16[2,96,768]{2,1,0:T(8,128)(2,1)S(1)}, u32[]{:S(2)}, u32[]{:S(2)}) collective-permute-start(bf16[2,96,768]{2,1,0:T(8,128)(2,1)S(1)} %get-tuple-element.361), channel_id=1, source_target_pairs={{0,8},{1,9},{2,10},{3,11},{4,12},{5,13},{6,14},{7,15},{8,0},{9,1},... | collective-permute-start | bytes 884744 | tf_op jit(solution)/shard_map/ppermute | solution.py:418
  337.6 21.5 %collective-permute-start.48 = (bf16[2,96,768]{2,1,0:T(8,128)(2,1)S(1)}, bf16[2,96,768]{2,1,0:T(8,128)(2,1)S(1)}, u32[]{:S(2)}, u32[]{:S(2)}) collective-permute-start(bf16[2,96,768]{2,1,0:T(8,128)(2,1)S(1)} %get-tuple-element.362), channel_id=1, source_target_pairs={{0,16},{1,17},{2,18},{3,19},{4,20},{5,21},{6,22},{7,23},{8,24},{9,... | collective-permute-start | bytes 884744 | tf_op jit(solution)/shard_map/ppermute | solution.py:418
  372.6 13.0 %collective-permute-start.52 = (bf16[96,768]{1,0:T(8,128)(2,1)S(1)}, bf16[96,768]{1,0:T(8,128)(2,1)S(1)}, u32[]{:S(2)}, u32[]{:S(2)}) collective-permute-start(bf16[96,768]{1,0:T(8,128)(2,1)S(1)} %get-tuple-element.372), channel_id=1, source_target_pairs={{0,2},{1,3},{2,0},{3,1},{4,6},{5,7},{6,4},{7,5},{8,10},{9,11},{10,... | collective-permute-start | bytes 442376 | tf_op jit(solution)/shard_map/ppermute | solution.py:418
  374.5 11.1 %collective-permute-start.53 = (bf16[96,768]{1,0:T(8,128)(2,1)S(1)}, bf16[96,768]{1,0:T(8,128)(2,1)S(1)}, u32[]{:S(2)}, u32[]{:S(2)}) collective-permute-start(bf16[96,768]{1,0:T(8,128)(2,1)S(1)} %get-tuple-element.373), channel_id=1, source_target_pairs={{0,3},{1,2},{2,1},{3,0},{4,7},{5,6},{6,5},{7,4},{8,11},{9,10},{10,... | collective-permute-start | bytes 442376 | tf_op jit(solution)/shard_map/ppermute | solution.py:418
  398.1 11.4 %all-to-all-start.3 = ((f32[32,3,24]{2,1,0:T(4,128)}), f32[32,3,24]{2,1,0:T(4,128)S(1)}, u32[]{:S(2)}, u32[]{:S(2)}) async-start(f32[32,3,24]{2,1,0:T(4,128)} %copy.65), calls=%async_computation.3 | async-start | bytes 131072 | tf_op jit(solution)/shard_map/all_to_all | solution.py:373
  (56 other events, 530.6 us)

commit v3 on v2

--- a/solution.py
+++ b/solution.py
@@ -149,6 +149,51 @@
     sums_ref[parts + 1 : parts + 2] += column_sum(mlp_grad.astype(F32))
 
 
+def block_settle_kernel(
+    mixed,
+    rows,
+    upstream_rows,
+    modulation,
+    proj,
+    proj_bias,
+    hidden_own,
+    hidden_other,
+    hidden_bias,
+    down_own,
+    down_other,
+    down_bias,
+    place,
+    *refs,
+):
+    made, (hidden, down) = refs[:-2], refs[-2:]
+
+    @pl.when(pl.program_id(0) == 0)
+    def _():
+        for number in range(hidden.shape[1]):
+            line = jnp.bitwise_xor(number, place[1])
+            for pair in range(hidden_own.shape[0]):
+                for core, sources in enumerate(
+                    ((hidden_own, down_own), (hidden_other, down_other))
+                ):
+                    spot = jnp.bitwise_xor(2 * pair + core, place[0])
+                    hidden[spot, line] = sources[0][pair, number]
+                    down[spot, line] = sources[1][pair, number]
+
+    block_kernel(
+        mixed,
+        rows,
+        upstream_rows,
+        modulation,
+        proj,
+        proj_bias,
+        hidden,
+        hidden_bias,
+        down,
+        down_bias,
+        *made,
+    )
+
+
 def attend_back_kernel(attended_grad, qkv, proj, grad_ref, sums_ref):
     width = qkv.shape[-1]
     masks = head_masks(width)
@@ -217,11 +262,15 @@
     return pl.BlockSpec((1,) + array.shape[1:], lambda step: (step + first, 0, 0))
 
 
+def scalars(array, first=0):
+    return pl.BlockSpec(memory_space=pltpu.SMEM)
+
+
 def kept(array, first=0):
     return pl.BlockSpec(array.shape, lambda step: (0,) * array.ndim)
 
 
-def over_latents(kernel, steps, inputs, outputs, flops, first=0, carried=()):
+def over_latents(kernel, steps, inputs, outputs, flops, first=0, carried=(), scratch=()):
     shapes = [jax.ShapeDtypeStruct(shape, kind) for _, shape, kind in outputs]
     moved = sum(a.size * a.dtype.itemsize for _, a in inputs) + sum(
         s.size * s.dtype.itemsize for s in shapes
@@ -238,6 +287,7 @@
         + [pl.BlockSpec(memory_space=pl.ANY) for _ in carried],
         out_specs=[spec(shape, first) for (spec, _, _), shape in zip(outputs, shapes)],
         out_shape=shapes,
+        scratch_shapes=list(scratch),
         input_output_aliases={taken + number: number for number in range(len(carried))},
         cost_estimate=pl.CostEstimate(flops=flops, transcendentals=0, bytes_accessed=moved),
         compiler_params=pltpu.CompilerParams(vmem_limit_bytes=56 << 20),
@@ -255,14 +305,6 @@
             self.pending = self.stages.send(results)
         except StopIteration as end:
             self.value = end.value
-
-
-def settle_kernel(place, own, other, whole_ref):
-    flip = place[0]
-    for pair in range(own.shape[0]):
-        for core, source in enumerate((own, other)):
-            slot = jnp.bitwise_xor(2 * pair + core, flip)
-            whole_ref[0, slot] = source[pair, 0]
 
 
 def settle_heads_kernel(place, own, other, qkv_ref, proj_ref):
@@ -275,6 +317,23 @@
             for kind in range(3):
                 qkv_ref[0, kind, slot] = block[:, kind * width : (kind + 1) * width]
             proj_ref[0, slot] = block[:, 3 * width :]
+
+
+def latent_back_kernel(
+    attended_grad,
+    qkv,
+    proj,
+    weight,
+    rows,
+    modulation,
+    middle_grad,
+    heads_ref,
+    grad_ref,
+    pieces_ref,
+    sums_ref,
+):
+    attend_back_kernel(attended_grad, qkv, proj, heads_ref, sums_ref)
+    entry_back_kernel(heads_ref, weight, rows, modulation, middle_grad, grad_ref, pieces_ref)
 
 
 def split_rows(place, grad, keep_ref, send_ref, lanes):
@@ -370,7 +429,19 @@
 
 
 def exchange(slots, axes):
-    return lax.all_to_all(slots, axes, 0, 0, tiled=True)
+    count, size = slots.shape
+    rows = -(-size // 128)
+    padded = jnp.pad(slots, ((0, 0), (0, rows * 128 - size))).reshape(count, rows, 128)
+    return lax.all_to_all(padded, axes, 0, 0, tiled=True).reshape(count, -1)[:, :size]
+
+
+def share(pieces, axes, count):
+    row = jnp.concatenate([piece.astype(BF16).reshape(-1, 128) for piece in pieces])
+    rows = row.shape[0]
+    row = jnp.pad(row, ((0, -rows % 8), (0, 0)))
+    return lax.all_to_all(
+        jnp.broadcast_to(row[None], (count,) + row.shape), axes, 0, 0, tiled=True
+    )[:, :rows]
 
 
 def on_device(
@@ -403,17 +474,21 @@
 
     silu_value, silu_pullback = jax.vjp(jax.nn.silu, condition.astype(F32))
     silu_cond = silu_value.astype(BF16)
-    sent = jnp.concatenate(
-        [
-            ada_weight.reshape(ada_rows, count, ada_cols).transpose(1, 0, 2).reshape(count, -1),
-            silu_cond.reshape(latents, count, ada_rows).transpose(1, 0, 2).reshape(count, -1),
-            jnp.broadcast_to(
-                jnp.concatenate([silu_cond.reshape(-1), qv_bias.reshape(-1), hidden_bias])[None],
-                (count, latents * D + 2 * head_width + hidden_width),
-            ),
-        ],
-        axis=1,
-    )
+    def packed_slots(weight, silu_rows):
+        return jnp.concatenate(
+            [
+                weight.reshape(ada_rows, count, ada_cols).transpose(1, 0, 2).reshape(count, -1),
+                silu_rows.reshape(latents, count, ada_rows).transpose(1, 0, 2).reshape(count, -1),
+                jnp.broadcast_to(
+                    jnp.concatenate([silu_rows.reshape(-1), qv_bias.reshape(-1), hidden_bias])[
+                        None
+                    ],
+                    (count, latents * D + 2 * head_width + hidden_width),
+                ),
+            ],
+            axis=1,
+        )
+
     def swap(array, mask):
         return lax.ppermute(array, axes, [(device, device ^ mask) for device in range(count)])
 
@@ -446,9 +521,14 @@
         (arrived,) = yield [(send, across)]
         summed = keep + arrived.astype(F32)
         line, side, above, far = [summed[number] for number in range(4)]
-        low = [block.astype(BF16) for block in (side[:half], above[half:], far[:half], far[half:])]
-        arrived = yield list(zip(low, (along, upward, along, upward)))
-        side_low, above_high, far_low, far_high = [block.astype(F32) for block in arrived]
+        moved = [
+            jnp.concatenate(pair).astype(BF16)
+            for pair in ((side[:half], far[:half]), (above[half:], far[half:]))
+        ]
+        arrived = yield list(zip(moved, (along, upward)))
+        arrived = [block.astype(F32) for block in arrived]
+        side_low, far_low = arrived[0][:half], arrived[0][half:]
+        above_high, far_high = arrived[1][:half], arrived[1][half:]
         arrived = yield [
             ((above[:half] + far_low).astype(BF16), upward),
             ((side[half:] + far_high).astype(BF16), along),
@@ -471,18 +551,6 @@
         flat = blocks.reshape(-1, blocks.shape[-1])
         flat = lax.psum_scatter(flat, "dp", scatter_dimension=0, tiled=True)
         return lax.psum_scatter(flat, "tensor", scatter_dimension=0, tiled=True).astype(F32)
-
-    def settled(own, other):
-        shape = (tensor_size, dp_size, slab, D)
-        (whole_set,) = placed_call(
-            settle_kernel,
-            position,
-            tensor_size,
-            [(by_second, own), (by_second, other)],
-            [(to_first, shape, BF16)],
-            0,
-        )
-        return whole_set.reshape(1, tensor_size, D, D)
 
     def settled_heads(own, other):
         qkv_set, proj_set = placed_call(
@@ -505,10 +573,22 @@
     for size in (ada_rows * latents, latents * D, 2 * head_width):
         ends.append(ends[-1] + size)
 
-    def modulate(silu_all, ada_columns):
-        columns = jnp.dot(silu_all, ada_columns, preferred_element_type=F32) + ada_bias.astype(F32)
-        back = exchange(columns.reshape(count, latents, ada_cols), axes)
-        return back.transpose(1, 0, 2).reshape(latents, 6, D)
+    def opened(slots):
+        got = exchange(slots, axes)
+        columns = jnp.dot(
+            got[:, ends[1] : ends[2]].reshape(count * latents, D),
+            got[:, : ends[0]].reshape(D, ada_cols),
+            preferred_element_type=F32,
+        )
+        columns = columns + ada_bias.astype(F32)
+        return got, jnp.pad(
+            columns.reshape(count, latents * ada_cols), ((0, 0), (0, -latents * ada_cols % 128))
+        ).reshape(count, -1, 128)
+
+    def modulate(columns):
+        back = lax.all_to_all(columns, axes, 0, 0, tiled=True)
+        back = back.reshape(count, -1)[:, : latents * ada_cols]
+        return back.reshape(count, latents, ada_cols).transpose(1, 0, 2).reshape(latents, 6, D)
 
     heads_in = hidden_in = down_in = None
     if direct:
@@ -520,19 +600,16 @@
                 down_weight.T,
             )
         ]
-    got = slot([heads_in] if direct else [], (sent,), lambda slots: exchange(slots, axes))
-    ada_columns = got[:, : ends[0]].reshape(D, ada_cols)
+    sent = slot([heads_in] if direct else [], (ada_weight, silu_cond), packed_slots)
+    got, columns = slot([heads_in, hidden_in] if direct else [], (sent,), opened)
     silu_columns = got[:, ends[0] : ends[1]].reshape(count * latents, ada_rows)
-    silu_all = got[:, ends[1] : ends[2]].reshape(count * latents, D)
     qv_full = got[:tensor_size, ends[2] : ends[3]].reshape(tensor_size, 2, head_width)
     hidden_bias_full = got[:tensor_size, ends[3] :]
     modulation = slot(
-        [heads_in, hidden_in] if direct else [], (silu_all, ada_columns), modulate
+        [heads_in, hidden_in, down_in] if direct else [], (columns,), modulate
     )
     if direct:
-        slot([heads_in, hidden_in, down_in], (), lambda: ())
-        slot([heads_in, hidden_in, down_in], (), lambda: ())
-        qkv_full, proj_full = settled_heads(*heads_in.value)
+        slot([heads_in, hidden_in], (), lambda: ())
     else:
         qkv_full = gathered(qkv_weight)
         proj_full = gathered(proj_weight.T)
@@ -544,27 +621,44 @@
 
     unit = 2 * tokens * D * D
 
-    def attend(rows, pieces, weight, bias):
-        return over_latents(
-            attend_kernel,
-            latents,
-            [(row_block, rows), (per_latent, pieces), (whole, weight), (whole, bias)],
-            [
-                (row_block, (tokens, D), BF16),
-                (row_block, spread(3, tokens, head_width), BF16),
-                (row_block, spread(tokens, head_width), BF16),
-            ],
-            5 * unit,
-        )
-
-    input_one, qkv, mixed = slot(
-        [hidden_in, down_in] if direct else [],
-        (latents_in, modulation, qkv_full, qv_full),
-        attend,
-    )
+    def attend(first, steps):
+        def run(rows, pieces, weight, bias, *kept_back):
+            return over_latents(
+                attend_kernel,
+                steps,
+                [(row_block, rows), (per_latent, pieces), (whole, weight), (whole, bias)],
+                [
+                    (row_block, (tokens, D), BF16),
+                    (row_block, spread(3, tokens, head_width), BF16),
+                    (row_block, spread(tokens, head_width), BF16),
+                ],
+                2 * unit * steps,
+                first,
+                kept_back,
+            )
+
+        return run
+
+    def entered(rows, pieces, bias, *weights):
+        weights = settled_heads(*weights)
+        return attend(0, 1)(rows, pieces, weights[0], bias), weights
+
     if direct:
-        hidden_full = slot([down_in], hidden_in.value, settled)
-        down_full = settled(*down_in.value)
+        carried, (qkv_full, proj_full) = slot(
+            [down_in], (latents_in, modulation, qv_full) + heads_in.value, entered
+        )
+        for latent in range(1, latents):
+            flows = [flow for flow in (hidden_in, down_in) if flow.value is None]
+            carried = slot(
+                flows,
+                (latents_in, modulation, qkv_full, qv_full) + tuple(carried),
+                attend(latent, 1),
+            )
+        while down_in.value is None:
+            slot([down_in], (), lambda: ())
+    else:
+        carried = attend(0, latents)(latents_in, modulation, qkv_full, qv_full)
+    input_one, qkv, mixed = carried
     (
         block_out,
         activated,
@@ -576,7 +670,7 @@
         late_pieces,
         late_sums,
     ) = over_latents(
-        block_kernel,
+        block_settle_kernel if direct else block_kernel,
         latents,
         [
             (row_block, mixed),
@@ -585,11 +679,12 @@
             (per_latent, modulation),
             (whole, proj_full),
             (whole, proj_bias[None]),
-            (whole, hidden_full),
-            (whole, hidden_bias_full),
-            (whole, down_full),
-            (whole, down_bias[None]),
-        ],
+        ]
+        + [(whole, array) for array in (hidden_in.value if direct else (hidden_full,))]
+        + [(whole, hidden_bias_full)]
+        + [(whole, array) for array in (down_in.value if direct else (down_full,))]
+        + [(whole, down_bias[None])]
+        + ([(scalars, position)] if direct else []),
         [
             (row_block, (tokens, D), F32),
             (row_block, spread(tokens, hidden_width), BF16),
@@ -602,6 +697,7 @@
             (kept, (tensor_size + 2, D), F32),
         ],
         18 * unit,
+        scratch=[pltpu.VMEM((dp_size, tensor_size, slab, D), BF16)] * 2 if direct else (),
     )
 
     split_shape = (dp_size // 2, tensor_size, slab, D)
@@ -627,42 +723,71 @@
             4 * unit,
         )
 
-    def attend_back(first, steps, carried):
-        def run(outer, heads, weight, *kept_back):
+    def latent_back(first, steps, carried):
+        def run(outer, heads, proj, weight, rows, pieces, middle, *kept_back):
             return over_latents(
-                attend_back_kernel,
+                latent_back_kernel,
                 steps,
-                [(row_block, outer), (row_block, heads), (whole, weight)],
+                [
+                    (row_block, outer),
+                    (row_block, heads),
+                    (whole, proj),
+                    (whole, weight),
+                    (row_block, rows),
+                    (per_latent, pieces),
+                    (row_block, middle),
+                ],
                 [
                     (row_block, spread(3, tokens, head_width), BF16),
+                    (row_block, (tokens, D), F32),
+                    (per_latent, (latents, 2, D), F32),
                     (kept, spread(3, head_width), F32),
                 ],
-                4 * unit * steps,
+                6 * unit * steps,
                 first,
                 kept_back,
             )
 
-        return (attended_grad, qkv, proj_full) + carried, run
-
-    def entry_back(first, steps, carried):
-        def run(heads, weight, rows, pieces, outer, *kept_back):
-            return over_latents(
-                entry_back_kernel,
-                steps,
-                [
-                    (row_block, heads),
-                    (whole, weight),
-                    (row_block, rows),
-                    (per_latent, pieces),
-                    (row_block, outer),
-                ],
-                [(row_block, (tokens, D), F32), (per_latent, (latents, 2, D), F32)],
-                unit * steps,
-                first,
-                kept_back,
-            )
-
-        return (qkv_grad, qkv_full, latents_in, modulation, middle_grad) + carried, run
+        inputs = (attended_grad, qkv, proj_full, qkv_full, latents_in, modulation, middle_grad)
+        return inputs + carried, run
+
+    vector_rows = latents * 6 * D // 128
+
+    def vectors(early, late, sums, head_sums):
+        row = jnp.concatenate(
+            [
+                piece.astype(BF16).reshape(-1, 128)
+                for piece in (jnp.concatenate([early, late], axis=1), sums, head_sums[:, ::2])
+            ]
+        )
+        return jnp.pad(row, ((0, -row.shape[0] % 16), (0, 0)))
+
+    def modulation_of(shared):
+        return shared[:, :vector_rows].reshape(count * latents, 6 * D)
+
+    def ada_back(shared, silu_columns, to_owner):
+        modulation_all = modulation_of(shared)
+        slots = contract(modulation_all, ada_weight, 1, 1).reshape(count, latents * ada_rows)
+        slots = jnp.dot(to_owner, slots, precision=lax.Precision.HIGHEST)
+        return exchange(slots, axes), contract(silu_columns, modulation_all, 0, 0)
+
+    def condition_back(slots):
+        grad = slots.reshape(count, latents, ada_rows).transpose(1, 0, 2).reshape(latents, D)
+        return silu_pullback(grad)[0]
+
+    numbers = lax.broadcasted_iota(jnp.int32, (count, count), 0)
+    order = lax.broadcasted_iota(jnp.int32, (count, count), 1)
+    if direct:
+        plane, cell = order // (count // 2), order % (count // 2)
+        pair, line = cell // tensor_size, cell % tensor_size
+        order = jnp.bitwise_xor(2 * pair + plane, position[0]) * tensor_size + jnp.bitwise_xor(
+            line, position[1]
+        )
+    to_owner = (numbers == order).astype(F32)
+    silu_columns = contract(
+        to_owner.astype(BF16), silu_columns.reshape(count, latents * ada_rows), 0, 0
+    )
+    silu_columns = silu_columns.astype(BF16).reshape(count * latents, ada_rows)
 
     if direct:
         down_out = Flow(reduce_stages(*square_grad(mlp_grad, activated)))
@@ -672,59 +797,60 @@
         qkv_sums, carried = 0.0, ()
         for latent in range(latents):
             flows = [flow for flow in (down_out, hidden_out) if flow.value is None]
-            qkv_grad, own_sums = slot(flows, *attend_back(latent, 1, carried))
-            carried, qkv_sums = (qkv_grad,), qkv_sums + own_sums
+            *carried, own_sums = slot(flows, *latent_back(latent, 1, tuple(carried)))
+            qkv_sums = qkv_sums + own_sums
+        qkv_grad, input_grad, early_pieces = carried
+        shared_in = Flow(
+            gather_stages(vectors(early_pieces, late_pieces, late_sums, qkv_sums))
+        )
         flows = [flow for flow in (down_out, hidden_out) if flow.value is None]
         heads_out = Flow(
-            reduce_stages(*slot(flows, (input_one, qkv_grad, attended_grad, mixed), heads_grad))
-        )
-        input_grad, early_pieces = slot([heads_out], *entry_back(0, latents, ()))
-        while heads_out.value is None:
-            slot([heads_out], (), lambda: ())
-        while hidden_out.value is None:
-            slot([hidden_out], (), lambda: ())
+            reduce_stages(
+                *slot(
+                    flows + [shared_in], (input_one, qkv_grad, attended_grad, mixed), heads_grad
+                )
+            )
+        )
+        for _ in range(3):
+            slot([heads_out, shared_in], (), lambda: ())
+        shared = jnp.stack(shared_in.value).reshape(count, -1, 128)
+        silu_grad, ada_weight_grad = slot(
+            [heads_out], (shared, silu_columns, to_owner), ada_back
+        )
+        condition_grad = condition_back(silu_grad)
         down_weight_grad, hidden_weight_grad = down_out.value.T, hidden_out.value
         packed_grad = heads_out.value.reshape(slab, 4, head_width)
         qkv_weight_grad = packed_grad[:, :3].swapaxes(0, 1)
         proj_weight_grad = packed_grad[:, 3].T
     else:
-        inputs, run = attend_back(0, latents, ())
-        qkv_grad, qkv_sums = run(*inputs)
+        inputs, run = latent_back(0, latents, ())
+        qkv_grad, input_grad, early_pieces, qkv_sums = run(*inputs)
         down_weight_grad = scattered(weight_grad(mlp_grad, activated)).T
         hidden_weight_grad = scattered(weight_grad(input_two, preact_grad))
         proj_weight_grad = scattered(weight_grad(attended_grad, mixed)).T
         qkv_weight_grad = scattered(
             weight_grad(input_one, qkv_grad.reshape(-1, tokens, head_width))
         ).reshape(qkv_weight.shape)
-        inputs, run = entry_back(0, latents, ())
-        input_grad, early_pieces = run(*inputs)
-    modulation_grad = jnp.concatenate([early_pieces, late_pieces], axis=1).astype(BF16)
-    vectors = jnp.concatenate(
-        [
-            modulation_grad.reshape(-1),
-            qkv_sums[:, ::2].astype(BF16).reshape(-1),
-            late_sums.astype(BF16).reshape(-1),
-        ]
-    )
-    shared = exchange(jnp.broadcast_to(vectors[None], (count, vectors.shape[0])), axes)
-    split = latents * 6 * D
-    modulation_all = shared[:, :split].reshape(count * latents, 6 * D)
-    ones = jnp.ones((1, count), BF16)
-    totals = contract(ones, shared[:, split:], 1, 0)[0]
+        shared = share([vectors(early_pieces, late_pieces, late_sums, qkv_sums)], axes, count)
+        silu_grad, ada_weight_grad = ada_back(shared, silu_columns, to_owner)
+        condition_grad = condition_back(silu_grad)
+    totals = jnp.sum(shared[:, vector_rows:].astype(F32), axis=0).reshape(-1)
+    sums_end = (tensor_size + 2) * D
+    rest = totals[:sums_end].reshape(tensor_size + 2, D)
     qv_bias_grad = lax.dynamic_index_in_dim(
-        totals[: 2 * D].reshape(tensor_size, 2, head_width), place, 0, keepdims=False
-    )
-    rest = totals[2 * D :].reshape(tensor_size + 2, D)
+        totals[sums_end : sums_end + 2 * D].reshape(tensor_size, 2, head_width),
+        place,
+        0,
+        keepdims=False,
+    )
     hidden_bias_grad = lax.dynamic_index_in_dim(rest, place, 0, keepdims=False)
     proj_bias_grad, down_bias_grad = rest[tensor_size], rest[tensor_size + 1]
-    ada_weight_grad = contract(silu_columns, modulation_all, 0, 0)
     ada_bias_grad = lax.dynamic_index_in_dim(
-        contract(jnp.ones((1, count * latents), BF16), modulation_all, 1, 0).reshape(count, ada_cols), here, 0, keepdims=False
-    )
-    silu_grad = exchange(
-        contract(modulation_all, ada_weight, 1, 1).reshape(count, latents, ada_rows), axes
-    )
-    condition_grad = silu_pullback(silu_grad.transpose(1, 0, 2).reshape(latents, D))[0]
+        jnp.sum(modulation_of(shared).astype(F32), axis=0).reshape(count, ada_cols),
+        here,
+        0,
+        keepdims=False,
+    )
     return (
         block_out,
         input_grad,

time: 417 us -> 382 us (0.916)
  waiting for transfers between devices: 97.8 us -> 70.1 us
  other arithmetic: 38.9 us -> 50.7 us
  local copies, waits for them, and re-layouts: 46 us -> 34.7 us
    ppermute x54 -> x56, waiting for transfers between devices: 86 us -> 64.6 us  [swap(): lax.ppermute(array, axes, [(device, device ^ mask) for device in range(co...]
    unnamed x105, local copies, waits for them, and re-layouts: 22.3 us -> 8.33 us
    pallas_call x6 -> x4, Pallas kernels: 48.2 us -> 36.2 us  [placed_call(): pl.pallas_call(kernel, grid_spec=pltpu.PrefetchScalarGridSpec(num_scalar_...]
    another operation x8 -> x11, other arithmetic: 11.4 us -> 22.5 us
    pallas_call x6 -> x7, Pallas kernels: 85.6 us -> 96.1 us  [over_latents(): pl.pallas_call(body, grid=(steps,), in_specs=[spec(array, first) for spec...]
    broadcast_in_dim x1 -> x0, other arithmetic: 9.48 us -> none  [on_device(): jnp.broadcast_to(vectors[None], (count, vectors.shape[0]))]
    all_to_all x3 -> x2, waiting for transfers between devices: 11.8 us -> 5.48 us  [exchange(): lax.all_to_all(padded, axes, 0, 0, tiled=True).reshape(count, -1)[:, :size]]
    all_to_all x3 -> x2, starting transfers between devices: 14.8 us -> 10.2 us  [exchange(): lax.all_to_all(padded, axes, 0, 0, tiled=True).reshape(count, -1)[:, :size]]
  transfers between devices with their start and end apart: 57 -> 58, of which waited for: 20 -> 18; matrix products, arithmetic and copies ran while one was open for 5% -> 7% of each run, Pallas kernels for 20% -> 25%
where the time goes in v3:
time: 382 us; the launch traced here: 375 us
  Pallas kernels  132 us (35%)
  starting transfers between devices  72.8 us (19%)
  waiting for transfers between devices  70.1 us (18%)
  other arithmetic  50.7 us (13%)
  local copies, waits for them, and re-layouts  34.7 us (9%)
  blocking collectives  9.8 us (3%)
    pallas_call x7, Pallas kernels, over_latents(): pl.pallas_call(body, grid=(steps,), in_specs=[spec(array, first) for spec...  96.1 us
    ppermute x56, waiting for transfers between devices, swap(): lax.ppermute(array, axes, [(device, device ^ mask) for device in range(co...  64.6 us
    ppermute x56, starting transfers between devices, swap(): lax.ppermute(array, axes, [(device, device ^ mask) for device in range(co...  62.6 us
    pallas_call x4, Pallas kernels, placed_call(): pl.pallas_call(kernel, grid_spec=pltpu.PrefetchScalarGridSpec(num_scalar_...  36.2 us
    another operation x9, other arithmetic  20.2 us
    all_to_all x2, starting transfers between devices, exchange(): lax.all_to_all(padded, axes, 0, 0, tiled=True).reshape(count, -1)[:, :size]  10.2 us
    another operation x11, other arithmetic, gather_stages(): own = jnp.stack([line, side, above, jnp.concatenate([first, second])])  9.94 us
    all_to_all x1, blocking collectives, modulate(): back = lax.all_to_all(columns, axes, 0, 0, tiled=True)  9.8 us
  transfers between devices with their start and end apart: 58, of which 18 were waited for; matrix products, arithmetic and copies ran while one was open for 7% of the time, Pallas kernels for 25%

profile of v3, /device:TPU:0, one launch (start us, length us, event | category | flops | bytes accessed | tf_op | source)
XLA Modules:
  0.0 375.4 jit_solution(12993512399173543444)
XLA Ops:
  3.2 3.1 collective-permute-start
  6.3 2.6 collective-permute-start.1
  10.6 1.6 reshape.184
  13.3 7.0 %collective-permute-done.1 = bf16[96,768]{1,0:T(8,128)(2,1)S(1)} collective-permute-done((bf16[96,768]{1,0:T(8,128)(2,1)S(1)}, bf16[96,768]{1,0:T(8,128)(2,1)S(1)}, u32[]{:S(2)}, u32[]{:S(2)}) %collective-permute-start.1) | collective-permute-done | bytes 147488 | tf_op jit(solution)/shard_map/ppermute | solution.py:493
  21.5 5.6 %all-to-all-start = ((bf16[32,55,128]{2,1,0:T(8,128)(2,1)}), bf16[32,55,128]{2,1,0:T(8,128)(2,1)S(1)}, u32[]{:S(2)}, u32[]{:S(2)}) async-start(bf16[32,55,128]{2,1,0:T(8,128)(2,1)} %reshape.190), calls=%async_computation | async-start | bytes 917504 | tf_op jit(solution)/shard_map/all_to_all | solution.py:435
  27.1 1.8 collective-permute-start.3
  31.8 2.5 collective-permute-start.6
  34.8 5.5 %all-to-all-done = bf16[32,55,128]{2,1,0:T(8,128)(2,1)S(1)} async-done(((bf16[32,55,128]{2,1,0:T(8,128)(2,1)}), bf16[32,55,128]{2,1,0:T(8,128)(2,1)S(1)}, u32[]{:S(2)}, u32[]{:S(2)}) %all-to-all-start) | async-done | bytes 450592 | tf_op jit(solution)/shard_map/all_to_all | solution.py:435
  43.2 7.5 %collective-permute-done.6 = bf16[96,768]{1,0:T(8,128)(2,1)} collective-permute-done((bf16[96,768]{1,0:T(8,128)(2,1)}, bf16[96,768]{1,0:T(8,128)(2,1)}, u32[]{:S(2)}, u32[]{:S(2)}) %collective-permute-start.6) | collective-permute-done | bytes 147488 | tf_op jit(solution)/shard_map/ppermute | solution.py:493
  52.3 2.0 fusion.56
  57.3 3.2 collective-permute-start.12
  61.1 4.1 %collective-permute-done.12 = bf16[96,768]{1,0:T(8,128)(2,1)S(1)} collective-permute-done((bf16[96,768]{1,0:T(8,128)(2,1)}, bf16[96,768]{1,0:T(8,128)(2,1)S(1)}, u32[]{:S(2)}, u32[]{:S(2)}) %collective-permute-start.12) | collective-permute-done | bytes 147488 | tf_op jit(solution)/shard_map/ppermute | solution.py:493
  65.7 3.7 collective-permute-done.13
  69.4 1.7 collective-permute-start.14
  71.1 9.8 %all_to_all.15 = f32[32,4,128]{2,1,0:T(4,128)S(1)} all-to-all(f32[32,4,128]{2,1,0:T(4,128)S(1)} %reshape.195), channel_id=1, replica_groups=mesh['dp'=8,'tensor'=4] {'dp','tensor'}, dimensions={0} | all-to-all | bytes 131072 | tf_op jit(solution)/shard_map/all_to_all | solution.py:589
  88.5 2.0 fusion.55
  90.6 5.0 %collective-permute-done.16 = bf16[2,96,768]{2,1,0:T(8,128)(2,1)} collective-permute-done((bf16[2,96,768]{2,1,0:T(8,128)(2,1)}, bf16[2,96,768]{2,1,0:T(8,128)(2,1)}, u32[]{:S(2)}, u32[]{:S(2)}) %collective-permute-start.16) | collective-permute-done | bytes 294944 | tf_op jit(solution)/shard_map/ppermute | solution.py:493
  98.6 6.8 %shard_map.228 = (bf16[4,3,8,96,192]{4,3,2,1,0:T(8,128)(2,1)}, bf16[4,8,96,192]{3,2,1,0:T(8,128)(2,1)}) custom-call(s32[2]{0:T(128)} %pad_add_fusion.place.refs_12_, bf16[4,4,96,768]{3,2,1,0:T(8,128)(2,1)} %copy-done.1, bf16[4,4,96,768]{3,2,1,0:T(8,128)(2,1)} %collective-permute-done.15.other), custom_call_target="tpu_custom_call" | custom-call | bytes 9437184 | tf_op jit(solution)/shard_map/pallas_call | solution.py:369
  106.6 8.4 %shard_map.229 = (bf16[768,768]{1,0:T(8,128)(2,1)}, bf16[4,3,768,192]{3,2,1,0:T(8,128)(2,1)}, bf16[4,768,192]{2,1,0:T(8,128)(2,1)}) custom-call(bf16[768,768]{1,0:T(8,128)(2,1)} %refs_4_.2, f32[3,6,768]{2,1,0:T(8,128)} %reshape.198.refs_1_.refs_3_.refs_5_, bf16[1,4,3,768,192]{4,3,2,1,0:T(8,128)(2,1)} %bitcast.222, bf16[4,2,192]{2,1,0:T(2,128)(2,1)} %reshape.199.refs_3_), custom_call_target="tpu_custom_call" | custom-call | flops 1811939328 | bytes 10675200 | tf_op jit(solution)/shard_map/pallas_call | solution.py:283
  118.8 8.3 %shard_map.230 = (bf16[768,768]{1,0:T(8,128)(2,1)}, bf16[4,3,768,192]{3,2,1,0:T(8,128)(2,1)}, bf16[4,768,192]{2,1,0:T(8,128)(2,1)}) custom-call(bf16[768,768]{1,0:T(8,128)(2,1)} %refs_4_.2, f32[3,6,768]{2,1,0:T(8,128)} %reshape.198.refs_1_.refs_3_.refs_5_, ...), custom_call_target="tpu_custom_call", output_to_operand_aliasing={{0}: (4, {}), {1}: (5, {}), {2}: (6, {})} | custom-call | flops 1811939328 | bytes 10675200 | tf_op jit(solution)/shard_map/pallas_call | solution.py:283
  127.2 1.9 pad_maximum_fusion.2.refs_9_
  131.9 8.4 %shard_map.231 = (bf16[768,768]{1,0:T(8,128)(2,1)}, bf16[4,3,768,192]{3,2,1,0:T(8,128)(2,1)}, bf16[4,768,192]{2,1,0:T(8,128)(2,1)}) custom-call(bf16[768,768]{1,0:T(8,128)(2,1)} %refs_4_.2, f32[3,6,768]{2,1,0:T(8,128)} %reshape.198.refs_1_.refs_3_.refs_5_, ...), custom_call_target="tpu_custom_call", output_to_operand_aliasing={{0}: (4, {}), {1}: (5, {}), {2}: (6, {})} | custom-call | flops 1811939328 | bytes 10675200 | tf_op jit(solution)/shard_map/pallas_call | solution.py:283
  140.3 30.5 %shard_map.232 = (f32[768,768]{1,0:T(8,128)}, bf16[4,768,768]{2,1,0:T(8,128)(2,1)}, bf16[4,768,768]{2,1,0:T(8,128)(2,1)}, bf16[768,768]{1,0:T(8,128)(2,1)}, bf16...) custom-call(bf16[4,768,192]{2,1,0:T(8,128)(2,1)} %get-tuple-element., ...), custom_call_target="tpu_custom_call" | custom-call | flops 16307453952 | bytes 31970312 | tf_op jit(solution)/shard_map/pallas_call | solution.py:283
  170.8 9.0 %shard_map.233 = (f32[4,4,96,768]{3,2,1,0:T(8,128)}, bf16[4,4,96,768]{3,2,1,0:T(8,128)(2,1)}) custom-call(s32[2]{0:T(128)} %pad_add_fusion.place.refs_12_, bf16[768,768]{1,0:T(8,128)(2,1)} %get-tuple-element.351.left, bf16[4,768,768]{2,1,0:T(8,128)(2,1)} %get-tuple-element.352.right), custom_call_target="tpu_custom_call" | custom-call | flops 3623878656 | bytes 12976128 | tf_op jit(solution)/shard_map/pallas_call | solution.py:369
  180.2 9.1 %shard_map.234 = (f32[4,4,96,768]{3,2,1,0:T(8,128)}, bf16[4,4,96,768]{3,2,1,0:T(8,128)(2,1)}) custom-call(s32[2]{0:T(128)} %pad_add_fusion.place.refs_12_, bf16[768,768]{1,0:T(8,128)(2,1)} %get-tuple-element.358.left, bf16[4,768,768]{2,1,0:T(8,128)(2,1)} %get-tuple-element.359.right), custom_call_target="tpu_custom_call" | custom-call | flops 3623878656 | bytes 12976128 | tf_op jit(solution)/shard_map/pallas_call | solution.py:369
  189.4 3.0 fusion.61
  196.0 13.4 %shard_map.235 = (bf16[4,3,768,192]{3,2,1,0:T(8,128)(2,1)}, f32[768,768]{1,0:T(8,128)}, f32[3,2,768]{2,1,0:T(2,128)}, f32[4,3,192]{2,1,0:T(4,128)}) custom-call(bf16[768,768]{1,0:T(8,128)(2,1)} %get-tuple-element.451.refs_0_.outer, bf16[4,3,768,192]{3,2,1,0:T(8,128)(2,1)} %get-tuple-element.419.refs_1_, bf16[1,4,768,192]{3,2,1,0:T(8,128)(2,1)} %bitcast.232, ...), custom_call_target="tpu_custom_call" | custom-call | flops 5435817984 | bytes 18957312 | tf_op jit(solution)/shard_map/pallas_call | solution.py:283
  210.1 5.5 %fusion.60 = (bf16[4,4,96,768]{3,2,1,0:T(8,128)(2,1)S(1)}, f32[4,4,96,768]{3,2,1,0:T(8,128)}) fusion(f32[4,4,96,768]{3,2,1,0:T(8,128)} %get-tuple-element.383, bf16[4,4,96,768]{3,2,1,0:T(8,128)(2,1)S(1)} %collective-permute-done.27), kind=kLoop, calls=%fused_computation.170 | loop fusion | flops 3538944 | bytes 14155776 | tf_op jit(solution)/shard_map/convert.36
  224.5 13.6 %shard_map.236 = (bf16[4,3,768,192]{3,2,1,0:T(8,128)(2,1)}, f32[768,768]{1,0:T(8,128)}, f32[3,2,768]{2,1,0:T(2,128)}, f32[4,3,192]{2,1,0:T(4,128)}) custom-call(bf16[768,768]{1,0:T(8,128)(2,1)} %get-tuple-element.451.refs_0_.outer, bf16[4,3,768,192]{3,2,1,0:T(8,128)(2,1)} %get-tuple-element.419.refs_1_, ...), custom_call_target="tpu_custom_call", output_to_operand_aliasing={{0}: (7, {}), {1}: (8, {}), {2}: (9, {})} | custom-call | flops 5435817984 | bytes 18957312 | tf_op jit(solution)/shard_map/pallas_call | solution.py:283
  238.1 3.8 %collective-permute-done.28 = bf16[2,96,768]{2,1,0:T(8,128)(2,1)S(1)} collective-permute-done((bf16[2,96,768]{2,1,0:T(8,128)(2,1)}, bf16[2,96,768]{2,1,0:T(8,128)(2,1)S(1)}, u32[]{:S(2)}, u32[]{:S(2)}) %collective-permute-start.28) | collective-permute-done | bytes 294944 | tf_op jit(solution)/shard_map/ppermute | solution.py:493
  251.7 2.8 collective-permute-start.34
  254.5 13.4 %shard_map.237 = (bf16[4,3,768,192]{3,2,1,0:T(8,128)(2,1)}, f32[768,768]{1,0:T(8,128)}, f32[3,2,768]{2,1,0:T(2,128)}, f32[4,3,192]{2,1,0:T(4,128)}) custom-call(bf16[768,768]{1,0:T(8,128)(2,1)} %get-tuple-element.451.refs_0_.outer, bf16[4,3,768,192]{3,2,1,0:T(8,128)(2,1)} %get-tuple-element.419.refs_1_, ...), custom_call_target="tpu_custom_call", output_to_operand_aliasing={{0}: (7, {}), {1}: (8, {}), {2}: (9, {})} | custom-call | flops 5435817984 | bytes 18957312 | tf_op jit(solution)/shard_map/pallas_call | solution.py:283
  273.9 2.8 collective-permute-start.39
  278.3 11.2 %shard_map.238 = (f32[4,4,96,768]{3,2,1,0:T(8,128)}, bf16[4,4,96,768]{3,2,1,0:T(8,128)(2,1)}) custom-call(s32[2]{0:T(128)} %pad_add_fusion.place.refs_12_, bf16[768,768]{1,0:T(8,128)(2,1)} %get-tuple-element.449.entry, bf16[4,3,768,192]{3,2,1,0:T(8,128)(2,1)} %get-tuple-element.450.qkv_grad, bf16[768,768]{1,0:T(8,128)(2,1)} %get-tuple-element.451.refs_0_.outer, ...), custom_call_target="tpu_custom_call" | custom-call | flops 3623878656 | bytes 14155776 | tf_op jit(solution)/shard_map/pallas_call | solution.py:369
  289.5 2.8 collective-permute-start.42
  292.4 3.0 collective-permute-done.42
  297.4 4.7 %collective-permute-done.44 = bf16[4,160,128]{2,1,0:T(8,128)(2,1)S(1)} collective-permute-done((bf16[4,160,128]{2,1,0:T(8,128)(2,1)S(1)}, bf16[4,160,128]{2,1,0:T(8,128)(2,1)S(1)}, u32[]{:S(2)}, u32[]{:S(2)}) %collective-permute-start.44) | collective-permute-done | bytes 163872 | tf_op jit(solution)/shard_map/ppermute | solution.py:493
  303.1 5.3 %fusion.59 = (bf16[4,4,96,768]{3,2,1,0:T(8,128)(2,1)S(1)}, f32[4,4,96,768]{3,2,1,0:T(8,128)}) fusion(f32[4,4,96,768]{3,2,1,0:T(8,128)} %get-tuple-element.455, bf16[4,4,96,768]{3,2,1,0:T(8,128)(2,1)S(1)} %collective-permute-done.43), kind=kLoop, calls=%fused_computation.169 | loop fusion | flops 3538944 | bytes 14155776 | tf_op jit(solution)/shard_map/convert.15
  312.9 12.7 %collective-permute-done.48 = bf16[2,160,128]{2,1,0:T(8,128)(2,1)S(1)} collective-permute-done((bf16[2,160,128]{2,1,0:T(8,128)(2,1)S(1)}, bf16[2,160,128]{2,1,0:T(8,128)(2,1)S(1)}, u32[]{:S(2)}, u32[]{:S(2)}) %collective-permute-start.48) | collective-permute-done | bytes 81952 | tf_op jit(solution)/shard_map/ppermute | solution.py:493
  327.2 2.6 fusion.2
  333.7 1.8 fusion.18
  335.5 1.8 fusion.21
  337.3 4.1 %collective-permute-done.50 = bf16[2,96,768]{2,1,0:T(8,128)(2,1)S(1)} collective-permute-done((bf16[2,96,768]{2,1,0:T(8,128)(2,1)}, bf16[2,96,768]{2,1,0:T(8,128)(2,1)S(1)}, u32[]{:S(2)}, u32[]{:S(2)}) %collective-permute-start.50) | collective-permute-done | bytes 294944 | tf_op jit(solution)/shard_map/ppermute | solution.py:493
  347.3 2.1 reshape.206
  351.7 4.6 %all-to-all-start.2 = ((f32[32,1,128]{2,1,0:T(1,128)}), f32[32,1,128]{2,1,0:T(1,128)S(1)}, u32[]{:S(2)}, u32[]{:S(2)}) async-start(f32[32,1,128]{2,1,0:T(1,128)} %bitcast.82), calls=%async_computation.2 | async-start | bytes 32768 | tf_op jit(solution)/shard_map/all_to_all | solution.py:435
  356.3 1.8 collective-permute-start.53
  358.2 2.4 collective-permute-start.54
  366.0 6.1 %collective-permute-done.54 = bf16[96,768]{1,0:T(8,128)(2,1)S(1)} collective-permute-done((bf16[96,768]{1,0:T(8,128)(2,1)S(1)}, bf16[96,768]{1,0:T(8,128)(2,1)S(1)}, u32[]{:S(2)}, u32[]{:S(2)}) %collective-permute-start.54) | collective-permute-done | bytes 147488 | tf_op jit(solution)/shard_map/ppermute | solution.py:493
  (318 shorter events, 96.1 us)
Async XLA Ops:
  3.2 10.1 %collective-permute-start = (bf16[96,768]{1,0:T(8,128)(2,1)S(1)}, bf16[96,768]{1,0:T(8,128)(2,1)S(1)}, u32[]{:S(2)}, u32[]{:S(2)}) collective-permute-start(bf16[96,768]{1,0:T(8,128)(2,1)S(1)} %pad_maximum_fusion.15), channel_id=1, source_target_pairs={{0,1},{1,0},{2,3},{3,2},{4,5},{5,4},{6,7},{7,6},{8,9},{9,8},{10,11... | collective-permute-start | bytes 442376 | tf_op jit(solution)/shard_map/ppermute | solution.py:493
  6.3 14.0 %collective-permute-start.1 = (bf16[96,768]{1,0:T(8,128)(2,1)S(1)}, bf16[96,768]{1,0:T(8,128)(2,1)S(1)}, u32[]{:S(2)}, u32[]{:S(2)}) collective-permute-start(bf16[96,768]{1,0:T(8,128)(2,1)S(1)} %pad_maximum_fusion.15), channel_id=1, source_target_pairs={{0,2},{1,3},{2,0},{3,1},{4,6},{5,7},{6,4},{7,5},{8,10},{9,11},{10,... | collective-permute-start | bytes 442376 | tf_op jit(solution)/shard_map/ppermute | solution.py:493
  8.9 11.4 %collective-permute-start.2 = (bf16[96,768]{1,0:T(8,128)(2,1)S(1)}, bf16[96,768]{1,0:T(8,128)(2,1)S(1)}, u32[]{:S(2)}, u32[]{:S(2)}) collective-permute-start(bf16[96,768]{1,0:T(8,128)(2,1)S(1)} %pad_maximum_fusion.15), channel_id=1, source_target_pairs={{0,3},{1,2},{2,1},{3,0},{4,7},{5,6},{6,5},{7,4},{8,11},{9,10},{10,... | collective-permute-start | bytes 442376 | tf_op jit(solution)/shard_map/ppermute | solution.py:493
  21.5 18.7 %all-to-all-start = ((bf16[32,55,128]{2,1,0:T(8,128)(2,1)}), bf16[32,55,128]{2,1,0:T(8,128)(2,1)S(1)}, u32[]{:S(2)}, u32[]{:S(2)}) async-start(bf16[32,55,128]{2,1,0:T(8,128)(2,1)} %reshape.190), calls=%async_computation | async-start | bytes 917504 | tf_op jit(solution)/shard_map/all_to_all | solution.py:435
  27.1 23.7 %collective-permute-start.3 = (bf16[4,96,768]{2,1,0:T(8,128)(2,1)S(1)}, bf16[4,96,768]{2,1,0:T(8,128)(2,1)S(1)}, u32[]{:S(2)}, u32[]{:S(2)}) collective-permute-start(bf16[4,96,768]{2,1,0:T(8,128)(2,1)S(1)} %get-tuple-element.265), channel_id=1, source_target_pairs={{0,8},{1,9},{2,10},{3,11},{4,12},{5,13},{6,14},{7,15},{8,0},{9,1},... | collective-permute-start | bytes 1769480 | tf_op jit(solution)/shard_map/ppermute | solution.py:493
  28.9 21.8 %collective-permute-start.4 = (bf16[4,96,768]{2,1,0:T(8,128)(2,1)S(1)}, bf16[4,96,768]{2,1,0:T(8,128)(2,1)S(1)}, u32[]{:S(2)}, u32[]{:S(2)}) collective-permute-start(bf16[4,96,768]{2,1,0:T(8,128)(2,1)S(1)} %get-tuple-element.265), channel_id=1, source_target_pairs={{0,16},{1,17},{2,18},{3,19},{4,20},{5,21},{6,22},{7,23},{8,24},{9,... | collective-permute-start | bytes 1769480 | tf_op jit(solution)/shard_map/ppermute | solution.py:493
  30.4 12.8 %collective-permute-start.5 = (bf16[96,768]{1,0:T(8,128)(2,1)}, bf16[96,768]{1,0:T(8,128)(2,1)}, u32[]{:S(2)}, u32[]{:S(2)}) collective-permute-start(bf16[96,768]{1,0:T(8,128)(2,1)} %param.21), channel_id=1, source_target_pairs={{0,1},{1,0},{2,3},{3,2},{4,5},{5,4},{6,7},{7,6},{8,9},{9,8},{10,11... | collective-permute-start | bytes 442376 | tf_op jit(solution)/shard_map/ppermute | solution.py:493
  31.8 18.9 %collective-permute-start.6 = (bf16[96,768]{1,0:T(8,128)(2,1)}, bf16[96,768]{1,0:T(8,128)(2,1)}, u32[]{:S(2)}, u32[]{:S(2)}) collective-permute-start(bf16[96,768]{1,0:T(8,128)(2,1)} %param.21), channel_id=1, source_target_pairs={{0,2},{1,3},{2,0},{3,1},{4,6},{5,7},{6,4},{7,5},{8,10},{9,11},{10,... | collective-permute-start | bytes 442376 | tf_op jit(solution)/shard_map/ppermute | solution.py:493
  34.3 16.4 %collective-permute-start.7 = (bf16[96,768]{1,0:T(8,128)(2,1)}, bf16[96,768]{1,0:T(8,128)(2,1)}, u32[]{:S(2)}, u32[]{:S(2)}) collective-permute-start(bf16[96,768]{1,0:T(8,128)(2,1)} %param.21), channel_id=1, source_target_pairs={{0,3},{1,2},{2,1},{3,0},{4,7},{5,6},{6,5},{7,4},{8,11},{9,10},{10,... | collective-permute-start | bytes 442376 | tf_op jit(solution)/shard_map/ppermute | solution.py:493
  54.3 27.5 %collective-permute-start.10 = (bf16[4,96,768]{2,1,0:T(8,128)(2,1)}, bf16[4,96,768]{2,1,0:T(8,128)(2,1)S(1)}, u32[]{:S(2)}, u32[]{:S(2)}) collective-permute-start(bf16[4,96,768]{2,1,0:T(8,128)(2,1)} %get-tuple-element.279), channel_id=1, source_target_pairs={{0,8},{1,9},{2,10},{3,11},{4,12},{5,13},{6,14},{7,15},{8,0},{9,1},... | collective-permute-start | bytes 1769480 | tf_op jit(solution)/shard_map/ppermute | solution.py:493
  55.8 26.0 %collective-permute-start.11 = (bf16[4,96,768]{2,1,0:T(8,128)(2,1)}, bf16[4,96,768]{2,1,0:T(8,128)(2,1)S(1)}, u32[]{:S(2)}, u32[]{:S(2)}) collective-permute-start(bf16[4,96,768]{2,1,0:T(8,128)(2,1)} %get-tuple-element.279), channel_id=1, source_target_pairs={{0,16},{1,17},{2,18},{3,19},{4,20},{5,21},{6,22},{7,23},{8,24},{9,... | collective-permute-start | bytes 1769480 | tf_op jit(solution)/shard_map/ppermute | solution.py:493
  60.5 21.3 %collective-permute-start.8 = (bf16[2,96,768]{2,1,0:T(8,128)(2,1)}, bf16[2,96,768]{2,1,0:T(8,128)(2,1)S(1)}, u32[]{:S(2)}, u32[]{:S(2)}) collective-permute-start(bf16[2,96,768]{2,1,0:T(8,128)(2,1)} %slice.363), channel_id=1, source_target_pairs={{0,16},{1,17},{2,18},{3,19},{4,20},{5,21},{6,22},{7,23},{8,24},{9,... | collective-permute-start | bytes 884744 | tf_op jit(solution)/shard_map/ppermute | solution.py:493
  65.1 16.7 %collective-permute-start.9 = (bf16[2,96,768]{2,1,0:T(8,128)(2,1)}, bf16[2,96,768]{2,1,0:T(8,128)(2,1)}, u32[]{:S(2)}, u32[]{:S(2)}) collective-permute-start(bf16[2,96,768]{2,1,0:T(8,128)(2,1)} %slice.364), channel_id=1, source_target_pairs={{0,8},{1,9},{2,10},{3,11},{4,12},{5,13},{6,14},{7,15},{8,0},{9,1},... | collective-permute-start | bytes 884744 | tf_op jit(solution)/shard_map/ppermute | solution.py:493
  69.4 12.4 %collective-permute-start.14 = (bf16[96,768]{1,0:T(8,128)(2,1)}, bf16[96,768]{1,0:T(8,128)(2,1)}, u32[]{:S(2)}, u32[]{:S(2)}) collective-permute-start(bf16[96,768]{1,0:T(8,128)(2,1)} %bitcast), channel_id=1, source_target_pairs={{0,3},{1,2},{2,1},{3,0},{4,7},{5,6},{6,5},{7,4},{8,11},{9,10},{10,... | collective-permute-start | bytes 442376 | tf_op jit(solution)/shard_map/ppermute | solution.py:493
  85.7 10.2 %collective-permute-start.15 = (bf16[4,4,96,768]{3,2,1,0:T(8,128)(2,1)S(1)}, bf16[4,4,96,768]{3,2,1,0:T(8,128)(2,1)}, u32[]{:S(2)}, u32[]{:S(2)}) collective-permute-start(bf16[4,4,96,768]{3,2,1,0:T(8,128)(2,1)S(1)} %pad_maximum_fusion.own), channel_id=1, source_target_pairs={{0,4},{1,5},{2,6},{3,7},{4,0},{5,1},{6,2},{7,3},{8,12},{9,13},{10,... | collective-permute-start | bytes 7077896 | tf_op jit(solution)/shard_map/ppermute | solution.py:493
  85.8 9.7 %collective-permute-start.16 = (bf16[2,96,768]{2,1,0:T(8,128)(2,1)}, bf16[2,96,768]{2,1,0:T(8,128)(2,1)}, u32[]{:S(2)}, u32[]{:S(2)}) collective-permute-start(bf16[2,96,768]{2,1,0:T(8,128)(2,1)} %slice.367), channel_id=1, source_target_pairs={{0,16},{1,17},{2,18},{3,19},{4,20},{5,21},{6,22},{7,23},{8,24},{9,... | collective-permute-start | bytes 884744 | tf_op jit(solution)/shard_map/ppermute | solution.py:493
  96.0 19.4 %collective-permute-start.18 = (bf16[4,96,768]{2,1,0:T(8,128)(2,1)}, bf16[4,96,768]{2,1,0:T(8,128)(2,1)S(1)}, u32[]{:S(2)}, u32[]{:S(2)}) collective-permute-start(bf16[4,96,768]{2,1,0:T(8,128)(2,1)} %get-tuple-element.298), channel_id=1, source_target_pairs={{0,8},{1,9},{2,10},{3,11},{4,12},{5,13},{6,14},{7,15},{8,0},{9,1},... | collective-permute-start | bytes 1769480 | tf_op jit(solution)/shard_map/ppermute | solution.py:493
  96.5 18.9 %collective-permute-start.19 = (bf16[4,96,768]{2,1,0:T(8,128)(2,1)}, bf16[4,96,768]{2,1,0:T(8,128)(2,1)}, u32[]{:S(2)}, u32[]{:S(2)}) collective-permute-start(bf16[4,96,768]{2,1,0:T(8,128)(2,1)} %get-tuple-element.298), channel_id=1, source_target_pairs={{0,16},{1,17},{2,18},{3,19},{4,20},{5,21},{6,22},{7,23},{8,24},{9,... | collective-permute-start | bytes 1769480 | tf_op jit(solution)/shard_map/ppermute | solution.py:493
  116.6 10.5 %collective-permute-start.20 = (bf16[4,4,96,768]{3,2,1,0:T(8,128)(2,1)S(1)}, bf16[4,4,96,768]{3,2,1,0:T(8,128)(2,1)S(1)}, u32[]{:S(2)}, u32[]{:S(2)}) collective-permute-start(bf16[4,4,96,768]{3,2,1,0:T(8,128)(2,1)S(1)} %pad_maximum_fusion.1.refs_6_), channel_id=1, source_target_pairs={{0,4},{1,5},{2,6},{3,7},{4,0},{5,1},{6,2},{7,3},{8,12},{9,13},{10,... | collective-permute-start | bytes 7077896 | tf_op jit(solution)/shard_map/ppermute | solution.py:493
  116.7 10.4 %collective-permute-start.21 = (bf16[2,96,768]{2,1,0:T(8,128)(2,1)S(1)}, bf16[2,96,768]{2,1,0:T(8,128)(2,1)S(1)}, u32[]{:S(2)}, u32[]{:S(2)}) collective-permute-start(bf16[2,96,768]{2,1,0:T(8,128)(2,1)S(1)} %slice.369), channel_id=1, source_target_pairs={{0,16},{1,17},{2,18},{3,19},{4,20},{5,21},{6,22},{7,23},{8,24},{9,... | collective-permute-start | bytes 884744 | tf_op jit(solution)/shard_map/ppermute | solution.py:493
  117.3 9.8 %collective-permute-start.22 = (bf16[2,96,768]{2,1,0:T(8,128)(2,1)S(1)}, bf16[2,96,768]{2,1,0:T(8,128)(2,1)S(1)}, u32[]{:S(2)}, u32[]{:S(2)}) collective-permute-start(bf16[2,96,768]{2,1,0:T(8,128)(2,1)S(1)} %slice.370), channel_id=1, source_target_pairs={{0,8},{1,9},{2,10},{3,11},{4,12},{5,13},{6,14},{7,15},{8,0},{9,1},... | collective-permute-start | bytes 884744 | tf_op jit(solution)/shard_map/ppermute | solution.py:493
  129.1 11.1 %collective-permute-start.23 = (bf16[4,4,96,768]{3,2,1,0:T(8,128)(2,1)S(1)}, bf16[4,4,96,768]{3,2,1,0:T(8,128)(2,1)}, u32[]{:S(2)}, u32[]{:S(2)}) collective-permute-start(bf16[4,4,96,768]{3,2,1,0:T(8,128)(2,1)S(1)} %pad_maximum_fusion.2.refs_9_), channel_id=1, source_target_pairs={{0,4},{1,5},{2,6},{3,7},{4,0},{5,1},{6,2},{7,3},{8,12},{9,13},{10,... | collective-permute-start | bytes 7077896 | tf_op jit(solution)/shard_map/ppermute | solution.py:493
  193.8 16.3 %collective-permute-start.27 = (bf16[4,4,96,768]{3,2,1,0:T(8,128)(2,1)}, bf16[4,4,96,768]{3,2,1,0:T(8,128)(2,1)S(1)}, u32[]{:S(2)}, u32[]{:S(2)}) collective-permute-start(bf16[4,4,96,768]{3,2,1,0:T(8,128)(2,1)} %get-tuple-element.369), channel_id=1, source_target_pairs={{0,4},{1,5},{2,6},{3,7},{4,0},{5,1},{6,2},{7,3},{8,12},{9,13},{10,... | collective-permute-start | bytes 7077896 | tf_op jit(solution)/shard_map/ppermute | solution.py:493
  193.9 15.9 %collective-permute-start.25 = (bf16[4,96,768]{2,1,0:T(8,128)(2,1)}, bf16[4,96,768]{2,1,0:T(8,128)(2,1)S(1)}, u32[]{:S(2)}, u32[]{:S(2)}) collective-permute-start(bf16[4,96,768]{2,1,0:T(8,128)(2,1)} %get-tuple-element.367), channel_id=1, source_target_pairs={{0,8},{1,9},{2,10},{3,11},{4,12},{5,13},{6,14},{7,15},{8,0},{9,1},... | collective-permute-start | bytes 1769480 | tf_op jit(solution)/shard_map/ppermute | solution.py:493
  194.6 15.5 %collective-permute-start.26 = (bf16[4,96,768]{2,1,0:T(8,128)(2,1)}, bf16[4,96,768]{2,1,0:T(8,128)(2,1)S(1)}, u32[]{:S(2)}, u32[]{:S(2)}) collective-permute-start(bf16[4,96,768]{2,1,0:T(8,128)(2,1)} %get-tuple-element.368), channel_id=1, source_target_pairs={{0,16},{1,17},{2,18},{3,19},{4,20},{5,21},{6,22},{7,23},{8,24},{9,... | collective-permute-start | bytes 1769480 | tf_op jit(solution)/shard_map/ppermute | solution.py:493
  219.8 22.2 %collective-permute-start.30 = (bf16[4,96,768]{2,1,0:T(8,128)(2,1)}, bf16[4,96,768]{2,1,0:T(8,128)(2,1)S(1)}, u32[]{:S(2)}, u32[]{:S(2)}) collective-permute-start(bf16[4,96,768]{2,1,0:T(8,128)(2,1)} %pad_maximum_fusion.10), channel_id=1, source_target_pairs={{0,8},{1,9},{2,10},{3,11},{4,12},{5,13},{6,14},{7,15},{8,0},{9,1},... | collective-permute-start | bytes 1769480 | tf_op jit(solution)/shard_map/ppermute | solution.py:493
  221.1 20.8 %collective-permute-start.31 = (bf16[4,96,768]{2,1,0:T(8,128)(2,1)}, bf16[4,96,768]{2,1,0:T(8,128)(2,1)S(1)}, u32[]{:S(2)}, u32[]{:S(2)}) collective-permute-start(bf16[4,96,768]{2,1,0:T(8,128)(2,1)} %pad_maximum_fusion.11), channel_id=1, source_target_pairs={{0,16},{1,17},{2,18},{3,19},{4,20},{5,21},{6,22},{7,23},{8,24},{9,... | collective-permute-start | bytes 1769480 | tf_op jit(solution)/shard_map/ppermute | solution.py:493
  223.2 18.8 %collective-permute-start.28 = (bf16[2,96,768]{2,1,0:T(8,128)(2,1)}, bf16[2,96,768]{2,1,0:T(8,128)(2,1)S(1)}, u32[]{:S(2)}, u32[]{:S(2)}) collective-permute-start(bf16[2,96,768]{2,1,0:T(8,128)(2,1)} %get-tuple-element.388), channel_id=1, source_target_pairs={{0,16},{1,17},{2,18},{3,19},{4,20},{5,21},{6,22},{7,23},{8,24},{9,... | collective-permute-start | bytes 884744 | tf_op jit(solution)/shard_map/ppermute | solution.py:493
  223.9 18.1 %collective-permute-start.29 = (bf16[2,96,768]{2,1,0:T(8,128)(2,1)}, bf16[2,96,768]{2,1,0:T(8,128)(2,1)S(1)}, u32[]{:S(2)}, u32[]{:S(2)}) collective-permute-start(bf16[2,96,768]{2,1,0:T(8,128)(2,1)} %get-tuple-element.389), channel_id=1, source_target_pairs={{0,8},{1,9},{2,10},{3,11},{4,12},{5,13},{6,14},{7,15},{8,0},{9,1},... | collective-permute-start | bytes 884744 | tf_op jit(solution)/shard_map/ppermute | solution.py:493
  247.8 20.4 %collective-permute-start.35 = (bf16[2,96,768]{2,1,0:T(8,128)(2,1)S(1)}, bf16[2,96,768]{2,1,0:T(8,128)(2,1)S(1)}, u32[]{:S(2)}, u32[]{:S(2)}) collective-permute-start(bf16[2,96,768]{2,1,0:T(8,128)(2,1)S(1)} %get-tuple-element.416), channel_id=1, source_target_pairs={{0,16},{1,17},{2,18},{3,19},{4,20},{5,21},{6,22},{7,23},{8,24},{9,... | collective-permute-start | bytes 884744 | tf_op jit(solution)/shard_map/ppermute | solution.py:493
  249.3 18.9 %collective-permute-start.36 = (bf16[2,96,768]{2,1,0:T(8,128)(2,1)S(1)}, bf16[2,96,768]{2,1,0:T(8,128)(2,1)S(1)}, u32[]{:S(2)}, u32[]{:S(2)}) collective-permute-start(bf16[2,96,768]{2,1,0:T(8,128)(2,1)S(1)} %get-tuple-element.417), channel_id=1, source_target_pairs={{0,8},{1,9},{2,10},{3,11},{4,12},{5,13},{6,14},{7,15},{8,0},{9,1},... | collective-permute-start | bytes 884744 | tf_op jit(solution)/shard_map/ppermute | solution.py:493
  250.1 17.8 %collective-permute-start.32 = (bf16[96,768]{1,0:T(8,128)(2,1)S(1)}, bf16[96,768]{1,0:T(8,128)(2,1)S(1)}, u32[]{:S(2)}, u32[]{:S(2)}) collective-permute-start(bf16[96,768]{1,0:T(8,128)(2,1)S(1)} %fusion.25), channel_id=1, source_target_pairs={{0,1},{1,0},{2,3},{3,2},{4,5},{5,4},{6,7},{7,6},{8,9},{9,8},{10,11... | collective-permute-start | bytes 442376 | tf_op jit(solution)/shard_map/ppermute | solution.py:493
  250.4 17.5 %collective-permute-start.33 = (bf16[96,768]{1,0:T(8,128)(2,1)S(1)}, bf16[96,768]{1,0:T(8,128)(2,1)S(1)}, u32[]{:S(2)}, u32[]{:S(2)}) collective-permute-start(bf16[96,768]{1,0:T(8,128)(2,1)S(1)} %get-tuple-element.414), channel_id=1, source_target_pairs={{0,2},{1,3},{2,0},{3,1},{4,6},{5,7},{6,4},{7,5},{8,10},{9,11},{10,... | collective-permute-start | bytes 442376 | tf_op jit(solution)/shard_map/ppermute | solution.py:493
  251.7 16.3 %collective-permute-start.34 = (bf16[96,768]{1,0:T(8,128)(2,1)S(1)}, bf16[96,768]{1,0:T(8,128)(2,1)S(1)}, u32[]{:S(2)}, u32[]{:S(2)}) collective-permute-start(bf16[96,768]{1,0:T(8,128)(2,1)S(1)} %get-tuple-element.415), channel_id=1, source_target_pairs={{0,3},{1,2},{2,1},{3,0},{4,7},{5,6},{6,5},{7,4},{8,11},{9,10},{10,... | collective-permute-start | bytes 442376 | tf_op jit(solution)/shard_map/ppermute | solution.py:493
  272.3 23.1 %collective-permute-start.37 = (bf16[96,768]{1,0:T(8,128)(2,1)S(1)}, bf16[96,768]{1,0:T(8,128)(2,1)S(1)}, u32[]{:S(2)}, u32[]{:S(2)}) collective-permute-start(bf16[96,768]{1,0:T(8,128)(2,1)S(1)} %fusion.26), channel_id=1, source_target_pairs={{0,1},{1,0},{2,3},{3,2},{4,5},{5,4},{6,7},{7,6},{8,9},{9,8},{10,11... | collective-permute-start | bytes 442376 | tf_op jit(solution)/shard_map/ppermute | solution.py:493
  272.3 23.0 %collective-permute-start.38 = (bf16[96,768]{1,0:T(8,128)(2,1)S(1)}, bf16[96,768]{1,0:T(8,128)(2,1)S(1)}, u32[]{:S(2)}, u32[]{:S(2)}) collective-permute-start(bf16[96,768]{1,0:T(8,128)(2,1)S(1)} %get-tuple-element.444), channel_id=1, source_target_pairs={{0,2},{1,3},{2,0},{3,1},{4,6},{5,7},{6,4},{7,5},{8,10},{9,11},{10,... | collective-permute-start | bytes 442376 | tf_op jit(solution)/shard_map/ppermute | solution.py:493
  273.9 21.5 %collective-permute-start.39 = (bf16[96,768]{1,0:T(8,128)(2,1)S(1)}, bf16[96,768]{1,0:T(8,128)(2,1)S(1)}, u32[]{:S(2)}, u32[]{:S(2)}) collective-permute-start(bf16[96,768]{1,0:T(8,128)(2,1)S(1)} %get-tuple-element.445), channel_id=1, source_target_pairs={{0,3},{1,2},{2,1},{3,0},{4,7},{5,6},{6,5},{7,4},{8,11},{9,10},{10,... | collective-permute-start | bytes 442376 | tf_op jit(solution)/shard_map/ppermute | solution.py:493
  276.7 12.8 %collective-permute-start.40 = (bf16[160,128]{1,0:T(8,128)(2,1)S(1)}, bf16[160,128]{1,0:T(8,128)(2,1)S(1)}, u32[]{:S(2)}, u32[]{:S(2)}) collective-permute-start(bf16[160,128]{1,0:T(8,128)(2,1)S(1)} %fusion.32), channel_id=1, source_target_pairs={{0,1},{1,0},{2,3},{3,2},{4,5},{5,4},{6,7},{7,6},{8,9},{9,8},{10,11... | collective-permute-start | bytes 122888 | tf_op jit(solution)/shard_map/ppermute | solution.py:493
  276.7 15.6 %collective-permute-start.41 = (bf16[160,128]{1,0:T(8,128)(2,1)S(1)}, bf16[160,128]{1,0:T(8,128)(2,1)S(1)}, u32[]{:S(2)}, u32[]{:S(2)}) collective-permute-start(bf16[160,128]{1,0:T(8,128)(2,1)S(1)} %fusion.32), channel_id=1, source_target_pairs={{0,2},{1,3},{2,0},{3,1},{4,6},{5,7},{6,4},{7,5},{8,10},{9,11},{10,... | collective-permute-start | bytes 122888 | tf_op jit(solution)/shard_map/ppermute | solution.py:493
  308.6 16.9 %collective-permute-start.46 = (bf16[4,96,768]{2,1,0:T(8,128)(2,1)S(1)}, bf16[4,96,768]{2,1,0:T(8,128)(2,1)S(1)}, u32[]{:S(2)}, u32[]{:S(2)}) collective-permute-start(bf16[4,96,768]{2,1,0:T(8,128)(2,1)S(1)} %pad_maximum_fusion.12), channel_id=1, source_target_pairs={{0,8},{1,9},{2,10},{3,11},{4,12},{5,13},{6,14},{7,15},{8,0},{9,1},... | collective-permute-start | bytes 1769480 | tf_op jit(solution)/shard_map/ppermute | solution.py:493
  309.5 16.7 %collective-permute-start.47 = (bf16[4,96,768]{2,1,0:T(8,128)(2,1)S(1)}, bf16[4,96,768]{2,1,0:T(8,128)(2,1)S(1)}, u32[]{:S(2)}, u32[]{:S(2)}) collective-permute-start(bf16[4,96,768]{2,1,0:T(8,128)(2,1)S(1)} %pad_maximum_fusion.13), channel_id=1, source_target_pairs={{0,16},{1,17},{2,18},{3,19},{4,20},{5,21},{6,22},{7,23},{8,24},{9,... | collective-permute-start | bytes 1769480 | tf_op jit(solution)/shard_map/ppermute | solution.py:493
  310.2 15.4 %collective-permute-start.48 = (bf16[2,160,128]{2,1,0:T(8,128)(2,1)S(1)}, bf16[2,160,128]{2,1,0:T(8,128)(2,1)S(1)}, u32[]{:S(2)}, u32[]{:S(2)}) collective-permute-start(bf16[2,160,128]{2,1,0:T(8,128)(2,1)S(1)} %slice.429), channel_id=1, source_target_pairs={{0,16},{1,17},{2,18},{3,19},{4,20},{5,21},{6,22},{7,23},{8,24},{9,... | collective-permute-start | bytes 245768 | tf_op jit(solution)/shard_map/ppermute | solution.py:493
  311.6 13.9 %collective-permute-start.49 = (bf16[2,160,128]{2,1,0:T(8,128)(2,1)S(1)}, bf16[2,160,128]{2,1,0:T(8,128)(2,1)S(1)}, u32[]{:S(2)}, u32[]{:S(2)}) collective-permute-start(bf16[2,160,128]{2,1,0:T(8,128)(2,1)S(1)} %slice.430), channel_id=1, source_target_pairs={{0,8},{1,9},{2,10},{3,11},{4,12},{5,13},{6,14},{7,15},{8,0},{9,1},... | collective-permute-start | bytes 245768 | tf_op jit(solution)/shard_map/ppermute | solution.py:493
  330.8 11.0 %collective-permute-start.52 = (bf16[4,4,160,128]{3,2,1,0:T(8,128)(2,1)}, bf16[4,4,160,128]{3,2,1,0:T(8,128)(2,1)}, u32[]{:S(2)}, u32[]{:S(2)}) collective-permute-start(bf16[4,4,160,128]{3,2,1,0:T(8,128)(2,1)} %get-tuple-element.476), channel_id=1, source_target_pairs={{0,4},{1,5},{2,6},{3,7},{4,0},{5,1},{6,2},{7,3},{8,12},{9,13},{10,... | collective-permute-start | bytes 1966088 | tf_op jit(solution)/shard_map/ppermute | solution.py:493
  331.8 9.7 %collective-permute-start.50 = (bf16[2,96,768]{2,1,0:T(8,128)(2,1)}, bf16[2,96,768]{2,1,0:T(8,128)(2,1)S(1)}, u32[]{:S(2)}, u32[]{:S(2)}) collective-permute-start(bf16[2,96,768]{2,1,0:T(8,128)(2,1)} %get-tuple-element.474), channel_id=1, source_target_pairs={{0,16},{1,17},{2,18},{3,19},{4,20},{5,21},{6,22},{7,23},{8,24},{9,... | collective-permute-start | bytes 884744 | tf_op jit(solution)/shard_map/ppermute | solution.py:493
  351.7 14.2 %all-to-all-start.2 = ((f32[32,1,128]{2,1,0:T(1,128)}), f32[32,1,128]{2,1,0:T(1,128)S(1)}, u32[]{:S(2)}, u32[]{:S(2)}) async-start(f32[32,1,128]{2,1,0:T(1,128)} %bitcast.82), calls=%async_computation.2 | async-start | bytes 32768 | tf_op jit(solution)/shard_map/all_to_all | solution.py:435
  358.2 13.9 %collective-permute-start.54 = (bf16[96,768]{1,0:T(8,128)(2,1)S(1)}, bf16[96,768]{1,0:T(8,128)(2,1)S(1)}, u32[]{:S(2)}, u32[]{:S(2)}) collective-permute-start(bf16[96,768]{1,0:T(8,128)(2,1)S(1)} %get-tuple-element.481), channel_id=1, source_target_pairs={{0,2},{1,3},{2,0},{3,1},{4,6},{5,7},{6,4},{7,5},{8,10},{9,11},{10,... | collective-permute-start | bytes 442376 | tf_op jit(solution)/shard_map/ppermute | solution.py:493
  360.6 11.5 %collective-permute-start.55 = (bf16[96,768]{1,0:T(8,128)(2,1)S(1)}, bf16[96,768]{1,0:T(8,128)(2,1)S(1)}, u32[]{:S(2)}, u32[]{:S(2)}) collective-permute-start(bf16[96,768]{1,0:T(8,128)(2,1)S(1)} %get-tuple-element.482), channel_id=1, source_target_pairs={{0,3},{1,2},{2,1},{3,0},{4,7},{5,6},{6,5},{7,4},{8,11},{9,10},{10,... | collective-permute-start | bytes 442376 | tf_op jit(solution)/shard_map/ppermute | solution.py:493
  (60 other events, 448.6 us)

commit v4 on v3

--- a/solution.py
+++ b/solution.py
@@ -344,7 +344,7 @@
         low = grad[2 * pair * slab : (2 * pair + 1) * slab]
         high = grad[(2 * pair + 1) * slab : (2 * pair + 2) * slab]
         slot = jnp.bitwise_xor(pair, flip)
-        keep_ref[slot, 0, :, lanes] = jnp.where(core == 0, low, high)
+        keep_ref[slot, 0, :, lanes] = jnp.where(core == 0, low, high).astype(BF16)
         send_ref[slot, 0, :, lanes] = jnp.where(core == 0, high, low).astype(BF16)
 
 
@@ -517,9 +517,15 @@
         (other,) = yield [(own, across)]
         return own, other
 
+    def vector_stages(row):
+        line = yield [(row, mask) for mask in range(1, tensor_size)]
+        line = jnp.stack([row] + line)
+        near = yield [(line, along), (line, upward), (line, along + upward)]
+        return jnp.stack([line] + near)
+
     def reduce_stages(keep, send):
         (arrived,) = yield [(send, across)]
-        summed = keep + arrived.astype(F32)
+        summed = keep.astype(F32) + arrived.astype(F32)
         line, side, above, far = [summed[number] for number in range(4)]
         moved = [
             jnp.concatenate(pair).astype(BF16)
@@ -573,6 +579,11 @@
     for size in (ada_rows * latents, latents * D, 2 * head_width):
         ends.append(ends[-1] + size)
 
+    def modulate(columns):
+        back = lax.all_to_all(columns, axes, 0, 0, tiled=True)
+        back = back.reshape(count, -1)[:, : latents * ada_cols]
+        return back.reshape(count, latents, ada_cols).transpose(1, 0, 2).reshape(latents, 6, D)
+
     def opened(slots):
         got = exchange(slots, axes)
         columns = jnp.dot(
@@ -581,14 +592,10 @@
             preferred_element_type=F32,
         )
         columns = columns + ada_bias.astype(F32)
-        return got, jnp.pad(
+        columns = jnp.pad(
             columns.reshape(count, latents * ada_cols), ((0, 0), (0, -latents * ada_cols % 128))
         ).reshape(count, -1, 128)
-
-    def modulate(columns):
-        back = lax.all_to_all(columns, axes, 0, 0, tiled=True)
-        back = back.reshape(count, -1)[:, : latents * ada_cols]
-        return back.reshape(count, latents, ada_cols).transpose(1, 0, 2).reshape(latents, 6, D)
+        return got, modulate(columns)
 
     heads_in = hidden_in = down_in = None
     if direct:
@@ -601,14 +608,12 @@
             )
         ]
     sent = slot([heads_in] if direct else [], (ada_weight, silu_cond), packed_slots)
-    got, columns = slot([heads_in, hidden_in] if direct else [], (sent,), opened)
+    got, modulation = slot([heads_in, hidden_in] if direct else [], (sent,), opened)
     silu_columns = got[:, ends[0] : ends[1]].reshape(count * latents, ada_rows)
     qv_full = got[:tensor_size, ends[2] : ends[3]].reshape(tensor_size, 2, head_width)
     hidden_bias_full = got[:tensor_size, ends[3] :]
-    modulation = slot(
-        [heads_in, hidden_in, down_in] if direct else [], (columns,), modulate
-    )
     if direct:
+        slot([heads_in, hidden_in, down_in], (), lambda: ())
         slot([heads_in, hidden_in], (), lambda: ())
     else:
         qkv_full = gathered(qkv_weight)
@@ -701,7 +706,7 @@
     )
 
     split_shape = (dp_size // 2, tensor_size, slab, D)
-    split_out = [(to_second, split_shape, F32), (to_second, split_shape, BF16)]
+    split_out = [(to_second, split_shape, BF16), (to_second, split_shape, BF16)]
 
     def square_grad(left, right):
         return placed_call(
@@ -801,7 +806,7 @@
             qkv_sums = qkv_sums + own_sums
         qkv_grad, input_grad, early_pieces = carried
         shared_in = Flow(
-            gather_stages(vectors(early_pieces, late_pieces, late_sums, qkv_sums))
+            vector_stages(vectors(early_pieces, late_pieces, late_sums, qkv_sums))
         )
         flows = [flow for flow in (down_out, hidden_out) if flow.value is None]
         heads_out = Flow(
@@ -811,13 +816,17 @@
                 )
             )
         )
-        for _ in range(3):
-            slot([heads_out, shared_in], (), lambda: ())
-        shared = jnp.stack(shared_in.value).reshape(count, -1, 128)
-        silu_grad, ada_weight_grad = slot(
-            [heads_out], (shared, silu_columns, to_owner), ada_back
-        )
-        condition_grad = condition_back(silu_grad)
+        slot([heads_out, shared_in], (), lambda: ())
+
+        def finish_vectors(own, columns, order):
+            both = jnp.stack([own, swap(own, across)]).reshape(count, -1, 128)
+            return both, ada_back(both, columns, order)
+
+        shared, (silu_grad, ada_weight_grad) = slot(
+            [heads_out], (shared_in.value, silu_columns, to_owner), finish_vectors
+        )
+        condition_grad = slot([heads_out], (silu_grad,), condition_back)
+        slot([heads_out], (), lambda: ())
         down_weight_grad, hidden_weight_grad = down_out.value.T, hidden_out.value
         packed_grad = heads_out.value.reshape(slab, 4, head_width)
         qkv_weight_grad = packed_grad[:, :3].swapaxes(0, 1)

time: 382 us -> 372 us (0.974)
  waiting for transfers between devices: 70.1 us -> 58.4 us
    ppermute x56 -> x55, waiting for transfers between devices: 64.6 us -> 46.9 us  [swap(): lax.ppermute(array, axes, [(device, device ^ mask) for device in range(co...]
    another operation x11 -> x10, other arithmetic: 22.5 us -> 9.99 us
    add x0 -> x3, other arithmetic: none -> 11.7 us  [reduce_stages(): summed = keep.astype(F32) + arrived.astype(F32)]
    all_to_all x2, waiting for transfers between devices: 5.48 us -> 11.5 us  [exchange(): lax.all_to_all(padded, axes, 0, 0, tiled=True).reshape(count, -1)[:, :size]]
    unnamed x105 -> x109, local copies, waits for them, and re-layouts: 8.33 us -> 11 us
    another operation x11 -> x9, other arithmetic: 9.94 us -> 7.58 us  [gather_stages(): own = jnp.stack([line, side, above, jnp.concatenate([first, second])])]
    ppermute x56 -> x55, starting transfers between devices: 62.6 us -> 62.5 us  [swap(): lax.ppermute(array, axes, [(device, device ^ mask) for device in range(co...]
  transfers between devices with their start and end apart: 58 -> 57, of which waited for: 18 -> 20; matrix products, arithmetic and copies ran while one was open for 7% -> 9% of each run, Pallas kernels for 25% -> 25%
where the time goes in v4:
time: 372 us; the launch traced here: 366 us
  Pallas kernels  131 us (35%)
  starting transfers between devices  71.9 us (19%)
  waiting for transfers between devices  58.4 us (16%)
  other arithmetic  49.9 us (13%)
  local copies, waits for them, and re-layouts  35 us (9%)
  blocking collectives  13.1 us (4%)
  matrix products  4.2 us (1%)
    pallas_call x7, Pallas kernels, over_latents(): pl.pallas_call(body, grid=(steps,), in_specs=[spec(array, first) for spec...  96.2 us
    ppermute x55, starting transfers between devices, swap(): lax.ppermute(array, axes, [(device, device ^ mask) for device in range(co...  62.5 us
    ppermute x55, waiting for transfers between devices, swap(): lax.ppermute(array, axes, [(device, device ^ mask) for device in range(co...  46.9 us
    pallas_call x4, Pallas kernels, placed_call(): pl.pallas_call(kernel, grid_spec=pltpu.PrefetchScalarGridSpec(num_scalar_...  34.8 us
    all_to_all x1, blocking collectives, modulate(): back = lax.all_to_all(columns, axes, 0, 0, tiled=True)  13.1 us
    add x3, other arithmetic, reduce_stages(): summed = keep.astype(F32) + arrived.astype(F32)  11.7 us
    all_to_all x2, waiting for transfers between devices, exchange(): lax.all_to_all(padded, axes, 0, 0, tiled=True).reshape(count, -1)[:, :size]  11.5 us
    unnamed x109, local copies, waits for them, and re-layouts  11 us
  transfers between devices with their start and end apart: 57, of which 20 were waited for; matrix products, arithmetic and copies ran while one was open for 9% of the time, Pallas kernels for 25%

profile of v4, /device:TPU:0, one launch (start us, length us, event | category | flops | bytes accessed | tf_op | source)
XLA Modules:
  0.0 365.5 jit_solution(3712786593746964036)
XLA Ops:
  3.2 3.1 collective-permute-start
  6.3 2.6 collective-permute-start.1
  10.6 1.6 reshape.184
  13.3 7.0 %collective-permute-done.1 = bf16[96,768]{1,0:T(8,128)(2,1)S(1)} collective-permute-done((bf16[96,768]{1,0:T(8,128)(2,1)S(1)}, bf16[96,768]{1,0:T(8,128)(2,1)S(1)}, u32[]{:S(2)}, u32[]{:S(2)}) %collective-permute-start.1) | collective-permute-done | bytes 147488 | tf_op jit(solution)/shard_map/ppermute | solution.py:493
  21.5 5.6 %all-to-all-start = ((bf16[32,55,128]{2,1,0:T(8,128)(2,1)}), bf16[32,55,128]{2,1,0:T(8,128)(2,1)S(1)}, u32[]{:S(2)}, u32[]{:S(2)}) async-start(bf16[32,55,128]{2,1,0:T(8,128)(2,1)} %reshape.190), calls=%async_computation | async-start | bytes 917504 | tf_op jit(solution)/shard_map/all_to_all | solution.py:435
  27.1 1.8 collective-permute-start.3
  31.8 2.5 collective-permute-start.6
  34.8 5.5 %all-to-all-done = bf16[32,55,128]{2,1,0:T(8,128)(2,1)S(1)} async-done(((bf16[32,55,128]{2,1,0:T(8,128)(2,1)}), bf16[32,55,128]{2,1,0:T(8,128)(2,1)S(1)}, u32[]{:S(2)}, u32[]{:S(2)}) %all-to-all-start) | async-done | bytes 450592 | tf_op jit(solution)/shard_map/all_to_all | solution.py:435
  43.2 13.1 %all_to_all.15 = f32[32,4,128]{2,1,0:T(4,128)S(1)} all-to-all(f32[32,4,128]{2,1,0:T(4,128)S(1)} %reshape.195), channel_id=1, replica_groups=mesh['dp'=8,'tensor'=4] {'dp','tensor'}, dimensions={0} | all-to-all | bytes 131072 | tf_op jit(solution)/shard_map/all_to_all | solution.py:583
  63.8 3.7 %collective-permute-done.12 = bf16[96,768]{1,0:T(8,128)(2,1)S(1)} collective-permute-done((bf16[96,768]{1,0:T(8,128)(2,1)}, bf16[96,768]{1,0:T(8,128)(2,1)S(1)}, u32[]{:S(2)}, u32[]{:S(2)}) %collective-permute-start.12) | collective-permute-done | bytes 147488 | tf_op jit(solution)/shard_map/ppermute | solution.py:493
  67.4 1.6 collective-permute-start.9
  71.5 5.8 %collective-permute-done.14 = bf16[96,768]{1,0:T(8,128)(2,1)S(1)} collective-permute-done((bf16[96,768]{1,0:T(8,128)(2,1)}, bf16[96,768]{1,0:T(8,128)(2,1)S(1)}, u32[]{:S(2)}, u32[]{:S(2)}) %collective-permute-start.14) | collective-permute-done | bytes 147488 | tf_op jit(solution)/shard_map/ppermute | solution.py:493
  77.3 3.6 collective-permute-done.8
  88.1 2.0 fusion.58
  90.1 4.0 %collective-permute-done.16 = bf16[2,96,768]{2,1,0:T(8,128)(2,1)S(1)} collective-permute-done((bf16[2,96,768]{2,1,0:T(8,128)(2,1)}, bf16[2,96,768]{2,1,0:T(8,128)(2,1)S(1)}, u32[]{:S(2)}, u32[]{:S(2)}) %collective-permute-start.16) | collective-permute-done | bytes 294944 | tf_op jit(solution)/shard_map/ppermute | solution.py:493
  98.6 6.9 %shard_map.228 = (bf16[4,3,8,96,192]{4,3,2,1,0:T(8,128)(2,1)}, bf16[4,8,96,192]{3,2,1,0:T(8,128)(2,1)}) custom-call(s32[2]{0:T(128)} %pad_add_fusion.place.refs_12_, bf16[4,4,96,768]{3,2,1,0:T(8,128)(2,1)} %copy-done.1, bf16[4,4,96,768]{3,2,1,0:T(8,128)(2,1)} %collective-permute-done.15.other), custom_call_target="tpu_custom_call" | custom-call | bytes 9437184 | tf_op jit(solution)/shard_map/pallas_call | solution.py:369
  105.6 8.4 %shard_map.229 = (bf16[768,768]{1,0:T(8,128)(2,1)}, bf16[4,3,768,192]{3,2,1,0:T(8,128)(2,1)}, bf16[4,768,192]{2,1,0:T(8,128)(2,1)}) custom-call(bf16[768,768]{1,0:T(8,128)(2,1)} %refs_4_.2, f32[3,6,768]{2,1,0:T(8,128)} %reshape.198.refs_1_.refs_3_.refs_5_, bf16[1,4,3,768,192]{4,3,2,1,0:T(8,128)(2,1)} %bitcast.220, bf16[4,2,192]{2,1,0:T(2,128)(2,1)} %reshape.199.refs_3_), custom_call_target="tpu_custom_call" | custom-call | flops 1811939328 | bytes 10675200 | tf_op jit(solution)/shard_map/pallas_call | solution.py:283
  117.0 8.3 %shard_map.230 = (bf16[768,768]{1,0:T(8,128)(2,1)}, bf16[4,3,768,192]{3,2,1,0:T(8,128)(2,1)}, bf16[4,768,192]{2,1,0:T(8,128)(2,1)}) custom-call(bf16[768,768]{1,0:T(8,128)(2,1)} %refs_4_.2, f32[3,6,768]{2,1,0:T(8,128)} %reshape.198.refs_1_.refs_3_.refs_5_, ...), custom_call_target="tpu_custom_call", output_to_operand_aliasing={{0}: (4, {}), {1}: (5, {}), {2}: (6, {})} | custom-call | flops 1811939328 | bytes 10675200 | tf_op jit(solution)/shard_map/pallas_call | solution.py:283
  125.6 1.9 pad_maximum_fusion.2.refs_9_
  130.3 8.3 %shard_map.231 = (bf16[768,768]{1,0:T(8,128)(2,1)}, bf16[4,3,768,192]{3,2,1,0:T(8,128)(2,1)}, bf16[4,768,192]{2,1,0:T(8,128)(2,1)}) custom-call(bf16[768,768]{1,0:T(8,128)(2,1)} %refs_4_.2, f32[3,6,768]{2,1,0:T(8,128)} %reshape.198.refs_1_.refs_3_.refs_5_, ...), custom_call_target="tpu_custom_call", output_to_operand_aliasing={{0}: (4, {}), {1}: (5, {}), {2}: (6, {})} | custom-call | flops 1811939328 | bytes 10675200 | tf_op jit(solution)/shard_map/pallas_call | solution.py:283
  138.6 30.5 %shard_map.232 = (f32[768,768]{1,0:T(8,128)}, bf16[4,768,768]{2,1,0:T(8,128)(2,1)}, bf16[4,768,768]{2,1,0:T(8,128)(2,1)}, bf16[768,768]{1,0:T(8,128)(2,1)}, bf16...) custom-call(bf16[4,768,192]{2,1,0:T(8,128)(2,1)} %get-tuple-element., ...), custom_call_target="tpu_custom_call" | custom-call | flops 16307453952 | bytes 31970312 | tf_op jit(solution)/shard_map/pallas_call | solution.py:283
  169.1 8.6 %shard_map.233 = (bf16[4,4,96,768]{3,2,1,0:T(8,128)(2,1)}, bf16[4,4,96,768]{3,2,1,0:T(8,128)(2,1)}) custom-call(s32[2]{0:T(128)} %pad_add_fusion.place.refs_12_, bf16[768,768]{1,0:T(8,128)(2,1)} %get-tuple-element.346.left, bf16[4,768,768]{2,1,0:T(8,128)(2,1)} %get-tuple-element.347.right), custom_call_target="tpu_custom_call" | custom-call | flops 3623878656 | bytes 10616832 | tf_op jit(solution)/shard_map/pallas_call | solution.py:369
  178.1 8.9 %shard_map.234 = (bf16[4,4,96,768]{3,2,1,0:T(8,128)(2,1)}, bf16[4,4,96,768]{3,2,1,0:T(8,128)(2,1)}) custom-call(s32[2]{0:T(128)} %pad_add_fusion.place.refs_12_, bf16[768,768]{1,0:T(8,128)(2,1)} %get-tuple-element.353.left, bf16[4,768,768]{2,1,0:T(8,128)(2,1)} %get-tuple-element.354.right), custom_call_target="tpu_custom_call" | custom-call | flops 3623878656 | bytes 10616832 | tf_op jit(solution)/shard_map/pallas_call | solution.py:369
  188.4 2.4 convert_add_fusion.2
  195.0 13.6 %shard_map.235 = (bf16[4,3,768,192]{3,2,1,0:T(8,128)(2,1)}, f32[768,768]{1,0:T(8,128)}, f32[3,2,768]{2,1,0:T(2,128)}, f32[4,3,192]{2,1,0:T(4,128)}) custom-call(bf16[768,768]{1,0:T(8,128)(2,1)} %get-tuple-element.446.refs_0_.outer, bf16[4,3,768,192]{3,2,1,0:T(8,128)(2,1)} %get-tuple-element.414.refs_1_, bf16[1,4,768,192]{3,2,1,0:T(8,128)(2,1)} %bitcast.230, ...), custom_call_target="tpu_custom_call" | custom-call | flops 5435817984 | bytes 18957312 | tf_op jit(solution)/shard_map/pallas_call | solution.py:283
  210.9 4.7 %convert_add_fusion.1 = (f32[4,4,96,768]{3,2,1,0:T(8,128)}, bf16[4,4,96,768]{3,2,1,0:T(8,128)(2,1)S(1)}) fusion(bf16[4,4,96,768]{3,2,1,0:T(8,128)(2,1)} %copy-done.7, bf16[4,4,96,768]{3,2,1,0:T(8,128)(2,1)S(1)} %copy-done.6), kind=kLoop, calls=%fused_computation.1 | loop fusion | flops 4718592 | bytes 11796480 | tf_op jit(solution)/shard_map/add | solution.py:528
  225.1 13.6 %shard_map.236 = (bf16[4,3,768,192]{3,2,1,0:T(8,128)(2,1)}, f32[768,768]{1,0:T(8,128)}, f32[3,2,768]{2,1,0:T(2,128)}, f32[4,3,192]{2,1,0:T(4,128)}) custom-call(bf16[768,768]{1,0:T(8,128)(2,1)} %get-tuple-element.446.refs_0_.outer, bf16[4,3,768,192]{3,2,1,0:T(8,128)(2,1)} %get-tuple-element.414.refs_1_, ...), custom_call_target="tpu_custom_call", output_to_operand_aliasing={{0}: (7, {}), {1}: (8, {}), {2}: (9, {})} | custom-call | flops 5435817984 | bytes 18957312 | tf_op jit(solution)/shard_map/pallas_call | solution.py:283
  238.7 1.9 collective-permute-done.28
  246.6 2.4 collective-permute-start.34
  251.0 13.4 %shard_map.237 = (bf16[4,3,768,192]{3,2,1,0:T(8,128)(2,1)}, f32[768,768]{1,0:T(8,128)}, f32[3,2,768]{2,1,0:T(2,128)}, f32[4,3,192]{2,1,0:T(4,128)}) custom-call(bf16[768,768]{1,0:T(8,128)(2,1)} %get-tuple-element.446.refs_0_.outer, bf16[4,3,768,192]{3,2,1,0:T(8,128)(2,1)} %get-tuple-element.414.refs_1_, ...), custom_call_target="tpu_custom_call", output_to_operand_aliasing={{0}: (7, {}), {1}: (8, {}), {2}: (9, {})} | custom-call | flops 5435817984 | bytes 18957312 | tf_op jit(solution)/shard_map/pallas_call | solution.py:283
  267.1 1.6 fusion.6
  269.7 1.7 collective-permute-start.41
  271.7 2.9 collective-permute-start.38
  275.8 10.4 %shard_map.238 = (bf16[4,4,96,768]{3,2,1,0:T(8,128)(2,1)}, bf16[4,4,96,768]{3,2,1,0:T(8,128)(2,1)}) custom-call(s32[2]{0:T(128)} %pad_add_fusion.place.refs_12_, bf16[768,768]{1,0:T(8,128)(2,1)} %get-tuple-element.444.entry, bf16[4,3,768,192]{3,2,1,0:T(8,128)(2,1)} %get-tuple-element.445.qkv_grad, bf16[768,768]{1,0:T(8,128)(2,1)} %get-tuple-element.446.refs_0_.outer, ...), custom_call_target="tpu_custom_call" | custom-call | flops 3623878656 | bytes 11796480 | tf_op jit(solution)/shard_map/pallas_call | solution.py:369
  286.2 2.7 collective-permute-start.42
  288.9 3.2 collective-permute-done.42
  300.4 2.7 collective-permute-done.45
  304.2 4.6 %convert_add_fusion = (f32[4,4,96,768]{3,2,1,0:T(8,128)}, bf16[4,4,96,768]{3,2,1,0:T(8,128)(2,1)S(1)}) fusion(bf16[4,4,96,768]{3,2,1,0:T(8,128)(2,1)S(1)} %collective-permute-done.43, bf16[4,4,96,768]{3,2,1,0:T(8,128)(2,1)} %get-tuple-element.450), kind=kLoop, calls=%fused_computation | loop fusion | flops 4718592 | bytes 11796480 | tf_op jit(solution)/shard_map/add | solution.py:528
  312.8 1.7 fusion.21
  321.1 3.8 %all-to-all-start.2 = ((f32[32,1,128]{2,1,0:T(1,128)}), f32[32,1,128]{2,1,0:T(1,128)S(1)}, u32[]{:S(2)}, u32[]{:S(2)}) async-start(f32[32,1,128]{2,1,0:T(1,128)} %bitcast.76), calls=%async_computation.2 | async-start | bytes 32768 | tf_op jit(solution)/shard_map/all_to_all | solution.py:435
  325.9 6.0 %all-to-all-done.2 = f32[32,1,128]{2,1,0:T(1,128)S(1)} async-done(((f32[32,1,128]{2,1,0:T(1,128)}), f32[32,1,128]{2,1,0:T(1,128)S(1)}, u32[]{:S(2)}, u32[]{:S(2)}) %all-to-all-start.2) | async-done | bytes 16416 | tf_op jit(solution)/shard_map/all_to_all | solution.py:435
  335.8 2.1 fusion.3
  340.3 1.6 reshape.216
  341.9 1.7 reduce_sum.18
  344.5 2.4 collective-permute-done.50
  347.4 1.6 fusion.1
  349.3 3.2 collective-permute-start.53
  355.8 7.3 %collective-permute-done.53 = bf16[96,768]{1,0:T(8,128)(2,1)S(1)} collective-permute-done((bf16[96,768]{1,0:T(8,128)(2,1)S(1)}, bf16[96,768]{1,0:T(8,128)(2,1)S(1)}, u32[]{:S(2)}, u32[]{:S(2)}) %collective-permute-start.53) | collective-permute-done | bytes 147488 | tf_op jit(solution)/shard_map/ppermute | solution.py:493
  (317 shorter events, 104.9 us)
Async XLA Ops:
  3.2 10.1 %collective-permute-start = (bf16[96,768]{1,0:T(8,128)(2,1)S(1)}, bf16[96,768]{1,0:T(8,128)(2,1)S(1)}, u32[]{:S(2)}, u32[]{:S(2)}) collective-permute-start(bf16[96,768]{1,0:T(8,128)(2,1)S(1)} %pad_maximum_fusion.15), channel_id=1, source_target_pairs={{0,1},{1,0},{2,3},{3,2},{4,5},{5,4},{6,7},{7,6},{8,9},{9,8},{10,11... | collective-permute-start | bytes 442376 | tf_op jit(solution)/shard_map/ppermute | solution.py:493
  6.3 14.0 %collective-permute-start.1 = (bf16[96,768]{1,0:T(8,128)(2,1)S(1)}, bf16[96,768]{1,0:T(8,128)(2,1)S(1)}, u32[]{:S(2)}, u32[]{:S(2)}) collective-permute-start(bf16[96,768]{1,0:T(8,128)(2,1)S(1)} %pad_maximum_fusion.15), channel_id=1, source_target_pairs={{0,2},{1,3},{2,0},{3,1},{4,6},{5,7},{6,4},{7,5},{8,10},{9,11},{10,... | collective-permute-start | bytes 442376 | tf_op jit(solution)/shard_map/ppermute | solution.py:493
  8.9 11.4 %collective-permute-start.2 = (bf16[96,768]{1,0:T(8,128)(2,1)S(1)}, bf16[96,768]{1,0:T(8,128)(2,1)S(1)}, u32[]{:S(2)}, u32[]{:S(2)}) collective-permute-start(bf16[96,768]{1,0:T(8,128)(2,1)S(1)} %pad_maximum_fusion.15), channel_id=1, source_target_pairs={{0,3},{1,2},{2,1},{3,0},{4,7},{5,6},{6,5},{7,4},{8,11},{9,10},{10,... | collective-permute-start | bytes 442376 | tf_op jit(solution)/shard_map/ppermute | solution.py:493
  21.5 18.7 %all-to-all-start = ((bf16[32,55,128]{2,1,0:T(8,128)(2,1)}), bf16[32,55,128]{2,1,0:T(8,128)(2,1)S(1)}, u32[]{:S(2)}, u32[]{:S(2)}) async-start(bf16[32,55,128]{2,1,0:T(8,128)(2,1)} %reshape.190), calls=%async_computation | async-start | bytes 917504 | tf_op jit(solution)/shard_map/all_to_all | solution.py:435
  27.1 30.1 %collective-permute-start.3 = (bf16[4,96,768]{2,1,0:T(8,128)(2,1)S(1)}, bf16[4,96,768]{2,1,0:T(8,128)(2,1)S(1)}, u32[]{:S(2)}, u32[]{:S(2)}) collective-permute-start(bf16[4,96,768]{2,1,0:T(8,128)(2,1)S(1)} %get-tuple-element.262), channel_id=1, source_target_pairs={{0,8},{1,9},{2,10},{3,11},{4,12},{5,13},{6,14},{7,15},{8,0},{9,1},... | collective-permute-start | bytes 1769480 | tf_op jit(solution)/shard_map/ppermute | solution.py:493
  28.9 28.3 %collective-permute-start.4 = (bf16[4,96,768]{2,1,0:T(8,128)(2,1)S(1)}, bf16[4,96,768]{2,1,0:T(8,128)(2,1)S(1)}, u32[]{:S(2)}, u32[]{:S(2)}) collective-permute-start(bf16[4,96,768]{2,1,0:T(8,128)(2,1)S(1)} %get-tuple-element.262), channel_id=1, source_target_pairs={{0,16},{1,17},{2,18},{3,19},{4,20},{5,21},{6,22},{7,23},{8,24},{9,... | collective-permute-start | bytes 1769480 | tf_op jit(solution)/shard_map/ppermute | solution.py:493
  30.4 26.8 %collective-permute-start.5 = (bf16[96,768]{1,0:T(8,128)(2,1)}, bf16[96,768]{1,0:T(8,128)(2,1)}, u32[]{:S(2)}, u32[]{:S(2)}) collective-permute-start(bf16[96,768]{1,0:T(8,128)(2,1)} %param.21), channel_id=1, source_target_pairs={{0,1},{1,0},{2,3},{3,2},{4,5},{5,4},{6,7},{7,6},{8,9},{9,8},{10,11... | collective-permute-start | bytes 442376 | tf_op jit(solution)/shard_map/ppermute | solution.py:493
  31.8 25.3 %collective-permute-start.6 = (bf16[96,768]{1,0:T(8,128)(2,1)}, bf16[96,768]{1,0:T(8,128)(2,1)}, u32[]{:S(2)}, u32[]{:S(2)}) collective-permute-start(bf16[96,768]{1,0:T(8,128)(2,1)} %param.21), channel_id=1, source_target_pairs={{0,2},{1,3},{2,0},{3,1},{4,6},{5,7},{6,4},{7,5},{8,10},{9,11},{10,... | collective-permute-start | bytes 442376 | tf_op jit(solution)/shard_map/ppermute | solution.py:493
  34.3 22.9 %collective-permute-start.7 = (bf16[96,768]{1,0:T(8,128)(2,1)}, bf16[96,768]{1,0:T(8,128)(2,1)}, u32[]{:S(2)}, u32[]{:S(2)}) collective-permute-start(bf16[96,768]{1,0:T(8,128)(2,1)} %param.21), channel_id=1, source_target_pairs={{0,3},{1,2},{2,1},{3,0},{4,7},{5,6},{6,5},{7,4},{8,11},{9,10},{10,... | collective-permute-start | bytes 442376 | tf_op jit(solution)/shard_map/ppermute | solution.py:493
  58.8 22.1 %collective-permute-start.10 = (bf16[4,96,768]{2,1,0:T(8,128)(2,1)S(1)}, bf16[4,96,768]{2,1,0:T(8,128)(2,1)S(1)}, u32[]{:S(2)}, u32[]{:S(2)}) collective-permute-start(bf16[4,96,768]{2,1,0:T(8,128)(2,1)S(1)} %get-tuple-element.275), channel_id=1, source_target_pairs={{0,8},{1,9},{2,10},{3,11},{4,12},{5,13},{6,14},{7,15},{8,0},{9,1},... | collective-permute-start | bytes 1769480 | tf_op jit(solution)/shard_map/ppermute | solution.py:493
  59.5 21.4 %collective-permute-start.11 = (bf16[4,96,768]{2,1,0:T(8,128)(2,1)S(1)}, bf16[4,96,768]{2,1,0:T(8,128)(2,1)S(1)}, u32[]{:S(2)}, u32[]{:S(2)}) collective-permute-start(bf16[4,96,768]{2,1,0:T(8,128)(2,1)S(1)} %get-tuple-element.275), channel_id=1, source_target_pairs={{0,16},{1,17},{2,18},{3,19},{4,20},{5,21},{6,22},{7,23},{8,24},{9,... | collective-permute-start | bytes 1769480 | tf_op jit(solution)/shard_map/ppermute | solution.py:493
  60.9 9.3 %collective-permute-start.13 = (bf16[96,768]{1,0:T(8,128)(2,1)}, bf16[96,768]{1,0:T(8,128)(2,1)S(1)}, u32[]{:S(2)}, u32[]{:S(2)}) collective-permute-start(bf16[96,768]{1,0:T(8,128)(2,1)} %bitcast.256), channel_id=1, source_target_pairs={{0,2},{1,3},{2,0},{3,1},{4,6},{5,7},{6,4},{7,5},{8,10},{9,11},{10,... | collective-permute-start | bytes 442376 | tf_op jit(solution)/shard_map/ppermute | solution.py:493
  62.3 18.6 %collective-permute-start.8 = (bf16[2,96,768]{2,1,0:T(8,128)(2,1)S(1)}, bf16[2,96,768]{2,1,0:T(8,128)(2,1)S(1)}, u32[]{:S(2)}, u32[]{:S(2)}) collective-permute-start(bf16[2,96,768]{2,1,0:T(8,128)(2,1)S(1)} %slice.358), channel_id=1, source_target_pairs={{0,16},{1,17},{2,18},{3,19},{4,20},{5,21},{6,22},{7,23},{8,24},{9,... | collective-permute-start | bytes 884744 | tf_op jit(solution)/shard_map/ppermute | solution.py:493
  67.4 13.5 %collective-permute-start.9 = (bf16[2,96,768]{2,1,0:T(8,128)(2,1)S(1)}, bf16[2,96,768]{2,1,0:T(8,128)(2,1)S(1)}, u32[]{:S(2)}, u32[]{:S(2)}) collective-permute-start(bf16[2,96,768]{2,1,0:T(8,128)(2,1)S(1)} %slice.359), channel_id=1, source_target_pairs={{0,8},{1,9},{2,10},{3,11},{4,12},{5,13},{6,14},{7,15},{8,0},{9,1},... | collective-permute-start | bytes 884744 | tf_op jit(solution)/shard_map/ppermute | solution.py:493
  84.4 10.0 %collective-permute-start.15 = (bf16[4,4,96,768]{3,2,1,0:T(8,128)(2,1)S(1)}, bf16[4,4,96,768]{3,2,1,0:T(8,128)(2,1)}, u32[]{:S(2)}, u32[]{:S(2)}) collective-permute-start(bf16[4,4,96,768]{3,2,1,0:T(8,128)(2,1)S(1)} %pad_maximum_fusion.own), channel_id=1, source_target_pairs={{0,4},{1,5},{2,6},{3,7},{4,0},{5,1},{6,2},{7,3},{8,12},{9,13},{10,... | collective-permute-start | bytes 7077896 | tf_op jit(solution)/shard_map/ppermute | solution.py:493
  84.5 9.6 %collective-permute-start.16 = (bf16[2,96,768]{2,1,0:T(8,128)(2,1)}, bf16[2,96,768]{2,1,0:T(8,128)(2,1)S(1)}, u32[]{:S(2)}, u32[]{:S(2)}) collective-permute-start(bf16[2,96,768]{2,1,0:T(8,128)(2,1)} %slice.361), channel_id=1, source_target_pairs={{0,16},{1,17},{2,18},{3,19},{4,20},{5,21},{6,22},{7,23},{8,24},{9,... | collective-permute-start | bytes 884744 | tf_op jit(solution)/shard_map/ppermute | solution.py:493
  85.2 9.3 %collective-permute-start.17 = (bf16[2,96,768]{2,1,0:T(8,128)(2,1)}, bf16[2,96,768]{2,1,0:T(8,128)(2,1)S(1)}, u32[]{:S(2)}, u32[]{:S(2)}) collective-permute-start(bf16[2,96,768]{2,1,0:T(8,128)(2,1)} %slice.362), channel_id=1, source_target_pairs={{0,8},{1,9},{2,10},{3,11},{4,12},{5,13},{6,14},{7,15},{8,0},{9,1},... | collective-permute-start | bytes 884744 | tf_op jit(solution)/shard_map/ppermute | solution.py:493
  95.2 19.2 %collective-permute-start.18 = (bf16[4,96,768]{2,1,0:T(8,128)(2,1)}, bf16[4,96,768]{2,1,0:T(8,128)(2,1)S(1)}, u32[]{:S(2)}, u32[]{:S(2)}) collective-permute-start(bf16[4,96,768]{2,1,0:T(8,128)(2,1)} %get-tuple-element.293), channel_id=1, source_target_pairs={{0,8},{1,9},{2,10},{3,11},{4,12},{5,13},{6,14},{7,15},{8,0},{9,1},... | collective-permute-start | bytes 1769480 | tf_op jit(solution)/shard_map/ppermute | solution.py:493
  96.6 17.8 %collective-permute-start.19 = (bf16[4,96,768]{2,1,0:T(8,128)(2,1)}, bf16[4,96,768]{2,1,0:T(8,128)(2,1)}, u32[]{:S(2)}, u32[]{:S(2)}) collective-permute-start(bf16[4,96,768]{2,1,0:T(8,128)(2,1)} %get-tuple-element.293), channel_id=1, source_target_pairs={{0,16},{1,17},{2,18},{3,19},{4,20},{5,21},{6,22},{7,23},{8,24},{9,... | collective-permute-start | bytes 1769480 | tf_op jit(solution)/shard_map/ppermute | solution.py:493
  115.6 9.9 %collective-permute-start.20 = (bf16[4,4,96,768]{3,2,1,0:T(8,128)(2,1)S(1)}, bf16[4,4,96,768]{3,2,1,0:T(8,128)(2,1)S(1)}, u32[]{:S(2)}, u32[]{:S(2)}) collective-permute-start(bf16[4,4,96,768]{3,2,1,0:T(8,128)(2,1)S(1)} %pad_maximum_fusion.1.refs_6_), channel_id=1, source_target_pairs={{0,4},{1,5},{2,6},{3,7},{4,0},{5,1},{6,2},{7,3},{8,12},{9,13},{10,... | collective-permute-start | bytes 7077896 | tf_op jit(solution)/shard_map/ppermute | solution.py:493
  115.7 9.6 %collective-permute-start.21 = (bf16[2,96,768]{2,1,0:T(8,128)(2,1)S(1)}, bf16[2,96,768]{2,1,0:T(8,128)(2,1)S(1)}, u32[]{:S(2)}, u32[]{:S(2)}) collective-permute-start(bf16[2,96,768]{2,1,0:T(8,128)(2,1)S(1)} %slice.363), channel_id=1, source_target_pairs={{0,16},{1,17},{2,18},{3,19},{4,20},{5,21},{6,22},{7,23},{8,24},{9,... | collective-permute-start | bytes 884744 | tf_op jit(solution)/shard_map/ppermute | solution.py:493
  116.4 9.1 %collective-permute-start.22 = (bf16[2,96,768]{2,1,0:T(8,128)(2,1)S(1)}, bf16[2,96,768]{2,1,0:T(8,128)(2,1)S(1)}, u32[]{:S(2)}, u32[]{:S(2)}) collective-permute-start(bf16[2,96,768]{2,1,0:T(8,128)(2,1)S(1)} %slice.364), channel_id=1, source_target_pairs={{0,8},{1,9},{2,10},{3,11},{4,12},{5,13},{6,14},{7,15},{8,0},{9,1},... | collective-permute-start | bytes 884744 | tf_op jit(solution)/shard_map/ppermute | solution.py:493
  127.5 11.0 %collective-permute-start.23 = (bf16[4,4,96,768]{3,2,1,0:T(8,128)(2,1)S(1)}, bf16[4,4,96,768]{3,2,1,0:T(8,128)(2,1)}, u32[]{:S(2)}, u32[]{:S(2)}) collective-permute-start(bf16[4,4,96,768]{3,2,1,0:T(8,128)(2,1)S(1)} %pad_maximum_fusion.2.refs_9_), channel_id=1, source_target_pairs={{0,4},{1,5},{2,6},{3,7},{4,0},{5,1},{6,2},{7,3},{8,12},{9,13},{10,... | collective-permute-start | bytes 7077896 | tf_op jit(solution)/shard_map/ppermute | solution.py:493
  177.7 9.3 %collective-permute-start.24 = (bf16[4,4,96,768]{3,2,1,0:T(8,128)(2,1)}, bf16[4,4,96,768]{3,2,1,0:T(8,128)(2,1)S(1)}, u32[]{:S(2)}, u32[]{:S(2)}) collective-permute-start(bf16[4,4,96,768]{3,2,1,0:T(8,128)(2,1)} %get-tuple-element.352), channel_id=1, source_target_pairs={{0,4},{1,5},{2,6},{3,7},{4,0},{5,1},{6,2},{7,3},{8,12},{9,13},{10,... | collective-permute-start | bytes 7077896 | tf_op jit(solution)/shard_map/ppermute | solution.py:493
  192.2 17.1 %collective-permute-start.27 = (bf16[4,4,96,768]{3,2,1,0:T(8,128)(2,1)}, bf16[4,4,96,768]{3,2,1,0:T(8,128)(2,1)S(1)}, u32[]{:S(2)}, u32[]{:S(2)}) collective-permute-start(bf16[4,4,96,768]{3,2,1,0:T(8,128)(2,1)} %get-tuple-element.364), channel_id=1, source_target_pairs={{0,4},{1,5},{2,6},{3,7},{4,0},{5,1},{6,2},{7,3},{8,12},{9,13},{10,... | collective-permute-start | bytes 7077896 | tf_op jit(solution)/shard_map/ppermute | solution.py:493
  192.3 16.3 %collective-permute-start.25 = (bf16[4,96,768]{2,1,0:T(8,128)(2,1)}, bf16[4,96,768]{2,1,0:T(8,128)(2,1)S(1)}, u32[]{:S(2)}, u32[]{:S(2)}) collective-permute-start(bf16[4,96,768]{2,1,0:T(8,128)(2,1)} %get-tuple-element.362), channel_id=1, source_target_pairs={{0,8},{1,9},{2,10},{3,11},{4,12},{5,13},{6,14},{7,15},{8,0},{9,1},... | collective-permute-start | bytes 1769480 | tf_op jit(solution)/shard_map/ppermute | solution.py:493
  193.6 15.6 %collective-permute-start.26 = (bf16[4,96,768]{2,1,0:T(8,128)(2,1)}, bf16[4,96,768]{2,1,0:T(8,128)(2,1)S(1)}, u32[]{:S(2)}, u32[]{:S(2)}) collective-permute-start(bf16[4,96,768]{2,1,0:T(8,128)(2,1)} %get-tuple-element.363), channel_id=1, source_target_pairs={{0,16},{1,17},{2,18},{3,19},{4,20},{5,21},{6,22},{7,23},{8,24},{9,... | collective-permute-start | bytes 1769480 | tf_op jit(solution)/shard_map/ppermute | solution.py:493
  218.3 22.3 %collective-permute-start.30 = (bf16[4,96,768]{2,1,0:T(8,128)(2,1)}, bf16[4,96,768]{2,1,0:T(8,128)(2,1)S(1)}, u32[]{:S(2)}, u32[]{:S(2)}) collective-permute-start(bf16[4,96,768]{2,1,0:T(8,128)(2,1)} %pad_maximum_fusion.10), channel_id=1, source_target_pairs={{0,8},{1,9},{2,10},{3,11},{4,12},{5,13},{6,14},{7,15},{8,0},{9,1},... | collective-permute-start | bytes 1769480 | tf_op jit(solution)/shard_map/ppermute | solution.py:493
  219.0 21.6 %collective-permute-start.31 = (bf16[4,96,768]{2,1,0:T(8,128)(2,1)}, bf16[4,96,768]{2,1,0:T(8,128)(2,1)S(1)}, u32[]{:S(2)}, u32[]{:S(2)}) collective-permute-start(bf16[4,96,768]{2,1,0:T(8,128)(2,1)} %pad_maximum_fusion.11), channel_id=1, source_target_pairs={{0,16},{1,17},{2,18},{3,19},{4,20},{5,21},{6,22},{7,23},{8,24},{9,... | collective-permute-start | bytes 1769480 | tf_op jit(solution)/shard_map/ppermute | solution.py:493
  223.1 17.5 %collective-permute-start.28 = (bf16[2,96,768]{2,1,0:T(8,128)(2,1)}, bf16[2,96,768]{2,1,0:T(8,128)(2,1)S(1)}, u32[]{:S(2)}, u32[]{:S(2)}) collective-permute-start(bf16[2,96,768]{2,1,0:T(8,128)(2,1)} %get-tuple-element.383), channel_id=1, source_target_pairs={{0,16},{1,17},{2,18},{3,19},{4,20},{5,21},{6,22},{7,23},{8,24},{9,... | collective-permute-start | bytes 884744 | tf_op jit(solution)/shard_map/ppermute | solution.py:493
  223.7 16.9 %collective-permute-start.29 = (bf16[2,96,768]{2,1,0:T(8,128)(2,1)}, bf16[2,96,768]{2,1,0:T(8,128)(2,1)S(1)}, u32[]{:S(2)}, u32[]{:S(2)}) collective-permute-start(bf16[2,96,768]{2,1,0:T(8,128)(2,1)} %get-tuple-element.384), channel_id=1, source_target_pairs={{0,8},{1,9},{2,10},{3,11},{4,12},{5,13},{6,14},{7,15},{8,0},{9,1},... | collective-permute-start | bytes 884744 | tf_op jit(solution)/shard_map/ppermute | solution.py:493
  244.6 19.9 %collective-permute-start.32 = (bf16[96,768]{1,0:T(8,128)(2,1)S(1)}, bf16[96,768]{1,0:T(8,128)(2,1)S(1)}, u32[]{:S(2)}, u32[]{:S(2)}) collective-permute-start(bf16[96,768]{1,0:T(8,128)(2,1)S(1)} %fusion.25), channel_id=1, source_target_pairs={{0,1},{1,0},{2,3},{3,2},{4,5},{5,4},{6,7},{7,6},{8,9},{9,8},{10,11... | collective-permute-start | bytes 442376 | tf_op jit(solution)/shard_map/ppermute | solution.py:493
  245.1 19.3 %collective-permute-start.33 = (bf16[96,768]{1,0:T(8,128)(2,1)S(1)}, bf16[96,768]{1,0:T(8,128)(2,1)S(1)}, u32[]{:S(2)}, u32[]{:S(2)}) collective-permute-start(bf16[96,768]{1,0:T(8,128)(2,1)S(1)} %get-tuple-element.409), channel_id=1, source_target_pairs={{0,2},{1,3},{2,0},{3,1},{4,6},{5,7},{6,4},{7,5},{8,10},{9,11},{10,... | collective-permute-start | bytes 442376 | tf_op jit(solution)/shard_map/ppermute | solution.py:493
  246.6 18.1 %collective-permute-start.34 = (bf16[96,768]{1,0:T(8,128)(2,1)S(1)}, bf16[96,768]{1,0:T(8,128)(2,1)S(1)}, u32[]{:S(2)}, u32[]{:S(2)}) collective-permute-start(bf16[96,768]{1,0:T(8,128)(2,1)S(1)} %get-tuple-element.410), channel_id=1, source_target_pairs={{0,3},{1,2},{2,1},{3,0},{4,7},{5,6},{6,5},{7,4},{8,11},{9,10},{10,... | collective-permute-start | bytes 442376 | tf_op jit(solution)/shard_map/ppermute | solution.py:493
  249.0 15.7 %collective-permute-start.35 = (bf16[2,96,768]{2,1,0:T(8,128)(2,1)S(1)}, bf16[2,96,768]{2,1,0:T(8,128)(2,1)S(1)}, u32[]{:S(2)}, u32[]{:S(2)}) collective-permute-start(bf16[2,96,768]{2,1,0:T(8,128)(2,1)S(1)} %get-tuple-element.411), channel_id=1, source_target_pairs={{0,16},{1,17},{2,18},{3,19},{4,20},{5,21},{6,22},{7,23},{8,24},{9,... | collective-permute-start | bytes 884744 | tf_op jit(solution)/shard_map/ppermute | solution.py:493
  249.6 15.2 %collective-permute-start.36 = (bf16[2,96,768]{2,1,0:T(8,128)(2,1)S(1)}, bf16[2,96,768]{2,1,0:T(8,128)(2,1)S(1)}, u32[]{:S(2)}, u32[]{:S(2)}) collective-permute-start(bf16[2,96,768]{2,1,0:T(8,128)(2,1)S(1)} %get-tuple-element.412), channel_id=1, source_target_pairs={{0,8},{1,9},{2,10},{3,11},{4,12},{5,13},{6,14},{7,15},{8,0},{9,1},... | collective-permute-start | bytes 884744 | tf_op jit(solution)/shard_map/ppermute | solution.py:493
  269.6 16.6 %collective-permute-start.40 = (bf16[160,128]{1,0:T(8,128)(2,1)S(1)}, bf16[160,128]{1,0:T(8,128)(2,1)S(1)}, u32[]{:S(2)}, u32[]{:S(2)}) collective-permute-start(bf16[160,128]{1,0:T(8,128)(2,1)S(1)} %fusion.32), channel_id=1, source_target_pairs={{0,1},{1,0},{2,3},{3,2},{4,5},{5,4},{6,7},{7,6},{8,9},{9,8},{10,11... | collective-permute-start | bytes 122888 | tf_op jit(solution)/shard_map/ppermute | solution.py:493
  269.7 19.2 %collective-permute-start.41 = (bf16[160,128]{1,0:T(8,128)(2,1)S(1)}, bf16[160,128]{1,0:T(8,128)(2,1)S(1)}, u32[]{:S(2)}, u32[]{:S(2)}) collective-permute-start(bf16[160,128]{1,0:T(8,128)(2,1)S(1)} %fusion.32), channel_id=1, source_target_pairs={{0,2},{1,3},{2,0},{3,1},{4,6},{5,7},{6,4},{7,5},{8,10},{9,11},{10,... | collective-permute-start | bytes 122888 | tf_op jit(solution)/shard_map/ppermute | solution.py:493
  271.4 20.6 %collective-permute-start.37 = (bf16[96,768]{1,0:T(8,128)(2,1)S(1)}, bf16[96,768]{1,0:T(8,128)(2,1)S(1)}, u32[]{:S(2)}, u32[]{:S(2)}) collective-permute-start(bf16[96,768]{1,0:T(8,128)(2,1)S(1)} %fusion.26), channel_id=1, source_target_pairs={{0,1},{1,0},{2,3},{3,2},{4,5},{5,4},{6,7},{7,6},{8,9},{9,8},{10,11... | collective-permute-start | bytes 442376 | tf_op jit(solution)/shard_map/ppermute | solution.py:493
  271.7 20.4 %collective-permute-start.38 = (bf16[96,768]{1,0:T(8,128)(2,1)S(1)}, bf16[96,768]{1,0:T(8,128)(2,1)S(1)}, u32[]{:S(2)}, u32[]{:S(2)}) collective-permute-start(bf16[96,768]{1,0:T(8,128)(2,1)S(1)} %get-tuple-element.439), channel_id=1, source_target_pairs={{0,2},{1,3},{2,0},{3,1},{4,6},{5,7},{6,4},{7,5},{8,10},{9,11},{10,... | collective-permute-start | bytes 442376 | tf_op jit(solution)/shard_map/ppermute | solution.py:493
  274.6 17.4 %collective-permute-start.39 = (bf16[96,768]{1,0:T(8,128)(2,1)S(1)}, bf16[96,768]{1,0:T(8,128)(2,1)S(1)}, u32[]{:S(2)}, u32[]{:S(2)}) collective-permute-start(bf16[96,768]{1,0:T(8,128)(2,1)S(1)} %get-tuple-element.440), channel_id=1, source_target_pairs={{0,3},{1,2},{2,1},{3,0},{4,7},{5,6},{6,5},{7,4},{8,11},{9,10},{10,... | collective-permute-start | bytes 442376 | tf_op jit(solution)/shard_map/ppermute | solution.py:493
  292.9 11.3 %collective-permute-start.43 = (bf16[4,4,96,768]{3,2,1,0:T(8,128)(2,1)}, bf16[4,4,96,768]{3,2,1,0:T(8,128)(2,1)S(1)}, u32[]{:S(2)}, u32[]{:S(2)}) collective-permute-start(bf16[4,4,96,768]{3,2,1,0:T(8,128)(2,1)} %get-tuple-element.455), channel_id=1, source_target_pairs={{0,4},{1,5},{2,6},{3,7},{4,0},{5,1},{6,2},{7,3},{8,12},{9,13},{10,... | collective-permute-start | bytes 7077896 | tf_op jit(solution)/shard_map/ppermute | solution.py:493
  294.0 9.1 %collective-permute-start.45 = (bf16[4,160,128]{2,1,0:T(8,128)(2,1)}, bf16[4,160,128]{2,1,0:T(8,128)(2,1)}, u32[]{:S(2)}, u32[]{:S(2)}) collective-permute-start(bf16[4,160,128]{2,1,0:T(8,128)(2,1)} %get-tuple-element.458), channel_id=1, source_target_pairs={{0,16},{1,17},{2,18},{3,19},{4,20},{5,21},{6,22},{7,23},{8,24},{9,... | collective-permute-start | bytes 491528 | tf_op jit(solution)/shard_map/ppermute | solution.py:493
  314.5 17.6 %collective-permute-start.47 = (bf16[4,96,768]{2,1,0:T(8,128)(2,1)}, bf16[4,96,768]{2,1,0:T(8,128)(2,1)}, u32[]{:S(2)}, u32[]{:S(2)}) collective-permute-start(bf16[4,96,768]{2,1,0:T(8,128)(2,1)} %pad_maximum_fusion.12), channel_id=1, source_target_pairs={{0,8},{1,9},{2,10},{3,11},{4,12},{5,13},{6,14},{7,15},{8,0},{9,1},... | collective-permute-start | bytes 1769480 | tf_op jit(solution)/shard_map/ppermute | solution.py:493
  315.6 16.5 %collective-permute-start.48 = (bf16[4,96,768]{2,1,0:T(8,128)(2,1)}, bf16[4,96,768]{2,1,0:T(8,128)(2,1)}, u32[]{:S(2)}, u32[]{:S(2)}) collective-permute-start(bf16[4,96,768]{2,1,0:T(8,128)(2,1)} %pad_maximum_fusion.13), channel_id=1, source_target_pairs={{0,16},{1,17},{2,18},{3,19},{4,20},{5,21},{6,22},{7,23},{8,24},{9,... | collective-permute-start | bytes 1769480 | tf_op jit(solution)/shard_map/ppermute | solution.py:493
  321.1 10.9 %all-to-all-start.2 = ((f32[32,1,128]{2,1,0:T(1,128)}), f32[32,1,128]{2,1,0:T(1,128)S(1)}, u32[]{:S(2)}, u32[]{:S(2)}) async-start(f32[32,1,128]{2,1,0:T(1,128)} %bitcast.76), calls=%async_computation.2 | async-start | bytes 32768 | tf_op jit(solution)/shard_map/all_to_all | solution.py:435
  349.3 13.8 %collective-permute-start.53 = (bf16[96,768]{1,0:T(8,128)(2,1)S(1)}, bf16[96,768]{1,0:T(8,128)(2,1)S(1)}, u32[]{:S(2)}, u32[]{:S(2)}) collective-permute-start(bf16[96,768]{1,0:T(8,128)(2,1)S(1)} %get-tuple-element.480), channel_id=1, source_target_pairs={{0,2},{1,3},{2,0},{3,1},{4,6},{5,7},{6,4},{7,5},{8,10},{9,11},{10,... | collective-permute-start | bytes 442376 | tf_op jit(solution)/shard_map/ppermute | solution.py:493
  352.5 10.6 %collective-permute-start.54 = (bf16[96,768]{1,0:T(8,128)(2,1)S(1)}, bf16[96,768]{1,0:T(8,128)(2,1)S(1)}, u32[]{:S(2)}, u32[]{:S(2)}) collective-permute-start(bf16[96,768]{1,0:T(8,128)(2,1)S(1)} %get-tuple-element.481), channel_id=1, source_target_pairs={{0,3},{1,2},{2,1},{3,0},{4,7},{5,6},{6,5},{7,4},{8,11},{9,10},{10,... | collective-permute-start | bytes 442376 | tf_op jit(solution)/shard_map/ppermute | solution.py:493
  (61 other events, 398.3 us)

commit v5 on v4

--- a/solution.py
+++ b/solution.py
@@ -812,7 +812,7 @@
         heads_out = Flow(
             reduce_stages(
                 *slot(
-                    flows + [shared_in], (input_one, qkv_grad, attended_grad, mixed), heads_grad
+                    [shared_in], (input_one, qkv_grad, attended_grad, mixed), heads_grad
                 )
             )
         )
@@ -823,7 +823,7 @@
             return both, ada_back(both, columns, order)
 
         shared, (silu_grad, ada_weight_grad) = slot(
-            [heads_out], (shared_in.value, silu_columns, to_owner), finish_vectors
+            [heads_out] + flows, (shared_in.value, silu_columns, to_owner), finish_vectors
         )
         condition_grad = slot([heads_out], (silu_grad,), condition_back)
         slot([heads_out], (), lambda: ())

time: 372 us -> 367 us (0.987)
    unnamed x109 -> x99, local copies, waits for them, and re-layouts: 11 us -> 9.18 us
  transfers between devices with their start and end apart: 57 -> 57, of which waited for: 20 -> 19; matrix products, arithmetic and copies ran while one was open for 9% -> 10% of each run, Pallas kernels for 25% -> 26%
where the time goes in v5:
time: 367 us; the launch traced here: 360 us
  Pallas kernels  131 us (36%)
  starting transfers between devices  70.7 us (19%)
  waiting for transfers between devices  57.8 us (16%)
  other arithmetic  49 us (13%)
  local copies, waits for them, and re-layouts  32.6 us (9%)
  blocking collectives  13.1 us (4%)
    pallas_call x7, Pallas kernels, over_latents(): pl.pallas_call(body, grid=(steps,), in_specs=[spec(array, first) for spec...  96.1 us
    ppermute x55, starting transfers between devices, swap(): lax.ppermute(array, axes, [(device, device ^ mask) for device in range(co...  62.6 us
    ppermute x55, waiting for transfers between devices, swap(): lax.ppermute(array, axes, [(device, device ^ mask) for device in range(co...  45.6 us
    pallas_call x4, Pallas kernels, placed_call(): pl.pallas_call(kernel, grid_spec=pltpu.PrefetchScalarGridSpec(num_scalar_...  34.8 us
    all_to_all x1, blocking collectives, modulate(): back = lax.all_to_all(columns, axes, 0, 0, tiled=True)  13.1 us
    all_to_all x2, waiting for transfers between devices, exchange(): lax.all_to_all(padded, axes, 0, 0, tiled=True).reshape(count, -1)[:, :size]  12.2 us
    add x3, other arithmetic, reduce_stages(): summed = keep.astype(F32) + arrived.astype(F32)  11.6 us
    unnamed x99, local copies, waits for them, and re-layouts  9.18 us
  transfers between devices with their start and end apart: 57, of which 19 were waited for; matrix products, arithmetic and copies ran while one was open for 10% of the time, Pallas kernels for 26%

profile of v5, /device:TPU:0, one launch (start us, length us, event | category | flops | bytes accessed | tf_op | source)
XLA Modules:
  0.0 360.1 jit_solution(3369830830039216746)
XLA Ops:
  3.2 3.1 collective-permute-start
  6.3 2.6 collective-permute-start.1
  10.6 1.6 reshape.184
  13.3 7.0 %collective-permute-done.1 = bf16[96,768]{1,0:T(8,128)(2,1)S(1)} collective-permute-done((bf16[96,768]{1,0:T(8,128)(2,1)S(1)}, bf16[96,768]{1,0:T(8,128)(2,1)S(1)}, u32[]{:S(2)}, u32[]{:S(2)}) %collective-permute-start.1) | collective-permute-done | bytes 147488 | tf_op jit(solution)/shard_map/ppermute | solution.py:493
  21.5 5.6 %all-to-all-start = ((bf16[32,55,128]{2,1,0:T(8,128)(2,1)}), bf16[32,55,128]{2,1,0:T(8,128)(2,1)S(1)}, u32[]{:S(2)}, u32[]{:S(2)}) async-start(bf16[32,55,128]{2,1,0:T(8,128)(2,1)} %reshape.190), calls=%async_computation | async-start | bytes 917504 | tf_op jit(solution)/shard_map/all_to_all | solution.py:435
  27.1 1.8 collective-permute-start.3
  31.8 2.5 collective-permute-start.6
  34.8 5.5 %all-to-all-done = bf16[32,55,128]{2,1,0:T(8,128)(2,1)S(1)} async-done(((bf16[32,55,128]{2,1,0:T(8,128)(2,1)}), bf16[32,55,128]{2,1,0:T(8,128)(2,1)S(1)}, u32[]{:S(2)}, u32[]{:S(2)}) %all-to-all-start) | async-done | bytes 450592 | tf_op jit(solution)/shard_map/all_to_all | solution.py:435
  43.2 13.1 %all_to_all.15 = f32[32,4,128]{2,1,0:T(4,128)S(1)} all-to-all(f32[32,4,128]{2,1,0:T(4,128)S(1)} %reshape.195), channel_id=1, replica_groups=mesh['dp'=8,'tensor'=4] {'dp','tensor'}, dimensions={0} | all-to-all | bytes 131072 | tf_op jit(solution)/shard_map/all_to_all | solution.py:583
  63.8 3.7 %collective-permute-done.12 = bf16[96,768]{1,0:T(8,128)(2,1)S(1)} collective-permute-done((bf16[96,768]{1,0:T(8,128)(2,1)}, bf16[96,768]{1,0:T(8,128)(2,1)S(1)}, u32[]{:S(2)}, u32[]{:S(2)}) %collective-permute-start.12) | collective-permute-done | bytes 147488 | tf_op jit(solution)/shard_map/ppermute | solution.py:493
  71.5 5.8 %collective-permute-done.14 = bf16[96,768]{1,0:T(8,128)(2,1)S(1)} collective-permute-done((bf16[96,768]{1,0:T(8,128)(2,1)}, bf16[96,768]{1,0:T(8,128)(2,1)S(1)}, u32[]{:S(2)}, u32[]{:S(2)}) %collective-permute-start.14) | collective-permute-done | bytes 147488 | tf_op jit(solution)/shard_map/ppermute | solution.py:493
  77.3 3.6 %collective-permute-done.8 = bf16[2,96,768]{2,1,0:T(8,128)(2,1)S(1)} collective-permute-done((bf16[2,96,768]{2,1,0:T(8,128)(2,1)S(1)}, bf16[2,96,768]{2,1,0:T(8,128)(2,1)S(1)}, u32[]{:S(2)}, u32[]{:S(2)}) %collective-permute-start.8) | collective-permute-done | bytes 294944 | tf_op jit(solution)/shard_map/ppermute | solution.py:493
  88.1 2.0 fusion.58
  90.1 4.0 %collective-permute-done.16 = bf16[2,96,768]{2,1,0:T(8,128)(2,1)S(1)} collective-permute-done((bf16[2,96,768]{2,1,0:T(8,128)(2,1)}, bf16[2,96,768]{2,1,0:T(8,128)(2,1)S(1)}, u32[]{:S(2)}, u32[]{:S(2)}) %collective-permute-start.16) | collective-permute-done | bytes 294944 | tf_op jit(solution)/shard_map/ppermute | solution.py:493
  98.6 6.9 %shard_map.228 = (bf16[4,3,8,96,192]{4,3,2,1,0:T(8,128)(2,1)}, bf16[4,8,96,192]{3,2,1,0:T(8,128)(2,1)}) custom-call(s32[2]{0:T(128)} %pad_add_fusion.place.refs_12_, bf16[4,4,96,768]{3,2,1,0:T(8,128)(2,1)} %copy-done.1, bf16[4,4,96,768]{3,2,1,0:T(8,128)(2,1)} %collective-permute-done.15.other), custom_call_target="tpu_custom_call" | custom-call | bytes 9437184 | tf_op jit(solution)/shard_map/pallas_call | solution.py:369
  105.6 8.5 %shard_map.229 = (bf16[768,768]{1,0:T(8,128)(2,1)}, bf16[4,3,768,192]{3,2,1,0:T(8,128)(2,1)}, bf16[4,768,192]{2,1,0:T(8,128)(2,1)}) custom-call(bf16[768,768]{1,0:T(8,128)(2,1)} %refs_4_.2, f32[3,6,768]{2,1,0:T(8,128)} %reshape.198.refs_1_.refs_3_.refs_5_, bf16[1,4,3,768,192]{4,3,2,1,0:T(8,128)(2,1)} %bitcast.220, bf16[4,2,192]{2,1,0:T(2,128)(2,1)} %reshape.199.refs_3_), custom_call_target="tpu_custom_call" | custom-call | flops 1811939328 | bytes 10675200 | tf_op jit(solution)/shard_map/pallas_call | solution.py:283
  117.0 8.4 %shard_map.230 = (bf16[768,768]{1,0:T(8,128)(2,1)}, bf16[4,3,768,192]{3,2,1,0:T(8,128)(2,1)}, bf16[4,768,192]{2,1,0:T(8,128)(2,1)}) custom-call(bf16[768,768]{1,0:T(8,128)(2,1)} %refs_4_.2, f32[3,6,768]{2,1,0:T(8,128)} %reshape.198.refs_1_.refs_3_.refs_5_, ...), custom_call_target="tpu_custom_call", output_to_operand_aliasing={{0}: (4, {}), {1}: (5, {}), {2}: (6, {})} | custom-call | flops 1811939328 | bytes 10675200 | tf_op jit(solution)/shard_map/pallas_call | solution.py:283
  125.6 1.9 pad_maximum_fusion.2.refs_9_
  130.3 8.3 %shard_map.231 = (bf16[768,768]{1,0:T(8,128)(2,1)}, bf16[4,3,768,192]{3,2,1,0:T(8,128)(2,1)}, bf16[4,768,192]{2,1,0:T(8,128)(2,1)}) custom-call(bf16[768,768]{1,0:T(8,128)(2,1)} %refs_4_.2, f32[3,6,768]{2,1,0:T(8,128)} %reshape.198.refs_1_.refs_3_.refs_5_, ...), custom_call_target="tpu_custom_call", output_to_operand_aliasing={{0}: (4, {}), {1}: (5, {}), {2}: (6, {})} | custom-call | flops 1811939328 | bytes 10675200 | tf_op jit(solution)/shard_map/pallas_call | solution.py:283
  138.6 30.5 %shard_map.232 = (f32[768,768]{1,0:T(8,128)}, bf16[4,768,768]{2,1,0:T(8,128)(2,1)}, bf16[4,768,768]{2,1,0:T(8,128)(2,1)}, bf16[768,768]{1,0:T(8,128)(2,1)}, bf16...) custom-call(bf16[4,768,192]{2,1,0:T(8,128)(2,1)} %get-tuple-element., ...), custom_call_target="tpu_custom_call" | custom-call | flops 16307453952 | bytes 31970312 | tf_op jit(solution)/shard_map/pallas_call | solution.py:283
  169.2 8.6 %shard_map.233 = (bf16[4,4,96,768]{3,2,1,0:T(8,128)(2,1)}, bf16[4,4,96,768]{3,2,1,0:T(8,128)(2,1)}) custom-call(s32[2]{0:T(128)} %pad_add_fusion.place.refs_12_, bf16[768,768]{1,0:T(8,128)(2,1)} %get-tuple-element.346.left, bf16[4,768,768]{2,1,0:T(8,128)(2,1)} %get-tuple-element.347.right), custom_call_target="tpu_custom_call" | custom-call | flops 3623878656 | bytes 10616832 | tf_op jit(solution)/shard_map/pallas_call | solution.py:369
  178.1 8.9 %shard_map.234 = (bf16[4,4,96,768]{3,2,1,0:T(8,128)(2,1)}, bf16[4,4,96,768]{3,2,1,0:T(8,128)(2,1)}) custom-call(s32[2]{0:T(128)} %pad_add_fusion.place.refs_12_, bf16[768,768]{1,0:T(8,128)(2,1)} %get-tuple-element.353.left, bf16[4,768,768]{2,1,0:T(8,128)(2,1)} %get-tuple-element.354.right), custom_call_target="tpu_custom_call" | custom-call | flops 3623878656 | bytes 10616832 | tf_op jit(solution)/shard_map/pallas_call | solution.py:369
  188.5 2.4 convert_add_fusion.2
  195.2 13.4 %shard_map.235 = (bf16[4,3,768,192]{3,2,1,0:T(8,128)(2,1)}, f32[768,768]{1,0:T(8,128)}, f32[3,2,768]{2,1,0:T(2,128)}, f32[4,3,192]{2,1,0:T(4,128)}) custom-call(bf16[768,768]{1,0:T(8,128)(2,1)} %get-tuple-element.441.refs_0_.outer, bf16[4,3,768,192]{3,2,1,0:T(8,128)(2,1)} %get-tuple-element.414.refs_1_, bf16[1,4,768,192]{3,2,1,0:T(8,128)(2,1)} %bitcast.230, ...), custom_call_target="tpu_custom_call" | custom-call | flops 5435817984 | bytes 18957312 | tf_op jit(solution)/shard_map/pallas_call | solution.py:283
  211.1 4.6 %convert_add_fusion.1 = (f32[4,4,96,768]{3,2,1,0:T(8,128)}, bf16[4,4,96,768]{3,2,1,0:T(8,128)(2,1)S(1)}) fusion(bf16[4,4,96,768]{3,2,1,0:T(8,128)(2,1)} %copy-done.8, bf16[4,4,96,768]{3,2,1,0:T(8,128)(2,1)S(1)} %copy-done.7), kind=kLoop, calls=%fused_computation.1 | loop fusion | flops 4718592 | bytes 11796480 | tf_op jit(solution)/shard_map/add | solution.py:528
  225.3 13.6 %shard_map.236 = (bf16[4,3,768,192]{3,2,1,0:T(8,128)(2,1)}, f32[768,768]{1,0:T(8,128)}, f32[3,2,768]{2,1,0:T(2,128)}, f32[4,3,192]{2,1,0:T(4,128)}) custom-call(bf16[768,768]{1,0:T(8,128)(2,1)} %get-tuple-element.441.refs_0_.outer, bf16[4,3,768,192]{3,2,1,0:T(8,128)(2,1)} %get-tuple-element.414.refs_1_, ...), custom_call_target="tpu_custom_call", output_to_operand_aliasing={{0}: (7, {}), {1}: (8, {}), {2}: (9, {})} | custom-call | flops 5435817984 | bytes 18957312 | tf_op jit(solution)/shard_map/pallas_call | solution.py:283
  238.9 1.7 collective-permute-done.28
  244.9 1.7 collective-permute-start.33
  246.6 2.4 collective-permute-start.34
  251.2 13.4 %shard_map.237 = (bf16[4,3,768,192]{3,2,1,0:T(8,128)(2,1)}, f32[768,768]{1,0:T(8,128)}, f32[3,2,768]{2,1,0:T(2,128)}, f32[4,3,192]{2,1,0:T(4,128)}) custom-call(bf16[768,768]{1,0:T(8,128)(2,1)} %get-tuple-element.441.refs_0_.outer, bf16[4,3,768,192]{3,2,1,0:T(8,128)(2,1)} %get-tuple-element.414.refs_1_, ...), custom_call_target="tpu_custom_call", output_to_operand_aliasing={{0}: (7, {}), {1}: (8, {}), {2}: (9, {})} | custom-call | flops 5435817984 | bytes 18957312 | tf_op jit(solution)/shard_map/pallas_call | solution.py:283
  267.5 1.6 collective-permute-start.38
  269.2 2.7 collective-permute-start.39
  271.9 10.4 %shard_map.238 = (bf16[4,4,96,768]{3,2,1,0:T(8,128)(2,1)}, bf16[4,4,96,768]{3,2,1,0:T(8,128)(2,1)}) custom-call(s32[2]{0:T(128)} %pad_add_fusion.place.refs_12_, bf16[768,768]{1,0:T(8,128)(2,1)} %get-tuple-element.439.entry, bf16[4,3,768,192]{3,2,1,0:T(8,128)(2,1)} %get-tuple-element.440.qkv_grad, bf16[768,768]{1,0:T(8,128)(2,1)} %get-tuple-element.441.refs_0_.outer, ...), custom_call_target="tpu_custom_call" | custom-call | flops 3623878656 | bytes 11796480 | tf_op jit(solution)/shard_map/pallas_call | solution.py:369
  284.1 1.7 fusion.6
  288.4 1.6 collective-permute-start.43
  290.1 3.5 collective-permute-done.41
  293.6 3.8 %collective-permute-done.43 = bf16[4,160,128]{2,1,0:T(8,128)(2,1)S(1)} collective-permute-done((bf16[4,160,128]{2,1,0:T(8,128)(2,1)S(1)}, bf16[4,160,128]{2,1,0:T(8,128)(2,1)S(1)}, u32[]{:S(2)}, u32[]{:S(2)}) %collective-permute-start.43) | collective-permute-done | bytes 163872 | tf_op jit(solution)/shard_map/ppermute | solution.py:493
  297.4 4.6 %convert_add_fusion = (f32[4,4,96,768]{3,2,1,0:T(8,128)}, bf16[4,4,96,768]{3,2,1,0:T(8,128)(2,1)S(1)}) fusion(bf16[4,4,96,768]{3,2,1,0:T(8,128)(2,1)} %collective-permute-done.40, bf16[4,4,96,768]{3,2,1,0:T(8,128)(2,1)S(1)} %copy-done.6), kind=kLoop, calls=%fused_computation | loop fusion | flops 4718592 | bytes 11796480 | tf_op jit(solution)/shard_map/add | solution.py:528
  304.9 1.6 collective-permute-start.47
  306.5 2.8 collective-permute-start.48
  315.1 2.5 all-to-all-start.2
  318.7 6.7 %all-to-all-done.2 = f32[32,1,128]{2,1,0:T(1,128)S(1)} async-done(((f32[32,1,128]{2,1,0:T(1,128)}), f32[32,1,128]{2,1,0:T(1,128)S(1)}, u32[]{:S(2)}, u32[]{:S(2)}) %all-to-all-start.2) | async-done | bytes 16416 | tf_op jit(solution)/shard_map/all_to_all | solution.py:435
  329.3 2.1 fusion.3
  336.3 1.7 reduce_sum.18
  338.0 1.9 fusion.21
  339.9 1.6 collective-permute-done.50
  345.4 3.0 collective-permute-start.54
  351.2 6.5 %collective-permute-done.53 = bf16[96,768]{1,0:T(8,128)(2,1)S(1)} collective-permute-done((bf16[96,768]{1,0:T(8,128)(2,1)S(1)}, bf16[96,768]{1,0:T(8,128)(2,1)S(1)}, u32[]{:S(2)}, u32[]{:S(2)}) %collective-permute-start.53) | collective-permute-done | bytes 147488 | tf_op jit(solution)/shard_map/ppermute | solution.py:493
  (307 shorter events, 100.1 us)
Async XLA Ops:
  3.2 10.1 %collective-permute-start = (bf16[96,768]{1,0:T(8,128)(2,1)S(1)}, bf16[96,768]{1,0:T(8,128)(2,1)S(1)}, u32[]{:S(2)}, u32[]{:S(2)}) collective-permute-start(bf16[96,768]{1,0:T(8,128)(2,1)S(1)} %pad_maximum_fusion.15), channel_id=1, source_target_pairs={{0,1},{1,0},{2,3},{3,2},{4,5},{5,4},{6,7},{7,6},{8,9},{9,8},{10,11... | collective-permute-start | bytes 442376 | tf_op jit(solution)/shard_map/ppermute | solution.py:493
  6.3 14.0 %collective-permute-start.1 = (bf16[96,768]{1,0:T(8,128)(2,1)S(1)}, bf16[96,768]{1,0:T(8,128)(2,1)S(1)}, u32[]{:S(2)}, u32[]{:S(2)}) collective-permute-start(bf16[96,768]{1,0:T(8,128)(2,1)S(1)} %pad_maximum_fusion.15), channel_id=1, source_target_pairs={{0,2},{1,3},{2,0},{3,1},{4,6},{5,7},{6,4},{7,5},{8,10},{9,11},{10,... | collective-permute-start | bytes 442376 | tf_op jit(solution)/shard_map/ppermute | solution.py:493
  8.9 11.4 %collective-permute-start.2 = (bf16[96,768]{1,0:T(8,128)(2,1)S(1)}, bf16[96,768]{1,0:T(8,128)(2,1)S(1)}, u32[]{:S(2)}, u32[]{:S(2)}) collective-permute-start(bf16[96,768]{1,0:T(8,128)(2,1)S(1)} %pad_maximum_fusion.15), channel_id=1, source_target_pairs={{0,3},{1,2},{2,1},{3,0},{4,7},{5,6},{6,5},{7,4},{8,11},{9,10},{10,... | collective-permute-start | bytes 442376 | tf_op jit(solution)/shard_map/ppermute | solution.py:493
  21.5 18.7 %all-to-all-start = ((bf16[32,55,128]{2,1,0:T(8,128)(2,1)}), bf16[32,55,128]{2,1,0:T(8,128)(2,1)S(1)}, u32[]{:S(2)}, u32[]{:S(2)}) async-start(bf16[32,55,128]{2,1,0:T(8,128)(2,1)} %reshape.190), calls=%async_computation | async-start | bytes 917504 | tf_op jit(solution)/shard_map/all_to_all | solution.py:435
  27.1 30.1 %collective-permute-start.3 = (bf16[4,96,768]{2,1,0:T(8,128)(2,1)S(1)}, bf16[4,96,768]{2,1,0:T(8,128)(2,1)S(1)}, u32[]{:S(2)}, u32[]{:S(2)}) collective-permute-start(bf16[4,96,768]{2,1,0:T(8,128)(2,1)S(1)} %get-tuple-element.262), channel_id=1, source_target_pairs={{0,8},{1,9},{2,10},{3,11},{4,12},{5,13},{6,14},{7,15},{8,0},{9,1},... | collective-permute-start | bytes 1769480 | tf_op jit(solution)/shard_map/ppermute | solution.py:493
  28.9 28.3 %collective-permute-start.4 = (bf16[4,96,768]{2,1,0:T(8,128)(2,1)S(1)}, bf16[4,96,768]{2,1,0:T(8,128)(2,1)S(1)}, u32[]{:S(2)}, u32[]{:S(2)}) collective-permute-start(bf16[4,96,768]{2,1,0:T(8,128)(2,1)S(1)} %get-tuple-element.262), channel_id=1, source_target_pairs={{0,16},{1,17},{2,18},{3,19},{4,20},{5,21},{6,22},{7,23},{8,24},{9,... | collective-permute-start | bytes 1769480 | tf_op jit(solution)/shard_map/ppermute | solution.py:493
  30.4 26.8 %collective-permute-start.5 = (bf16[96,768]{1,0:T(8,128)(2,1)}, bf16[96,768]{1,0:T(8,128)(2,1)}, u32[]{:S(2)}, u32[]{:S(2)}) collective-permute-start(bf16[96,768]{1,0:T(8,128)(2,1)} %param.21), channel_id=1, source_target_pairs={{0,1},{1,0},{2,3},{3,2},{4,5},{5,4},{6,7},{7,6},{8,9},{9,8},{10,11... | collective-permute-start | bytes 442376 | tf_op jit(solution)/shard_map/ppermute | solution.py:493
  31.8 25.3 %collective-permute-start.6 = (bf16[96,768]{1,0:T(8,128)(2,1)}, bf16[96,768]{1,0:T(8,128)(2,1)}, u32[]{:S(2)}, u32[]{:S(2)}) collective-permute-start(bf16[96,768]{1,0:T(8,128)(2,1)} %param.21), channel_id=1, source_target_pairs={{0,2},{1,3},{2,0},{3,1},{4,6},{5,7},{6,4},{7,5},{8,10},{9,11},{10,... | collective-permute-start | bytes 442376 | tf_op jit(solution)/shard_map/ppermute | solution.py:493
  34.3 22.9 %collective-permute-start.7 = (bf16[96,768]{1,0:T(8,128)(2,1)}, bf16[96,768]{1,0:T(8,128)(2,1)}, u32[]{:S(2)}, u32[]{:S(2)}) collective-permute-start(bf16[96,768]{1,0:T(8,128)(2,1)} %param.21), channel_id=1, source_target_pairs={{0,3},{1,2},{2,1},{3,0},{4,7},{5,6},{6,5},{7,4},{8,11},{9,10},{10,... | collective-permute-start | bytes 442376 | tf_op jit(solution)/shard_map/ppermute | solution.py:493
  58.8 22.1 %collective-permute-start.10 = (bf16[4,96,768]{2,1,0:T(8,128)(2,1)S(1)}, bf16[4,96,768]{2,1,0:T(8,128)(2,1)S(1)}, u32[]{:S(2)}, u32[]{:S(2)}) collective-permute-start(bf16[4,96,768]{2,1,0:T(8,128)(2,1)S(1)} %get-tuple-element.275), channel_id=1, source_target_pairs={{0,8},{1,9},{2,10},{3,11},{4,12},{5,13},{6,14},{7,15},{8,0},{9,1},... | collective-permute-start | bytes 1769480 | tf_op jit(solution)/shard_map/ppermute | solution.py:493
  59.5 21.4 %collective-permute-start.11 = (bf16[4,96,768]{2,1,0:T(8,128)(2,1)S(1)}, bf16[4,96,768]{2,1,0:T(8,128)(2,1)S(1)}, u32[]{:S(2)}, u32[]{:S(2)}) collective-permute-start(bf16[4,96,768]{2,1,0:T(8,128)(2,1)S(1)} %get-tuple-element.275), channel_id=1, source_target_pairs={{0,16},{1,17},{2,18},{3,19},{4,20},{5,21},{6,22},{7,23},{8,24},{9,... | collective-permute-start | bytes 1769480 | tf_op jit(solution)/shard_map/ppermute | solution.py:493
  60.9 9.3 %collective-permute-start.13 = (bf16[96,768]{1,0:T(8,128)(2,1)}, bf16[96,768]{1,0:T(8,128)(2,1)S(1)}, u32[]{:S(2)}, u32[]{:S(2)}) collective-permute-start(bf16[96,768]{1,0:T(8,128)(2,1)} %bitcast.259), channel_id=1, source_target_pairs={{0,2},{1,3},{2,0},{3,1},{4,6},{5,7},{6,4},{7,5},{8,10},{9,11},{10,... | collective-permute-start | bytes 442376 | tf_op jit(solution)/shard_map/ppermute | solution.py:493
  62.3 18.6 %collective-permute-start.8 = (bf16[2,96,768]{2,1,0:T(8,128)(2,1)S(1)}, bf16[2,96,768]{2,1,0:T(8,128)(2,1)S(1)}, u32[]{:S(2)}, u32[]{:S(2)}) collective-permute-start(bf16[2,96,768]{2,1,0:T(8,128)(2,1)S(1)} %slice.358), channel_id=1, source_target_pairs={{0,16},{1,17},{2,18},{3,19},{4,20},{5,21},{6,22},{7,23},{8,24},{9,... | collective-permute-start | bytes 884744 | tf_op jit(solution)/shard_map/ppermute | solution.py:493
  67.4 13.5 %collective-permute-start.9 = (bf16[2,96,768]{2,1,0:T(8,128)(2,1)S(1)}, bf16[2,96,768]{2,1,0:T(8,128)(2,1)S(1)}, u32[]{:S(2)}, u32[]{:S(2)}) collective-permute-start(bf16[2,96,768]{2,1,0:T(8,128)(2,1)S(1)} %slice.359), channel_id=1, source_target_pairs={{0,8},{1,9},{2,10},{3,11},{4,12},{5,13},{6,14},{7,15},{8,0},{9,1},... | collective-permute-start | bytes 884744 | tf_op jit(solution)/shard_map/ppermute | solution.py:493
  84.4 10.0 %collective-permute-start.15 = (bf16[4,4,96,768]{3,2,1,0:T(8,128)(2,1)S(1)}, bf16[4,4,96,768]{3,2,1,0:T(8,128)(2,1)}, u32[]{:S(2)}, u32[]{:S(2)}) collective-permute-start(bf16[4,4,96,768]{3,2,1,0:T(8,128)(2,1)S(1)} %pad_maximum_fusion.own), channel_id=1, source_target_pairs={{0,4},{1,5},{2,6},{3,7},{4,0},{5,1},{6,2},{7,3},{8,12},{9,13},{10,... | collective-permute-start | bytes 7077896 | tf_op jit(solution)/shard_map/ppermute | solution.py:493
  84.5 9.6 %collective-permute-start.16 = (bf16[2,96,768]{2,1,0:T(8,128)(2,1)}, bf16[2,96,768]{2,1,0:T(8,128)(2,1)S(1)}, u32[]{:S(2)}, u32[]{:S(2)}) collective-permute-start(bf16[2,96,768]{2,1,0:T(8,128)(2,1)} %slice.361), channel_id=1, source_target_pairs={{0,16},{1,17},{2,18},{3,19},{4,20},{5,21},{6,22},{7,23},{8,24},{9,... | collective-permute-start | bytes 884744 | tf_op jit(solution)/shard_map/ppermute | solution.py:493
  85.2 9.3 %collective-permute-start.17 = (bf16[2,96,768]{2,1,0:T(8,128)(2,1)}, bf16[2,96,768]{2,1,0:T(8,128)(2,1)S(1)}, u32[]{:S(2)}, u32[]{:S(2)}) collective-permute-start(bf16[2,96,768]{2,1,0:T(8,128)(2,1)} %slice.362), channel_id=1, source_target_pairs={{0,8},{1,9},{2,10},{3,11},{4,12},{5,13},{6,14},{7,15},{8,0},{9,1},... | collective-permute-start | bytes 884744 | tf_op jit(solution)/shard_map/ppermute | solution.py:493
  95.2 19.2 %collective-permute-start.18 = (bf16[4,96,768]{2,1,0:T(8,128)(2,1)}, bf16[4,96,768]{2,1,0:T(8,128)(2,1)S(1)}, u32[]{:S(2)}, u32[]{:S(2)}) collective-permute-start(bf16[4,96,768]{2,1,0:T(8,128)(2,1)} %get-tuple-element.293), channel_id=1, source_target_pairs={{0,8},{1,9},{2,10},{3,11},{4,12},{5,13},{6,14},{7,15},{8,0},{9,1},... | collective-permute-start | bytes 1769480 | tf_op jit(solution)/shard_map/ppermute | solution.py:493
  96.6 17.8 %collective-permute-start.19 = (bf16[4,96,768]{2,1,0:T(8,128)(2,1)}, bf16[4,96,768]{2,1,0:T(8,128)(2,1)}, u32[]{:S(2)}, u32[]{:S(2)}) collective-permute-start(bf16[4,96,768]{2,1,0:T(8,128)(2,1)} %get-tuple-element.293), channel_id=1, source_target_pairs={{0,16},{1,17},{2,18},{3,19},{4,20},{5,21},{6,22},{7,23},{8,24},{9,... | collective-permute-start | bytes 1769480 | tf_op jit(solution)/shard_map/ppermute | solution.py:493
  115.6 9.9 %collective-permute-start.20 = (bf16[4,4,96,768]{3,2,1,0:T(8,128)(2,1)S(1)}, bf16[4,4,96,768]{3,2,1,0:T(8,128)(2,1)S(1)}, u32[]{:S(2)}, u32[]{:S(2)}) collective-permute-start(bf16[4,4,96,768]{3,2,1,0:T(8,128)(2,1)S(1)} %pad_maximum_fusion.1.refs_6_), channel_id=1, source_target_pairs={{0,4},{1,5},{2,6},{3,7},{4,0},{5,1},{6,2},{7,3},{8,12},{9,13},{10,... | collective-permute-start | bytes 7077896 | tf_op jit(solution)/shard_map/ppermute | solution.py:493
  115.7 9.7 %collective-permute-start.21 = (bf16[2,96,768]{2,1,0:T(8,128)(2,1)S(1)}, bf16[2,96,768]{2,1,0:T(8,128)(2,1)S(1)}, u32[]{:S(2)}, u32[]{:S(2)}) collective-permute-start(bf16[2,96,768]{2,1,0:T(8,128)(2,1)S(1)} %slice.363), channel_id=1, source_target_pairs={{0,16},{1,17},{2,18},{3,19},{4,20},{5,21},{6,22},{7,23},{8,24},{9,... | collective-permute-start | bytes 884744 | tf_op jit(solution)/shard_map/ppermute | solution.py:493
  127.5 11.1 %collective-permute-start.23 = (bf16[4,4,96,768]{3,2,1,0:T(8,128)(2,1)S(1)}, bf16[4,4,96,768]{3,2,1,0:T(8,128)(2,1)}, u32[]{:S(2)}, u32[]{:S(2)}) collective-permute-start(bf16[4,4,96,768]{3,2,1,0:T(8,128)(2,1)S(1)} %pad_maximum_fusion.2.refs_9_), channel_id=1, source_target_pairs={{0,4},{1,5},{2,6},{3,7},{4,0},{5,1},{6,2},{7,3},{8,12},{9,13},{10,... | collective-permute-start | bytes 7077896 | tf_op jit(solution)/shard_map/ppermute | solution.py:493
  177.7 9.3 %collective-permute-start.24 = (bf16[4,4,96,768]{3,2,1,0:T(8,128)(2,1)}, bf16[4,4,96,768]{3,2,1,0:T(8,128)(2,1)S(1)}, u32[]{:S(2)}, u32[]{:S(2)}) collective-permute-start(bf16[4,4,96,768]{3,2,1,0:T(8,128)(2,1)} %get-tuple-element.352), channel_id=1, source_target_pairs={{0,4},{1,5},{2,6},{3,7},{4,0},{5,1},{6,2},{7,3},{8,12},{9,13},{10,... | collective-permute-start | bytes 7077896 | tf_op jit(solution)/shard_map/ppermute | solution.py:493
  192.4 17.1 %collective-permute-start.27 = (bf16[4,4,96,768]{3,2,1,0:T(8,128)(2,1)}, bf16[4,4,96,768]{3,2,1,0:T(8,128)(2,1)S(1)}, u32[]{:S(2)}, u32[]{:S(2)}) collective-permute-start(bf16[4,4,96,768]{3,2,1,0:T(8,128)(2,1)} %get-tuple-element.364), channel_id=1, source_target_pairs={{0,4},{1,5},{2,6},{3,7},{4,0},{5,1},{6,2},{7,3},{8,12},{9,13},{10,... | collective-permute-start | bytes 7077896 | tf_op jit(solution)/shard_map/ppermute | solution.py:493
  192.5 16.1 %collective-permute-start.25 = (bf16[4,96,768]{2,1,0:T(8,128)(2,1)}, bf16[4,96,768]{2,1,0:T(8,128)(2,1)S(1)}, u32[]{:S(2)}, u32[]{:S(2)}) collective-permute-start(bf16[4,96,768]{2,1,0:T(8,128)(2,1)} %get-tuple-element.362), channel_id=1, source_target_pairs={{0,8},{1,9},{2,10},{3,11},{4,12},{5,13},{6,14},{7,15},{8,0},{9,1},... | collective-permute-start | bytes 1769480 | tf_op jit(solution)/shard_map/ppermute | solution.py:493
  193.9 15.6 %collective-permute-start.26 = (bf16[4,96,768]{2,1,0:T(8,128)(2,1)}, bf16[4,96,768]{2,1,0:T(8,128)(2,1)S(1)}, u32[]{:S(2)}, u32[]{:S(2)}) collective-permute-start(bf16[4,96,768]{2,1,0:T(8,128)(2,1)} %get-tuple-element.363), channel_id=1, source_target_pairs={{0,16},{1,17},{2,18},{3,19},{4,20},{5,21},{6,22},{7,23},{8,24},{9,... | collective-permute-start | bytes 1769480 | tf_op jit(solution)/shard_map/ppermute | solution.py:493
  218.5 22.1 %collective-permute-start.30 = (bf16[4,96,768]{2,1,0:T(8,128)(2,1)}, bf16[4,96,768]{2,1,0:T(8,128)(2,1)S(1)}, u32[]{:S(2)}, u32[]{:S(2)}) collective-permute-start(bf16[4,96,768]{2,1,0:T(8,128)(2,1)} %pad_maximum_fusion.10), channel_id=1, source_target_pairs={{0,8},{1,9},{2,10},{3,11},{4,12},{5,13},{6,14},{7,15},{8,0},{9,1},... | collective-permute-start | bytes 1769480 | tf_op jit(solution)/shard_map/ppermute | solution.py:493
  219.1 21.5 %collective-permute-start.31 = (bf16[4,96,768]{2,1,0:T(8,128)(2,1)}, bf16[4,96,768]{2,1,0:T(8,128)(2,1)S(1)}, u32[]{:S(2)}, u32[]{:S(2)}) collective-permute-start(bf16[4,96,768]{2,1,0:T(8,128)(2,1)} %pad_maximum_fusion.11), channel_id=1, source_target_pairs={{0,16},{1,17},{2,18},{3,19},{4,20},{5,21},{6,22},{7,23},{8,24},{9,... | collective-permute-start | bytes 1769480 | tf_op jit(solution)/shard_map/ppermute | solution.py:493
  223.2 17.4 %collective-permute-start.28 = (bf16[2,96,768]{2,1,0:T(8,128)(2,1)}, bf16[2,96,768]{2,1,0:T(8,128)(2,1)S(1)}, u32[]{:S(2)}, u32[]{:S(2)}) collective-permute-start(bf16[2,96,768]{2,1,0:T(8,128)(2,1)} %get-tuple-element.383), channel_id=1, source_target_pairs={{0,16},{1,17},{2,18},{3,19},{4,20},{5,21},{6,22},{7,23},{8,24},{9,... | collective-permute-start | bytes 884744 | tf_op jit(solution)/shard_map/ppermute | solution.py:493
  223.8 16.8 %collective-permute-start.29 = (bf16[2,96,768]{2,1,0:T(8,128)(2,1)}, bf16[2,96,768]{2,1,0:T(8,128)(2,1)S(1)}, u32[]{:S(2)}, u32[]{:S(2)}) collective-permute-start(bf16[2,96,768]{2,1,0:T(8,128)(2,1)} %get-tuple-element.384), channel_id=1, source_target_pairs={{0,8},{1,9},{2,10},{3,11},{4,12},{5,13},{6,14},{7,15},{8,0},{9,1},... | collective-permute-start | bytes 884744 | tf_op jit(solution)/shard_map/ppermute | solution.py:493
  244.6 20.1 %collective-permute-start.32 = (bf16[96,768]{1,0:T(8,128)(2,1)S(1)}, bf16[96,768]{1,0:T(8,128)(2,1)S(1)}, u32[]{:S(2)}, u32[]{:S(2)}) collective-permute-start(bf16[96,768]{1,0:T(8,128)(2,1)S(1)} %fusion.25), channel_id=1, source_target_pairs={{0,1},{1,0},{2,3},{3,2},{4,5},{5,4},{6,7},{7,6},{8,9},{9,8},{10,11... | collective-permute-start | bytes 442376 | tf_op jit(solution)/shard_map/ppermute | solution.py:493
  244.9 20.0 %collective-permute-start.33 = (bf16[96,768]{1,0:T(8,128)(2,1)S(1)}, bf16[96,768]{1,0:T(8,128)(2,1)S(1)}, u32[]{:S(2)}, u32[]{:S(2)}) collective-permute-start(bf16[96,768]{1,0:T(8,128)(2,1)S(1)} %get-tuple-element.409), channel_id=1, source_target_pairs={{0,2},{1,3},{2,0},{3,1},{4,6},{5,7},{6,4},{7,5},{8,10},{9,11},{10,... | collective-permute-start | bytes 442376 | tf_op jit(solution)/shard_map/ppermute | solution.py:493
  246.6 18.3 %collective-permute-start.34 = (bf16[96,768]{1,0:T(8,128)(2,1)S(1)}, bf16[96,768]{1,0:T(8,128)(2,1)S(1)}, u32[]{:S(2)}, u32[]{:S(2)}) collective-permute-start(bf16[96,768]{1,0:T(8,128)(2,1)S(1)} %get-tuple-element.410), channel_id=1, source_target_pairs={{0,3},{1,2},{2,1},{3,0},{4,7},{5,6},{6,5},{7,4},{8,11},{9,10},{10,... | collective-permute-start | bytes 442376 | tf_op jit(solution)/shard_map/ppermute | solution.py:493
  249.1 15.9 %collective-permute-start.35 = (bf16[2,96,768]{2,1,0:T(8,128)(2,1)S(1)}, bf16[2,96,768]{2,1,0:T(8,128)(2,1)S(1)}, u32[]{:S(2)}, u32[]{:S(2)}) collective-permute-start(bf16[2,96,768]{2,1,0:T(8,128)(2,1)S(1)} %get-tuple-element.411), channel_id=1, source_target_pairs={{0,16},{1,17},{2,18},{3,19},{4,20},{5,21},{6,22},{7,23},{8,24},{9,... | collective-permute-start | bytes 884744 | tf_op jit(solution)/shard_map/ppermute | solution.py:493
  249.8 15.2 %collective-permute-start.36 = (bf16[2,96,768]{2,1,0:T(8,128)(2,1)S(1)}, bf16[2,96,768]{2,1,0:T(8,128)(2,1)S(1)}, u32[]{:S(2)}, u32[]{:S(2)}) collective-permute-start(bf16[2,96,768]{2,1,0:T(8,128)(2,1)S(1)} %get-tuple-element.412), channel_id=1, source_target_pairs={{0,8},{1,9},{2,10},{3,11},{4,12},{5,13},{6,14},{7,15},{8,0},{9,1},... | collective-permute-start | bytes 884744 | tf_op jit(solution)/shard_map/ppermute | solution.py:493
  267.5 14.8 %collective-permute-start.37 = (bf16[160,128]{1,0:T(8,128)(2,1)S(1)}, bf16[160,128]{1,0:T(8,128)(2,1)S(1)}, u32[]{:S(2)}, u32[]{:S(2)}) collective-permute-start(bf16[160,128]{1,0:T(8,128)(2,1)S(1)} %fusion.32), channel_id=1, source_target_pairs={{0,1},{1,0},{2,3},{3,2},{4,5},{5,4},{6,7},{7,6},{8,9},{9,8},{10,11... | collective-permute-start | bytes 122888 | tf_op jit(solution)/shard_map/ppermute | solution.py:493
  267.5 14.8 %collective-permute-start.38 = (bf16[160,128]{1,0:T(8,128)(2,1)S(1)}, bf16[160,128]{1,0:T(8,128)(2,1)S(1)}, u32[]{:S(2)}, u32[]{:S(2)}) collective-permute-start(bf16[160,128]{1,0:T(8,128)(2,1)S(1)} %fusion.32), channel_id=1, source_target_pairs={{0,2},{1,3},{2,0},{3,1},{4,6},{5,7},{6,4},{7,5},{8,10},{9,11},{10,... | collective-permute-start | bytes 122888 | tf_op jit(solution)/shard_map/ppermute | solution.py:493
  269.2 13.2 %collective-permute-start.39 = (bf16[160,128]{1,0:T(8,128)(2,1)S(1)}, bf16[160,128]{1,0:T(8,128)(2,1)S(1)}, u32[]{:S(2)}, u32[]{:S(2)}) collective-permute-start(bf16[160,128]{1,0:T(8,128)(2,1)S(1)} %fusion.32), channel_id=1, source_target_pairs={{0,3},{1,2},{2,1},{3,0},{4,7},{5,6},{6,5},{7,4},{8,11},{9,10},{10,... | collective-permute-start | bytes 122888 | tf_op jit(solution)/shard_map/ppermute | solution.py:493
  283.0 14.3 %collective-permute-start.40 = (bf16[4,4,96,768]{3,2,1,0:T(8,128)(2,1)}, bf16[4,4,96,768]{3,2,1,0:T(8,128)(2,1)}, u32[]{:S(2)}, u32[]{:S(2)}) collective-permute-start(bf16[4,4,96,768]{3,2,1,0:T(8,128)(2,1)} %get-tuple-element.450), channel_id=1, source_target_pairs={{0,4},{1,5},{2,6},{3,7},{4,0},{5,1},{6,2},{7,3},{8,12},{9,13},{10,... | collective-permute-start | bytes 7077896 | tf_op jit(solution)/shard_map/ppermute | solution.py:493
  304.9 20.6 %collective-permute-start.46 = (bf16[96,768]{1,0:T(8,128)(2,1)S(1)}, bf16[96,768]{1,0:T(8,128)(2,1)}, u32[]{:S(2)}, u32[]{:S(2)}) collective-permute-start(bf16[96,768]{1,0:T(8,128)(2,1)S(1)} %fusion.26), channel_id=1, source_target_pairs={{0,1},{1,0},{2,3},{3,2},{4,5},{5,4},{6,7},{7,6},{8,9},{9,8},{10,11... | collective-permute-start | bytes 442376 | tf_op jit(solution)/shard_map/ppermute | solution.py:493
  304.9 20.7 %collective-permute-start.47 = (bf16[96,768]{1,0:T(8,128)(2,1)}, bf16[96,768]{1,0:T(8,128)(2,1)}, u32[]{:S(2)}, u32[]{:S(2)}) collective-permute-start(bf16[96,768]{1,0:T(8,128)(2,1)} %get-tuple-element.463), channel_id=1, source_target_pairs={{0,2},{1,3},{2,0},{3,1},{4,6},{5,7},{6,4},{7,5},{8,10},{9,11},{10,... | collective-permute-start | bytes 442376 | tf_op jit(solution)/shard_map/ppermute | solution.py:493
  306.5 19.1 %collective-permute-start.48 = (bf16[96,768]{1,0:T(8,128)(2,1)}, bf16[96,768]{1,0:T(8,128)(2,1)}, u32[]{:S(2)}, u32[]{:S(2)}) collective-permute-start(bf16[96,768]{1,0:T(8,128)(2,1)} %get-tuple-element.464), channel_id=1, source_target_pairs={{0,3},{1,2},{2,1},{3,0},{4,7},{5,6},{6,5},{7,4},{8,11},{9,10},{10,... | collective-permute-start | bytes 442376 | tf_op jit(solution)/shard_map/ppermute | solution.py:493
  309.3 16.3 %collective-permute-start.44 = (bf16[4,96,768]{2,1,0:T(8,128)(2,1)}, bf16[4,96,768]{2,1,0:T(8,128)(2,1)}, u32[]{:S(2)}, u32[]{:S(2)}) collective-permute-start(bf16[4,96,768]{2,1,0:T(8,128)(2,1)} %pad_maximum_fusion.12), channel_id=1, source_target_pairs={{0,8},{1,9},{2,10},{3,11},{4,12},{5,13},{6,14},{7,15},{8,0},{9,1},... | collective-permute-start | bytes 1769480 | tf_op jit(solution)/shard_map/ppermute | solution.py:493
  310.4 15.2 %collective-permute-start.45 = (bf16[4,96,768]{2,1,0:T(8,128)(2,1)}, bf16[4,96,768]{2,1,0:T(8,128)(2,1)}, u32[]{:S(2)}, u32[]{:S(2)}) collective-permute-start(bf16[4,96,768]{2,1,0:T(8,128)(2,1)} %pad_maximum_fusion.13), channel_id=1, source_target_pairs={{0,16},{1,17},{2,18},{3,19},{4,20},{5,21},{6,22},{7,23},{8,24},{9,... | collective-permute-start | bytes 1769480 | tf_op jit(solution)/shard_map/ppermute | solution.py:493
  315.1 10.3 %all-to-all-start.2 = ((f32[32,1,128]{2,1,0:T(1,128)}), f32[32,1,128]{2,1,0:T(1,128)S(1)}, u32[]{:S(2)}, u32[]{:S(2)}) async-start(f32[32,1,128]{2,1,0:T(1,128)} %bitcast.76), calls=%async_computation.2 | async-start | bytes 32768 | tf_op jit(solution)/shard_map/all_to_all | solution.py:435
  332.3 9.3 %collective-permute-start.50 = (bf16[2,96,768]{2,1,0:T(8,128)(2,1)}, bf16[2,96,768]{2,1,0:T(8,128)(2,1)}, u32[]{:S(2)}, u32[]{:S(2)}) collective-permute-start(bf16[2,96,768]{2,1,0:T(8,128)(2,1)} %get-tuple-element.471), channel_id=1, source_target_pairs={{0,16},{1,17},{2,18},{3,19},{4,20},{5,21},{6,22},{7,23},{8,24},{9,... | collective-permute-start | bytes 884744 | tf_op jit(solution)/shard_map/ppermute | solution.py:493
  344.1 13.6 %collective-permute-start.53 = (bf16[96,768]{1,0:T(8,128)(2,1)S(1)}, bf16[96,768]{1,0:T(8,128)(2,1)S(1)}, u32[]{:S(2)}, u32[]{:S(2)}) collective-permute-start(bf16[96,768]{1,0:T(8,128)(2,1)S(1)} %get-tuple-element.480), channel_id=1, source_target_pairs={{0,2},{1,3},{2,0},{3,1},{4,6},{5,7},{6,4},{7,5},{8,10},{9,11},{10,... | collective-permute-start | bytes 442376 | tf_op jit(solution)/shard_map/ppermute | solution.py:493
  345.4 12.3 %collective-permute-start.54 = (bf16[96,768]{1,0:T(8,128)(2,1)S(1)}, bf16[96,768]{1,0:T(8,128)(2,1)S(1)}, u32[]{:S(2)}, u32[]{:S(2)}) collective-permute-start(bf16[96,768]{1,0:T(8,128)(2,1)S(1)} %get-tuple-element.481), channel_id=1, source_target_pairs={{0,3},{1,2},{2,1},{3,0},{4,7},{5,6},{6,5},{7,4},{8,11},{9,10},{10,... | collective-permute-start | bytes 442376 | tf_op jit(solution)/shard_map/ppermute | solution.py:493
  (56 other events, 426.7 us)
